TPU v7x, 128 devices: a whole 4x4x4 slice. The times are simulated.
128 devices in a mesh: mem: 32 (over z_lo, y, x), gx: 2 (over core), gy: 2 (over z_hi).
Axes of the slice: x: 4, y: 4, z: 4 (z_hi: 2, z_lo: 2; z = z_hi * 2 + z_lo), core: 2. Of those that a mesh axis runs over, the one named last changes fastest.
Arguments:
- fields: float32 [128, 3, 256, 256], P('mem', None, 'gx', 'gy'), may hold values from -3 to 3
- noise: float32 [64, 256, 256], P('mem', 'gx', 'gy'), may hold values from -6 to 6
- ancestors: int32 [2, 2, 64], P('gx', 'gy'), may hold values from 0 to 63
- obs_cells: int32 [2, 2, 256], P('gx', 'gy'), may hold values from 0 to 16383
- obs_values: float32 [2, 2, 256], P('gx', 'gy'), may hold values from -3 to 12
Outputs:
- resampled: float32 [128, 3, 256, 256], P('mem', None, 'gx', 'gy')
- log_weights: float32 [2, 2, 128], P('gx', 'gy', 'mem')
All inputs are finite; a program needn't handle non-finite values.
Results may differ from a plain program's by a relative error of at most 0.00012.
Values sent between devices are 32-bit elements; how exact they have to be, the bound alone decides.
No kernel may reach another device: no remote copies, remote signals or barrier semaphores. Data moves between devices by JAX's collectives and lax.ppermute only.
A program may use at most 128 MiB of HBM per device.

v0:
```python
import jax
import jax.numpy as jnp
from jax import lax
from jax.sharding import PartitionSpec as P

COURANT = 0.3
DIFFUSE = 0.05
HYPER = 0.005
NOISE_AMP = 0.1
OBS_VAR = 0.25


def padded_2(block, sides, width):
    for axis, dim in sides:
        count = lax.axis_size(axis)
        forward = [(i, i + 1) for i in range(count - 1)]
        forward.append((count - 1, 0))
        backward = [(target, source) for source, target in forward]
        low = lax.ppermute(
            lax.slice_in_dim(block, block.shape[dim] - width, None, axis=dim), axis, forward
        )
        high = lax.ppermute(lax.slice_in_dim(block, 0, width, axis=dim), axis, backward)
        block = jnp.concatenate([low, block, high], axis=dim)
    return block


def inner(a, width):
    return a[..., width : a.shape[-2] - width, width : a.shape[-1] - width]


def xdiff(a):
    return (a[..., 2:, 1:-1] - a[..., :-2, 1:-1]) * 0.5


def ydiff(a):
    return (a[..., 1:-1, 2:] - a[..., 1:-1, :-2]) * 0.5


def laplace(a):
    return (
        a[..., 2:, 1:-1]
        + a[..., :-2, 1:-1]
        + a[..., 1:-1, 2:]
        + a[..., 1:-1, :-2]
        - 4.0 * a[..., 1:-1, 1:-1]
    )


def smooth(a):
    return DIFFUSE * inner(laplace(a), 1) - HYPER * laplace(laplace(a))


def advance(eta, speed_x, speed_y, force, coriolis):
    depth = 1.0 + eta
    cor_one = coriolis[1:-1]
    u_one = inner(speed_x, 1)
    v_one = inner(speed_y, 1)
    tend_h = xdiff(depth * speed_x) + ydiff(depth * speed_y)
    tend_u = u_one * xdiff(speed_x) + v_one * ydiff(speed_x) + xdiff(eta) - cor_one * v_one
    tend_v = u_one * xdiff(speed_y) + v_one * ydiff(speed_y) + ydiff(eta) + cor_one * u_one
    new_eta = inner(eta, 2) - COURANT * inner(tend_h, 1) + smooth(eta) + NOISE_AMP * force
    new_u = inner(speed_x, 2) - COURANT * inner(tend_u, 1) + smooth(speed_x)
    new_v = inner(speed_y, 2) - COURANT * inner(tend_v, 1) + smooth(speed_y)
    return (new_eta, new_u, new_v)


def coriolis_rows(width, count):
    total_y = count * lax.axis_size("gy")
    first = lax.axis_index("gy") * count
    rows_y = (first + jnp.arange(-width, count + width, dtype=jnp.int32)) % total_y
    return 0.1 + 0.2 * ((rows_y.astype(jnp.float32) + 0.5) / total_y - 0.5)


def take_masked(table, wanted):
    inside = (wanted >= 0) & (wanted < table.shape[0])
    rows = jnp.take(table, jnp.clip(wanted, 0, table.shape[0] - 1), axis=0)
    return jnp.where(inside[:, None], rows, jnp.zeros_like(rows))


def shards(fields, noise, ancestors, obs_cells, obs_values):
    members, comps, count_x, count_y = fields.shape
    force = jnp.repeat(noise, 2, axis=0)
    state = fields
    coriolis = coriolis_rows(2, count_y)
    for step in range(2):
        padded = padded_2(state, (("gx", 2), ("gy", 3)), 2)
        eta, speed_x, speed_y = advance(padded[:, 0], padded[:, 1], padded[:, 2], force, coriolis)
        state = jnp.stack([eta, speed_x, speed_y], axis=1)
    heights = state[:, 0].reshape(members, count_x * count_y)
    observed = jnp.take(heights, obs_cells.reshape(-1), axis=1)
    misfit = observed - obs_values.reshape(1, -1)
    logw = -0.5 * jnp.sum(misfit * misfit, axis=1) / OBS_VAR
    peak = lax.pmax(jnp.max(logw), "mem")
    expo = jnp.exp(logw - peak)
    total = lax.psum(jnp.sum(expo), "mem")
    log_weights = (logw - peak - jnp.log(total)).reshape(1, 1, members)
    flat = state.reshape(members, comps * count_x * count_y)
    lineage = ancestors.reshape(-1)
    member_index = lax.axis_index("mem")
    own_pairs = lax.dynamic_slice_in_dim(lineage, member_index * (members // 2), members // 2)
    source = 2 * jnp.repeat(own_pairs, 2) + jnp.tile(jnp.arange(2, dtype=jnp.int32), members // 2)
    picked = take_masked(lax.all_gather(flat, "mem", axis=0, tiled=True), source)
    resampled = picked.reshape(members, comps, count_x, count_y)
    return (resampled, log_weights)


def solution(mesh):
    return jax.shard_map(
        shards,
        mesh=mesh,
        in_specs=(
            P("mem", None, "gx", "gy"),
            P("mem", "gx", "gy"),
            P("gx", "gy", None),
            P("gx", "gy", None),
            P("gx", "gy", None),
        ),
        out_specs=(P("mem", None, "gx", "gy"), P("gx", "gy", "mem")),
        check_vma=False,
    )
```

profile of v0, /device:TPU:0, one launch (start us, length us, event | category | flops | bytes accessed | tf_op | source)
XLA Modules:
  0.0 381.1 jit_solution(1533988229665999524)
XLA Ops:
  7.2 0.8 fusion.92
  8.1 0.1 collective-permute-start
  8.2 0.5 collective-permute-start.1
  8.7 0.9 broadcast_multiply_fusion
  9.6 1.4 copy.38
  11.0 0.3 copy.37
  11.4 0.3 copy.39
  11.8 0.1 pad_maximum_fusion.11
  11.9 4.0 %collective-permute-start.2 = (f32[4,3,132,2]{2,0,3,1:T(4,128)S(1)}, f32[4,3,132,2]{2,0,3,1:T(4,128)S(1)}, u32[]{:S(2)}, u32[]{:S(2)}) collective-permute-start(f32[4,3,132,2]{2,0,3,1:T(4,128)S(1)} %get-tuple-element.4), channel_id=1, source_target_pairs={{0,1},{1,0},{2,3},{3,2},{4,5},{5,4},{6,7},{7,6},{8,9},{9,8},{10,11... | collective-permute-start | bytes 38024 | tf_op jit(solution)/shard_map/ppermute | solution.py:19
  15.9 0.1 collective-permute-start.3
  16.0 0.1 copy.40
  16.2 1.5 collective-permute-done.2
  17.7 3.5 collective-permute-done.3
  21.2 1.3 pad_maximum_fusion
  22.5 0.3 slice_bitcast_fusion.4
  22.8 0.3 add_multiply_fusion.3
  23.1 1.2 fusion.100
  24.3 2.3 fusion.1
  26.5 0.9 fusion.97
  27.4 0.1 broadcast_in_dim.45
  27.5 1.3 fusion.76
  28.8 2.0 fusion.60
  30.8 2.0 fusion.45
  32.8 0.2 pad_maximum_fusion.2
  32.9 0.5 fusion.91
  33.4 0.3 copy.41
  33.7 0.2 collective-permute-start.4
  33.9 0.2 copy.42
  34.2 0.6 collective-permute-start.5
  34.7 0.4 collective-permute-done.4
  35.1 0.3 copy.43
  35.4 0.1 collective-permute-done.5
  35.6 0.3 copy.44
  35.9 0.1 pad_maximum_fusion.8
  36.0 0.3 collective-permute-start.6
  36.4 3.3 collective-permute-start.7
  39.6 1.8 collective-permute-done.6
  41.4 0.3 collective-permute-done.7
  41.7 2.3 pad_maximum_fusion.1
  44.0 0.3 slice_bitcast_fusion.1
  44.3 0.3 add_multiply_fusion.1
  44.6 1.2 fusion
  45.7 0.4 fusion.93
  46.1 0.6 fusion.94
  46.7 1.2 fusion.95
  47.9 1.2 fusion.96
  49.0 1.3 fusion.36
  50.3 2.0 fusion.21
  52.3 2.0 fusion.6
  54.3 0.2 pad_maximum_fusion.3
  54.5 0.3 copy.45
  54.8 1.2 reshape.175
  56.5 7.7 %copy.46 = f32[4,128,128]{0,2,1:T(8,128)} copy(f32[4,128,128]{1,0,2:T(4,128)S(1)} %fusion.36) | data formatting | bytes 524288 | tf_op jit(solution)/shard_map/add | solution.py:61
  64.2 4.4 %gather_fusion.1 = f32[256,4]{1,0:T(8,128)S(1)} fusion(f32[4,16384]{0,1:T(8,128)} %bitcast.57, s32[1024]{0:T(1024)S(1)} %pad_clamp_fusion), kind=kCustom, calls=%fused_computation.1 | custom fusion | bytes 9216 | tf_op jit(solution)/shard_map/jit(_take)/gather | solution.py:90
  68.6 0.2 multiply_reduce_fusion
  68.7 0.6 fusion.90
  69.4 83.9 %pmax.7 = f32[]{:T(128)} all-reduce(f32[]{:T(128)} %fusion.90), channel_id=1, replica_groups=mesh['mem'=32,'gx'=2,'gy'=2] {'mem'}, use_global_device_ids=true, to_apply=%region_2.3 | all-reduce | flops 1 | bytes 8 | tf_op jit(solution)/shard_map/pmax | solution.py:93
  153.3 1.2 exponential_reduce_fusion
  154.5 78.0 %psum.7 = f32[]{:T(128)} all-reduce(f32[]{:T(128)} %exponential_reduce_fusion), channel_id=1, replica_groups=mesh['mem'=32,'gx'=2,'gy'=2] {'mem'}, use_global_device_ids=true, to_apply=%region_4.5 | all-reduce | flops 1 | bytes 8 | tf_op jit(solution)/shard_map/psum | solution.py:95
  233.2 1.1 subtract_bitcast_fusion
  234.3 104.2 %all-gather.3.cloned.1.call-done = f32[32,4,49152]{2,1,0:T(4,128)} async-done(((f32[1,4,49152]{2,1,0:T(4,128)}), f32[32,4,49152]{2,1,0:T(4,128)}) %all-gather.3.cloned.1.call-update) | async-done | bytes 25165840 | tf_op jit(solution)/shard_map/all_gather | solution.py:102
  338.5 25.3 %reshape.176 = f32[128,49152]{1,0:T(8,128)} reshape(f32[32,4,49152]{2,1,0:T(4,128)} %all-gather.3.cloned.1.call-done) | data formatting | bytes 50331648
  363.7 9.4 %gather_fusion = f32[4,49152]{1,0:T(4,128)S(1)} fusion(f32[128,49152]{1,0:T(8,128)} %reshape.176, s32[1024]{0:T(1024)S(1)} %pad_clamp_fusion.1), kind=kCustom, calls=%fused_computation | custom fusion | bytes 1572880 | tf_op jit(solution)/shard_map/jit(_take)/gather | solution.py:76
  373.2 1.0 select_select_fusion
  (27 shorter events, 0.7 us)
Async XLA Ops:
  7.2 331.3 %all-gather.3.cloned.1.call-start = ((), (), s32[]{:S(2)}) async-start(), calls=%async_computation | async-start | bytes 25952256 | tf_op jit(solution)/shard_map/all_gather | solution.py:102
  8.1 3.0 collective-permute-start
  8.2 3.2 collective-permute-start.1
  11.9 5.8 %collective-permute-start.2 = (f32[4,3,132,2]{2,0,3,1:T(4,128)S(1)}, f32[4,3,132,2]{2,0,3,1:T(4,128)S(1)}, u32[]{:S(2)}, u32[]{:S(2)}) collective-permute-start(f32[4,3,132,2]{2,0,3,1:T(4,128)S(1)} %get-tuple-element.4), channel_id=1, source_target_pairs={{0,1},{1,0},{2,3},{3,2},{4,5},{5,4},{6,7},{7,6},{8,9},{9,8},{10,11... | collective-permute-start | bytes 38024 | tf_op jit(solution)/shard_map/ppermute | solution.py:19
  15.9 5.3 %collective-permute-start.3 = (f32[4,3,132,2]{2,0,3,1:T(4,128)S(1)}, f32[4,3,132,2]{2,0,3,1:T(4,128)S(1)}, u32[]{:S(2)}, u32[]{:S(2)}) collective-permute-start(f32[4,3,132,2]{2,0,3,1:T(4,128)S(1)} %get-tuple-element.5), channel_id=1, source_target_pairs={{1,0},{0,1},{3,2},{2,3},{5,4},{4,5},{7,6},{6,7},{9,8},{8,9},{11,10... | collective-permute-start | bytes 38024 | tf_op jit(solution)/shard_map/ppermute | solution.py:22
  33.7 1.4 collective-permute-start.4
  34.2 1.4 collective-permute-start.5
  36.0 5.4 %collective-permute-start.6 = (f32[4,3,132,2]{2,0,3,1:T(4,128)S(1)}, f32[4,3,132,2]{2,0,3,1:T(4,128)S(1)}, u32[]{:S(2)}, u32[]{:S(2)}) collective-permute-start(f32[4,3,132,2]{2,0,3,1:T(4,128)S(1)} %get-tuple-element.2), channel_id=1, source_target_pairs={{0,1},{1,0},{2,3},{3,2},{4,5},{5,4},{6,7},{7,6},{8,9},{9,8},{10,11... | collective-permute-start | bytes 38024 | tf_op jit(solution)/shard_map/ppermute | solution.py:19
  36.4 5.3 %collective-permute-start.7 = (f32[4,3,132,2]{2,0,3,1:T(4,128)S(1)}, f32[4,3,132,2]{2,0,3,1:T(4,128)S(1)}, u32[]{:S(2)}, u32[]{:S(2)}) collective-permute-start(f32[4,3,132,2]{2,0,3,1:T(4,128)S(1)} %get-tuple-element.3), channel_id=1, source_target_pairs={{1,0},{0,1},{3,2},{2,3},{5,4},{4,5},{7,6},{6,7},{9,8},{8,9},{11,10... | collective-permute-start | bytes 38024 | tf_op jit(solution)/shard_map/ppermute | solution.py:22
  54.4 1.6 copy-start.2
  54.5 1.9 copy-start.1
  56.5 12.1 %copy-start = (f32[1,1,256]{2,1,0:T(1,128)S(1)}, f32[1,1,256]{2,1,0:T(1,128)}, u32[]{:S(2)}) copy-start(f32[1,1,256]{2,1,0:T(1,128)} %param.9) | copy-start | bytes 3076
Sparse Core Ops, SparseCore 0:
  56.1 282.2 all-gather.2
where the time goes:
time: 382 us; the launch traced here: 381 us
  blocking collectives  162 us (42%)
  waiting for transfers between devices  112 us (29%)
  local copies, waits for them, and re-layouts  56 us (15%)
  other arithmetic  27.2 us (7%)
  between operations  15.1 us (4%)
  starting transfers between devices  9.15 us (2%)
    all_gather x1, waiting for transfers between devices, shards(): lax.all_gather(flat, 'mem', axis=0, tiled=True)  104 us
    pmax x1, blocking collectives, shards(): peak = lax.pmax(jnp.max(logw), 'mem')  83.9 us
    psum x1, blocking collectives, shards(): total = lax.psum(jnp.sum(expo), 'mem')  78 us
    unnamed x12, local copies, waits for them, and re-layouts  28 us
    another operation x7, other arithmetic, shards(): state = jnp.stack([eta, speed_x, speed_y], axis=1)  9.48 us
    gather x1, local copies, waits for them, and re-layouts, take_masked(): rows = jnp.take(table, jnp.clip(wanted, 0, table.shape[0] - 1), axis=0)  9.43 us
    add x1, local copies, waits for them, and re-layouts, advance(): inner(eta, 2) - COURANT * inner(tend_h, 1) + smooth(eta) + NOISE_AMP * force  7.74 us
  transfers between devices with their start and end apart: 9, of which 7 were waited for; matrix products, arithmetic and copies ran while one was open for 5% of the time, Pallas kernels for 0%

commit v1 on v0

v1 whole, which is shorter than its diff:
```python
import functools

import jax
import jax.numpy as jnp
from jax import lax
from jax.experimental import pallas as pl
from jax.experimental.pallas import tpu as pltpu
from jax.sharding import PartitionSpec as P

COURANT = 0.3
NOISE_AMP = 0.1
OBS_VAR = 0.25
T = 128
F32 = jnp.float32
CHUNK = 16


def lanes(shape):
    return lax.broadcasted_iota(jnp.int32, shape, len(shape) - 1)


def subl(shape):
    return lax.broadcasted_iota(jnp.int32, shape, len(shape) - 2)


def lroll(a, shift):
    return pltpu.roll(a, shift % T, 1)


def rows_at(ref, lead, start, off, count, total):
    first = start + off
    if first < 0:
        return pltpu.roll(ref[(*lead, pl.ds(0, count))], -first, 0)
    if first + count > total:
        over = first + count - total
        return pltpu.roll(ref[(*lead, pl.ds(total - count, count))], count - over, 0)
    return ref[(*lead, pl.ds(first, count))]


def one_step(ref, lead, start, count, total, force, cor):
    get = lambda f, off: rows_at(ref, (*lead, f), start, off, count, total)
    cen, low, high = [], [], []
    dx, dy, loc, q = [], [], [], []
    for f in range(3):
        a, am, ap = get(f, 0), get(f, -1), get(f, 1)
        far = get(f, -2) + get(f, 2)
        cross = am + ap
        yp, ym = lroll(a, -1), lroll(a, 1)
        cen.append(a)
        low.append(am)
        high.append(ap)
        dx.append(ap - am)
        dy.append(yp - ym)
        loc.append(0.71 * a + (0.09 * cross - 0.005 * far))
        q.append(0.09 * a - (0.01 * cross + 0.005 * (yp + ym)))
    eta, u, v = cen
    half = 0.5 * COURANT
    hv = half * ((1.0 + eta) * v)
    hu = (1.0 + high[0]) * high[1] - (1.0 + low[0]) * low[1]
    new_eta = loc[0] + lroll(q[0] - hv, -1) + lroll(q[0] + hv, 1) - half * hu + NOISE_AMP * force
    tend_u = u * dx[1] + v * dy[1] + dx[0]
    tend_v = u * dx[2] + v * dy[2] + dy[0]
    new_u = loc[1] + (lroll(q[1], -1) + lroll(q[1], 1)) - half * tend_u + (COURANT * cor) * v
    new_v = loc[2] + (lroll(q[2], -1) + lroll(q[2], 1)) - half * tend_v - (COURANT * cor) * u
    return new_eta, new_u, new_v


def coriolis(cols, total_y):
    y = lax.rem(lax.axis_index("gy") * T + cols + total_y, total_y)
    return 0.1 + 0.2 * ((y.astype(F32) + 0.5) / total_y - 0.5)


def pack_kernel(fields, noise, rowpack, colpack, cornpack):
    members = fields.shape[0]
    top = subl((8, T)) < 4
    for m in range(members):
        for f in range(3):
            rowpack[3 * m + f] = jnp.where(top, fields[m, f, 0:8], fields[m, f, T - 8 : T])
    for p in range(members // 2):
        rowpack[3 * members + p] = jnp.where(top, noise[p, 0:8], noise[p, T - 8 : T])
    for t in range(0, T, CHUNK):
        ln = lanes((CHUNK, T)) // 8
        acc = jnp.zeros((CHUNK, T), F32)
        for m in range(members):
            for f in range(4):
                src = fields[m, f, t : t + CHUNK] if f < 3 else noise[m // 2, t : t + CHUNK]
                acc = jnp.where(ln == 4 * m + f, lroll(src, 32 * m + 8 * f + 4), acc)
        colpack[t : t + CHUNK] = acc
    cornpack[...] = jnp.where(top, colpack[0:8], colpack[T - 8 : T])


def own_columns(tiles):
    shape = tiles[0].shape
    ln = lanes(shape) // 8
    acc = jnp.zeros(shape, F32)
    for m, a in enumerate(tiles):
        acc = jnp.where(ln == 4 * m, lroll(a, 32 * m + 8), acc)
        acc = jnp.where(ln == 4 * m + 3, lroll(a, 32 * m + 24), acc)
    return acc


def interior_kernel(total_y, fields, noise, inner, ownrow, owncol, tmp):
    members = fields.shape[0]
    cor = coriolis(lanes((1, T)), total_y)

    def body(m, carry):
        for r in range(0, T, CHUNK):
            new = one_step(fields, (m,), r, CHUNK, T, noise[m // 2, pl.ds(r, CHUNK)], cor)
            for f in range(3):
                tmp[f, pl.ds(r, CHUNK)] = new[f]
        for r in range(0, T, CHUNK):
            new = one_step(tmp, (), r, CHUNK, T, noise[m // 2, pl.ds(r, CHUNK)], cor)
            for f in range(3):
                inner[m, f, pl.ds(r, CHUNK)] = new[f]
        return carry

    lax.fori_loop(0, members, body, 0)
    for m in range(members):
        for f in range(4):
            src = fields.at[m, f] if f < 3 else noise.at[m // 2]
            ownrow[f, 2 * m] = src[0:8]
            ownrow[f, 2 * m + 1] = src[T - 8 : T]
    for f in range(4):
        for t in range(0, T, CHUNK):
            tiles = []
            for m in range(members):
                src = fields.at[m, f] if f < 3 else noise.at[m // 2]
                tiles.append(src[t : t + CHUNK])
            owncol[f, t : t + CHUNK] = own_columns(tiles)


def merge_kernel(total_y, inner, ownrow, owncol, rowrecv, colrecv, cornrecv, cells, values,
                 out, logw, rs, rs1, cs, cs1, eta_s):
    members = inner.shape[0]
    tall = T + 16
    l32 = lax.rem(lanes((1, T)), 32)
    cor_row = coriolis(lanes((1, T)), total_y)
    cor_col = coriolis(jnp.where(l32 < 16, l32 + 120, l32 - 24), total_y)
    is_low = (l32 >= 20) & (l32 < 24)
    is_high = (l32 >= 8) & (l32 < 12)

    for f in range(4):
        for m in range(members):
            halo = rowrecv[3 * m + f] if f < 3 else rowrecv[3 * members + m // 2]
            rs[f, 32 * m : 32 * m + 8] = halo
            rs[f, 32 * m + 8 : 32 * m + 16] = ownrow[f, 2 * m]
            rs[f, 32 * m + 16 : 32 * m + 24] = ownrow[f, 2 * m + 1]
            rs[f, 32 * m + 24 : 32 * m + 32] = halo
        with_halo = lambda own, recv: jnp.where(
            is_low, lroll(recv, 20 - 8 * f), jnp.where(is_high, lroll(recv, 4 - 8 * f), own)
        )
        tiles = [rowrecv[3 * m + f] if f < 3 else rowrecv[3 * members + m // 2] for m in range(members)]
        ends = with_halo(own_columns(tiles), cornrecv[...])
        cs[f, 0:8] = ends
        cs[f, T + 8 : T + 16] = ends
        for t in range(0, T, CHUNK):
            cs[f, t + 8 : t + 8 + CHUNK] = with_halo(owncol[f, t : t + CHUNK], colrecv[t : t + CHUNK])

    def twice(a, a1, total, cor):
        for src, dst in ((a, a1), (a1, a)):
            for r in range(0, total, CHUNK):
                new = one_step(src, (), r, CHUNK, total, a[3, r : r + CHUNK], cor)
                for f in range(3):
                    dst[f, r : r + CHUNK] = new[f]

    twice(rs, rs1, T, cor_row)
    twice(cs, cs1, tall, cor_col)

    top = subl((8, T)) < 4
    left = lanes((8, T)) < 4
    right = lanes((8, T)) >= T - 4
    for m in range(members):
        p, mm = m // 2, m % 2
        for f in range(3):
            for t in range(T // 8):
                a = inner[m, f, 8 * t : 8 * t + 8]
                if t == 0:
                    a = jnp.where(top, rs[f, 32 * m + 8 : 32 * m + 16], a)
                if t == T // 8 - 1:
                    a = jnp.where(top, a, rs[f, 32 * m + 16 : 32 * m + 24])
                col = cs[f, 8 * t + 8 : 8 * t + 16]
                a = jnp.where(left, lroll(col, 104 - 32 * m), a)
                a = jnp.where(right, lroll(col, 120 - 32 * m), a)
                k = mm * 48 + f * 16 + t
                per = 96 // out.shape[0]
                out[k // per, p, 8 * (k % per) : 8 * (k % per) + 8] = a
                if f == 0:
                    eta_s[m * T + 8 * t : m * T + 8 * t + 8] = a

    count = cells.shape[1]
    cell = cells[...]
    pick_y = (lax.broadcasted_iota(jnp.int32, (T, count), 0) == lax.rem(cell, T)).astype(F32)
    pick_x = lax.broadcasted_iota(jnp.int32, (T, count), 0) == cell // T
    for m in range(members):
        seen = jnp.dot(eta_s[m * T : (m + 1) * T], pick_y, precision=lax.Precision.HIGHEST,
                       preferred_element_type=F32)
        seen = jnp.sum(jnp.where(pick_x, seen, 0.0), axis=0, keepdims=True)
        miss = seen - values[...]
        total = jnp.sum(miss * miss, axis=1, keepdims=True)
        logw[m : m + 1] = jnp.broadcast_to(-0.5 * total / OBS_VAR, (1, T))


def select_kernel(lineage, recv, out):
    def body(k, carry):
        out[k] = recv[lineage[k]]
        return carry

    lax.fori_loop(0, recv.shape[0], body, 0, unroll=8)


VM = pl.BlockSpec(memory_space=pltpu.VMEM)
SM = pl.BlockSpec(memory_space=pltpu.SMEM)
PARAMS = pltpu.CompilerParams(vmem_limit_bytes=24 << 20)


def sds(*shape):
    return jax.ShapeDtypeStruct(shape, F32)


def shards(fields, noise, ancestors, obs_cells, obs_values):
    members = fields.shape[0]
    devices = lax.axis_size("mem")
    total_y = T * lax.axis_size("gy")
    rowpack, colpack, cornpack = pl.pallas_call(
        pack_kernel,
        out_shape=(sds(3 * members + members // 2, 8, T), sds(T, T), sds(8, T)),
        in_specs=[VM] * 2,
        out_specs=[VM] * 3,
        compiler_params=PARAMS,
        name="pack",
    )(fields, noise)
    swap = [(0, 1), (1, 0)]
    colrecv = lax.ppermute(colpack, "gy", swap)
    cornrecv = lax.ppermute(cornpack, ("gx", "gy"), [(0, 3), (1, 2), (2, 1), (3, 0)])
    rowrecv = lax.ppermute(rowpack, "gx", swap)
    inner, ownrow, owncol = pl.pallas_call(
        functools.partial(interior_kernel, total_y),
        out_shape=(sds(members, 3, T, T), sds(4, 2 * members, 8, T), sds(4, T, T)),
        in_specs=[VM] * 2,
        out_specs=[VM] * 3,
        scratch_shapes=[pltpu.VMEM((3, T, T), F32)],
        compiler_params=PARAMS,
        cost_estimate=pl.CostEstimate(flops=50_000_000, bytes_accessed=2_500_000, transcendentals=0),
        name="interior",
    )(fields, noise)
    rows = members // 2 * 96 // devices * 4
    pieces, logw = pl.pallas_call(
        functools.partial(merge_kernel, total_y),
        out_shape=(sds(devices, members // 2, 768 // devices, T), sds(members, T)),
        in_specs=[VM] * 8,
        out_specs=[VM] * 2,
        scratch_shapes=[
            pltpu.VMEM((4, T, T), F32),
            pltpu.VMEM((3, T, T), F32),
            pltpu.VMEM((4, T + 16, T), F32),
            pltpu.VMEM((3, T + 16, T), F32),
            pltpu.VMEM((members * T, T), F32),
        ],
        compiler_params=PARAMS,
        name="merge",
    )(inner, ownrow, owncol, rowrecv, colrecv, cornrecv, obs_cells.reshape(1, -1), obs_values.reshape(1, -1))
    held = lax.all_to_all(pieces, "mem", 0, 0)
    logw = logw[:, 0]
    logw_all = lax.all_gather(logw, "mem")
    picked = pl.pallas_call(
        select_kernel,
        out_shape=sds(devices * members // 2, 768 // devices, T),
        in_specs=[SM, VM],
        out_specs=VM,
        compiler_params=PARAMS,
        name="select",
    )(ancestors.reshape(-1), held.reshape(devices * members // 2, 768 // devices, T))
    back = lax.all_to_all(picked.reshape(held.shape), "mem", 0, 0)
    resampled = back.transpose(1, 0, 2, 3).reshape(fields.shape)
    peak = jnp.max(logw_all)
    total = jnp.sum(jnp.exp(logw_all - peak))
    log_weights = (logw - peak - jnp.log(total)).reshape(1, 1, members)
    return (resampled, log_weights)


def solution(mesh):
    return jax.shard_map(
        shards,
        mesh=mesh,
        in_specs=(
            P("mem", None, "gx", "gy"),
            P("mem", "gx", "gy"),
            P("gx", "gy", None),
            P("gx", "gy", None),
            P("gx", "gy", None),
        ),
        out_specs=(P("mem", None, "gx", "gy"), P("gx", "gy", "mem")),
        check_vma=False,
    )
```

time: 382 us -> 137 us (0.36)
  waiting for transfers between devices: 112 us -> 0.01 us
  blocking collectives: 162 us -> 105 us
  local copies, waits for them, and re-layouts: 56 us -> 5.87 us
  other arithmetic: 27.2 us -> 3.29 us
  between operations: 15.1 us -> 2.07 us
  Pallas kernels: 0 us -> 11.1 us
    all_gather x1 -> x0, waiting for transfers between devices: 104 us -> none  [shards(): lax.all_gather(flat, 'mem', axis=0, tiled=True)]
    pmax x1 -> x0, blocking collectives: 83.9 us -> none  [shards(): peak = lax.pmax(jnp.max(logw), 'mem')]
    unnamed x0 -> x1, blocking collectives: none -> 82.9 us
    psum x1 -> x0, blocking collectives: 78 us -> none  [shards(): total = lax.psum(jnp.sum(expo), 'mem')]
    unnamed x12 -> x15, local copies, waits for them, and re-layouts: 28 us -> 4.83 us
    all_to_all x0 -> x1, blocking collectives: none -> 22.2 us  [shards(): held = lax.all_to_all(pieces, 'mem', 0, 0)]
    gather x2 -> x0, local copies, waits for them, and re-layouts: 13.8 us -> none  [the longest x1 9.43 us: take_masked(): rows = jnp.take(table, jnp.clip(wanted, 0, table.shape[0] - 1), axis=0)]
    pallas_call x0 -> x4, Pallas kernels: none -> 11.1 us  [the longest x1 5.48 us: shards(): pl.pallas_call(functools.partial(interior_kernel, total_y), out_shape=(sd...]
  transfers between devices with their start and end apart: 9 -> 4, of which waited for: 7 -> 0; matrix products, arithmetic and copies ran while one was open for 5% -> 3% of each run, Pallas kernels for 0% -> 4%
where the time goes in v1:
time: 137 us; the launch traced here: 136 us
  blocking collectives  105 us (77%)
  Pallas kernels  11.1 us (8%)
  starting transfers between devices  8.69 us (6%)
  local copies, waits for them, and re-layouts  5.87 us (4%)
  other arithmetic  3.29 us (2%)
  between operations  2.07 us (2%)
    unnamed x1, blocking collectives  82.9 us
    all_to_all x1, blocking collectives, shards(): held = lax.all_to_all(pieces, 'mem', 0, 0)  22.2 us
    pallas_call x1, Pallas kernels, shards(): pl.pallas_call(functools.partial(interior_kernel, total_y), out_shape=(sd...  5.48 us
    unnamed x15, local copies, waits for them, and re-layouts  4.83 us
    all_to_all x1, starting transfers between devices, shards(): back = lax.all_to_all(picked.reshape(held.shape), 'mem', 0, 0)  4.43 us
    ppermute x1, starting transfers between devices, shards(): colrecv = lax.ppermute(colpack, 'gy', swap)  4.04 us
    pallas_call x1, Pallas kernels, shards(): pl.pallas_call(functools.partial(merge_kernel, total_y), out_shape=(sds(d...  3.76 us
  transfers between devices with their start and end apart: 4, of which 0 were waited for; matrix products, arithmetic and copies ran while one was open for 3% of the time, Pallas kernels for 4%

profile of v1, /device:TPU:0, one launch (start us, length us, event | category | flops | bytes accessed | tf_op | source)
XLA Modules:
  0.0 136.1 jit_solution(10485287191700873397)
XLA Ops:
  0.6 0.0 copy-start
  0.6 1.1 copy-done
  1.8 0.0 copy-start.1
  1.8 0.9 copy-done.1
  2.7 0.3 pack.1
  3.0 4.0 %collective-permute-start.1 = (f32[128,128]{1,0:T(8,128)S(1)}, f32[128,128]{1,0:T(8,128)S(1)}, u32[]{:S(2)}, u32[]{:S(2)}) collective-permute-start(f32[128,128]{1,0:T(8,128)S(1)} %get-tuple-element.14), channel_id=1, source_target_pairs={{0,1},{1,0},{2,3},{3,2},{4,5},{5,4},{6,7},{7,6},{8,9},{9,8},{10,11... | collective-permute-start | bytes 196616 | tf_op jit(solution)/shard_map/ppermute | solution.py:233
  7.0 0.0 collective-permute-start
  7.0 0.2 collective-permute-start.2
  7.3 0.0 copy-start.3
  7.3 5.5 %interior.1 = (f32[4,3,128,128]{3,2,1,0:T(8,128)S(1)}, f32[4,8,8,128]{3,2,1,0:T(8,128)S(1)}, f32[4,128,128]{2,1,0:T(8,128)S(1)}) custom-call(f32[4,3,128,128]{3,2,1,0:T(8,128)S(1)} %copy-done, f32[2,128,128]{2,1,0:T(8,128)S(1)} %copy-done.1), custom_call_target="tpu_custom_call" | custom-call | flops 50000000 | bytes 2500000 | tf_op jit(solution)/shard_map/interior/pallas_call | solution.py:236
  12.8 0.0 collective-permute-done.2.cornrecv
  12.8 0.0 collective-permute-done.rowrecv
  12.8 0.0 collective-permute-done.1.colrecv
  12.8 0.0 copy-start.2
  12.8 0.0 copy-done.3
  12.8 0.7 copy-done.2
  13.5 3.8 %merge.1 = (f32[32,2,24,128]{3,2,1,0:T(8,128)S(1)}, f32[4,128]{1,0:T(4,128)S(1)}) custom-call(f32[4,3,128,128]{3,2,1,0:T(8,128)S(1)} %get-tuple-element.10.inner, f32[4,8,8,128]{3,2,1,0:T(8,128)S(1)} %get-tuple-element.11.ownrow, f32[4,128,128]{2,1,0:T(8,128)S(1)} %get-tuple-element.12.owncol, f32[14,8,128]{2,1,0:T(8,128)S(1)} %collective-permute-done.rowrecv, ...), custom_call_target="tpu_custom_call" | custom-call | tf_op jit(solution)/shard_map/merge/pallas_call | solution.py:247
  17.2 22.2 %all_to_all.10 = f32[32,2,24,128]{3,2,1,0:T(8,128)S(1)} all-to-all(f32[32,2,24,128]{3,2,1,0:T(8,128)S(1)} %get-tuple-element.16), channel_id=1, replica_groups=mesh['mem'=32,'gx'=2,'gy'=2] {'mem'}, dimensions={0} | all-to-all | bytes 1572864 | tf_op jit(solution)/shard_map/all_to_all | solution.py:262
  39.4 0.0 copy-start.4
  39.4 0.7 copy-done.4
  40.1 1.5 %select.1 = f32[64,24,128]{2,1,0:T(8,128)} custom-call(s32[64]{0:T(128)S(1)} %bitcast.12, f32[64,24,128]{2,1,0:T(8,128)S(1)} %bitcast.9), custom_call_target="tpu_custom_call" | custom-call | tf_op jit(solution)/shard_map/select/pallas_call | solution.py:265
  41.6 4.4 %all-to-all-start.1 = ((f32[32,2,24,128]{3,2,1,0:T(8,128)}), f32[32,2,24,128]{3,2,1,0:T(8,128)S(1)}, u32[]{:S(2)}, u32[]{:S(2)}) async-start(f32[32,2,24,128]{3,2,1,0:T(8,128)} %bitcast.4), calls=%async_computation.1 | async-start | bytes 1572864 | tf_op jit(solution)/shard_map/all_to_all | solution.py:273
  46.1 0.0 copy-start.5
  46.1 0.6 copy-done.5
  46.7 0.6 dynamic-slice
  48.0 0.1 slice_reduce_fusion
  48.1 0.2 dynamic-update-slice
  48.3 82.9 %all-reduce = f32[128]{0:T(128)S(1)} all-reduce(f32[128]{0:T(128)S(1)} %dynamic-update-slice), channel_id=2, replica_groups=mesh['mem'=32,'gx'=2,'gy'=2] {'mem'}, use_global_device_ids=true, to_apply=%add | all-reduce | flops 128 | bytes 1024
  131.2 0.7 reduce_max.9
  131.9 1.3 exponential_reduce_fusion
  133.9 1.3 subtract_reduce_fusion
  135.2 0.0 all-to-all-done.1
  135.2 0.9 copy.8
  (1 shorter events, 0.0 us)
Async XLA Ops:
  0.6 1.1 copy-start
  1.8 0.9 copy-start.1
  3.0 9.8 %collective-permute-start.1 = (f32[128,128]{1,0:T(8,128)S(1)}, f32[128,128]{1,0:T(8,128)S(1)}, u32[]{:S(2)}, u32[]{:S(2)}) collective-permute-start(f32[128,128]{1,0:T(8,128)S(1)} %get-tuple-element.14), channel_id=1, source_target_pairs={{0,1},{1,0},{2,3},{3,2},{4,5},{5,4},{6,7},{7,6},{8,9},{9,8},{10,11... | collective-permute-start | bytes 196616 | tf_op jit(solution)/shard_map/ppermute | solution.py:233
  7.0 5.7 %collective-permute-start = (f32[14,8,128]{2,1,0:T(8,128)S(1)}, f32[14,8,128]{2,1,0:T(8,128)S(1)}, u32[]{:S(2)}, u32[]{:S(2)}) collective-permute-start(f32[14,8,128]{2,1,0:T(8,128)S(1)} %get-tuple-element.13), channel_id=1, source_target_pairs={{0,2},{2,0},{1,3},{3,1},{4,6},{6,4},{5,7},{7,5},{8,10},{10,8},{9,1... | collective-permute-start | bytes 172040 | tf_op jit(solution)/shard_map/ppermute | solution.py:235
  7.0 5.7 %collective-permute-start.2 = (f32[8,128]{1,0:T(8,128)S(1)}, f32[8,128]{1,0:T(8,128)S(1)}, u32[]{:S(2)}, u32[]{:S(2)}) collective-permute-start(f32[8,128]{1,0:T(8,128)S(1)} %get-tuple-element.15), channel_id=1, source_target_pairs={{0,3},{1,2},{2,1},{3,0},{4,7},{5,6},{6,5},{7,4},{8,11},{9,10},{10,... | collective-permute-start | bytes 12296 | tf_op jit(solution)/shard_map/ppermute | solution.py:234
  7.3 5.5 %copy-start.3 = (f32[1,1,256]{2,1,0:T(1,128)S(1)}, f32[1,1,256]{2,1,0:T(1,128)}, u32[]{:S(2)}) copy-start(f32[1,1,256]{2,1,0:T(1,128)} %param.9) | copy-start | bytes 3076
  12.8 0.7 copy-start.2
  39.4 0.7 copy-start.4
  41.6 93.6 %all-to-all-start.1 = ((f32[32,2,24,128]{3,2,1,0:T(8,128)}), f32[32,2,24,128]{3,2,1,0:T(8,128)S(1)}, u32[]{:S(2)}, u32[]{:S(2)}) async-start(f32[32,2,24,128]{3,2,1,0:T(8,128)} %bitcast.4), calls=%async_computation.1 | async-start | bytes 1572864 | tf_op jit(solution)/shard_map/all_to_all | solution.py:273
  46.1 0.7 copy-start.5

commit v2 on v1

--- a/solution.py
+++ b/solution.py
@@ -129,8 +129,8 @@
             owncol[f, t : t + CHUNK] = own_columns(tiles)
 
 
-def merge_kernel(total_y, inner, ownrow, owncol, rowrecv, colrecv, cornrecv, cells, values,
-                 out, logw, rs, rs1, cs, cs1, eta_s):
+def merge_kernel(total_y, devices, inner, ownrow, owncol, rowrecv, colrecv, cornrecv, cells, values,
+                 out, rs, rs1, cs, cs1, eta_s):
     members = inner.shape[0]
     tall = T + 16
     l32 = lax.rem(lanes((1, T)), 32)
@@ -166,6 +166,8 @@
     twice(rs, rs1, T, cor_row)
     twice(cs, cs1, tall, cor_col)
 
+    per = 96 // devices
+    stride = members // 2 * 8 * per + 1
     top = subl((8, T)) < 4
     left = lanes((8, T)) < 4
     right = lanes((8, T)) >= T - 4
@@ -182,8 +184,8 @@
                 a = jnp.where(left, lroll(col, 104 - 32 * m), a)
                 a = jnp.where(right, lroll(col, 120 - 32 * m), a)
                 k = mm * 48 + f * 16 + t
-                per = 96 // out.shape[0]
-                out[k // per, p, 8 * (k % per) : 8 * (k % per) + 8] = a
+                first = (k // per) * stride + p * 8 * per + 8 * (k % per)
+                out[first : first + 8] = a
                 if f == 0:
                     eta_s[m * T + 8 * t : m * T + 8 * t + 8] = a
 
@@ -191,21 +193,35 @@
     cell = cells[...]
     pick_y = (lax.broadcasted_iota(jnp.int32, (T, count), 0) == lax.rem(cell, T)).astype(F32)
     pick_x = lax.broadcasted_iota(jnp.int32, (T, count), 0) == cell // T
+    logw = jnp.zeros((1, T), F32)
     for m in range(members):
         seen = jnp.dot(eta_s[m * T : (m + 1) * T], pick_y, precision=lax.Precision.HIGHEST,
                        preferred_element_type=F32)
         seen = jnp.sum(jnp.where(pick_x, seen, 0.0), axis=0, keepdims=True)
         miss = seen - values[...]
         total = jnp.sum(miss * miss, axis=1, keepdims=True)
-        logw[m : m + 1] = jnp.broadcast_to(-0.5 * total / OBS_VAR, (1, T))
-
-
-def select_kernel(lineage, recv, out):
+        logw = jnp.where(lanes((1, T)) == m, -0.5 * total / OBS_VAR, logw)
+    for j in range(devices):
+        out[(j + 1) * stride - 1 : (j + 1) * stride] = logw
+
+
+def select_kernel(members, devices, lineage, recv, out, log_weights):
+    pairs, rows = members // 2 * devices, out.shape[1]
+    stride = members // 2 * rows + 1
+
     def body(k, carry):
-        out[k] = recv[lineage[k]]
+        pair = lineage[k]
+        first = lax.div(pair, members // 2) * stride + lax.rem(pair, members // 2) * rows
+        out[k] = recv[pl.ds(first, rows)]
         return carry
 
-    lax.fori_loop(0, recv.shape[0], body, 0, unroll=8)
+    lax.fori_loop(0, pairs, body, 0, unroll=8)
+    logw = recv[pl.ds(stride - 1, devices, stride)]
+    logw = jnp.where(lanes(logw.shape) < members, logw, -jnp.inf)
+    peak = jnp.max(jnp.max(logw, axis=1, keepdims=True), axis=0, keepdims=True)
+    total = jnp.sum(jnp.sum(jnp.exp(logw - peak), axis=1, keepdims=True), axis=0, keepdims=True)
+    own = recv[pl.ds(lax.axis_index("mem") * stride + stride - 1, 1)]
+    log_weights[0] = (own - peak - jnp.log(total))[:, :members]
 
 
 VM = pl.BlockSpec(memory_space=pltpu.VMEM)
@@ -243,12 +259,13 @@
         cost_estimate=pl.CostEstimate(flops=50_000_000, bytes_accessed=2_500_000, transcendentals=0),
         name="interior",
     )(fields, noise)
-    rows = members // 2 * 96 // devices * 4
-    pieces, logw = pl.pallas_call(
-        functools.partial(merge_kernel, total_y),
-        out_shape=(sds(devices, members // 2, 768 // devices, T), sds(members, T)),
+    rows = 768 // devices
+    stride = members // 2 * rows + 1
+    pieces = pl.pallas_call(
+        functools.partial(merge_kernel, total_y, devices),
+        out_shape=sds(devices * stride, T),
         in_specs=[VM] * 8,
-        out_specs=[VM] * 2,
+        out_specs=VM,
         scratch_shapes=[
             pltpu.VMEM((4, T, T), F32),
             pltpu.VMEM((3, T, T), F32),
@@ -259,22 +276,17 @@
         compiler_params=PARAMS,
         name="merge",
     )(inner, ownrow, owncol, rowrecv, colrecv, cornrecv, obs_cells.reshape(1, -1), obs_values.reshape(1, -1))
-    held = lax.all_to_all(pieces, "mem", 0, 0)
-    logw = logw[:, 0]
-    logw_all = lax.all_gather(logw, "mem")
-    picked = pl.pallas_call(
-        select_kernel,
-        out_shape=sds(devices * members // 2, 768 // devices, T),
+    held = lax.all_to_all(pieces.reshape(devices, stride, 1, T), "mem", 0, 0).reshape(devices * stride, T)
+    picked, log_weights = pl.pallas_call(
+        functools.partial(select_kernel, members, devices),
+        out_shape=(sds(devices * members // 2, rows, T), sds(1, 1, members)),
         in_specs=[SM, VM],
-        out_specs=VM,
+        out_specs=[VM] * 2,
         compiler_params=PARAMS,
         name="select",
-    )(ancestors.reshape(-1), held.reshape(devices * members // 2, 768 // devices, T))
-    back = lax.all_to_all(picked.reshape(held.shape), "mem", 0, 0)
+    )(ancestors.reshape(-1), held)
+    back = lax.all_to_all(picked.reshape(devices, members // 2, rows, T), "mem", 0, 0)
     resampled = back.transpose(1, 0, 2, 3).reshape(fields.shape)
-    peak = jnp.max(logw_all)
-    total = jnp.sum(jnp.exp(logw_all - peak))
-    log_weights = (logw - peak - jnp.log(total)).reshape(1, 1, members)
     return (resampled, log_weights)
 
 

time: 137 us -> 59.9 us (0.44)
  blocking collectives: 105 us -> 39.3 us
  starting transfers between devices: 8.69 us -> 4.26 us
  other arithmetic: 3.29 us -> 0 us
  local copies, waits for them, and re-layouts: 5.87 us -> 4.28 us
    unnamed x1 -> x0, blocking collectives: 82.9 us -> none
    all_to_all x1 -> x2, blocking collectives: 22.2 us -> 39.3 us  [the longest x1 22.4 us: shards(): lax.all_to_all(pieces.reshape(devices, stride, 1, T), 'mem', 0, 0)]
    all_to_all x1 -> x0, starting transfers between devices: 4.43 us -> none  [shards(): back = lax.all_to_all(picked.reshape(held.shape), 'mem', 0, 0)]
    unnamed x15 -> x10, local copies, waits for them, and re-layouts: 4.83 us -> 3.35 us
  transfers between devices with their start and end apart: 4 -> 3, of which waited for: 0 -> 0; matrix products, arithmetic and copies ran while one was open for 3% -> 0% of each run, Pallas kernels for 4% -> 9%
where the time goes in v2:
time: 59.9 us; the launch traced here: 59.6 us
  blocking collectives  39.3 us (66%)
  Pallas kernels  11.1 us (19%)
  local copies, waits for them, and re-layouts  4.28 us (7%)
  starting transfers between devices  4.26 us (7%)
  between operations  0.7 us (1%)
    all_to_all x1, blocking collectives, shards(): lax.all_to_all(pieces.reshape(devices, stride, 1, T), 'mem', 0, 0)  22.4 us
    all_to_all x1, blocking collectives, shards(): lax.all_to_all(picked.reshape(devices, members // 2, rows, T), 'mem', 0, 0)  16.9 us
    pallas_call x1, Pallas kernels, shards(): pl.pallas_call(functools.partial(interior_kernel, total_y), out_shape=(sd...  5.48 us
    ppermute x1, starting transfers between devices, shards(): colrecv = lax.ppermute(colpack, 'gy', swap)  4.04 us
    pallas_call x1, Pallas kernels, shards(): pl.pallas_call(functools.partial(merge_kernel, total_y, devices), out_sha...  3.75 us
    unnamed x10, local copies, waits for them, and re-layouts  3.35 us
    pallas_call x1, Pallas kernels, shards(): pl.pallas_call(functools.partial(select_kernel, members, devices), out_sh...  1.52 us
  transfers between devices with their start and end apart: 3, of which 0 were waited for; matrix products, arithmetic and copies ran while one was open for 0% of the time, Pallas kernels for 9%

profile of v2, /device:TPU:0, one launch (start us, length us, event | category | flops | bytes accessed | tf_op | source)
XLA Modules:
  0.0 59.6 jit_solution(6298839243737377054)
XLA Ops:
  0.6 0.0 copy-start
  0.6 1.1 %copy-done = f32[4,3,128,128]{3,2,1,0:T(8,128)S(1)} copy-done((f32[4,3,128,128]{3,2,1,0:T(8,128)S(1)}, f32[4,3,128,128]{3,2,1,0:T(8,128)}, u32[]{:S(2)}) %copy-start) | copy-done | bytes 786456
  1.8 0.0 copy-start.1
  1.8 0.9 %copy-done.1 = f32[2,128,128]{2,1,0:T(8,128)S(1)} copy-done((f32[2,128,128]{2,1,0:T(8,128)S(1)}, f32[2,128,128]{2,1,0:T(8,128)}, u32[]{:S(2)}) %copy-start.1) | copy-done | bytes 131096
  2.7 0.3 pack.1
  3.0 4.0 %collective-permute-start.1 = (f32[128,128]{1,0:T(8,128)S(1)}, f32[128,128]{1,0:T(8,128)S(1)}, u32[]{:S(2)}, u32[]{:S(2)}) collective-permute-start(f32[128,128]{1,0:T(8,128)S(1)} %get-tuple-element.14), channel_id=1, source_target_pairs={{0,1},{1,0},{2,3},{3,2},{4,5},{5,4},{6,7},{7,6},{8,9},{9,8},{10,11... | collective-permute-start | bytes 196616 | tf_op jit(solution)/shard_map/ppermute | solution.py:249
  7.0 0.0 collective-permute-start
  7.0 0.2 collective-permute-start.2
  7.3 0.0 copy-start.3
  7.3 5.5 %interior.1 = (f32[4,3,128,128]{3,2,1,0:T(8,128)S(1)}, f32[4,8,8,128]{3,2,1,0:T(8,128)S(1)}, f32[4,128,128]{2,1,0:T(8,128)S(1)}) custom-call(f32[4,3,128,128]{3,2,1,0:T(8,128)S(1)} %copy-done, f32[2,128,128]{2,1,0:T(8,128)S(1)} %copy-done.1), custom_call_target="tpu_custom_call" | custom-call | flops 50000000 | bytes 2500000 | tf_op jit(solution)/shard_map/interior/pallas_call | solution.py:252
  12.8 0.0 collective-permute-done.2.cornrecv
  12.8 0.0 collective-permute-done.rowrecv
  12.8 0.0 collective-permute-done.1.colrecv
  12.8 0.0 copy-start.2
  12.8 0.0 copy-done.3
  12.8 0.7 %copy-done.2 = s32[1,1,256]{2,1,0:T(1,128)S(1)} copy-done((s32[1,1,256]{2,1,0:T(1,128)S(1)}, s32[1,1,256]{2,1,0:T(1,128)}, u32[]{:S(2)}) %copy-start.2) | copy-done | bytes 1048
  13.5 3.8 %merge.1 = f32[1568,128]{1,0:T(8,128)S(1)} custom-call(f32[4,3,128,128]{3,2,1,0:T(8,128)S(1)} %get-tuple-element.10.inner, f32[4,8,8,128]{3,2,1,0:T(8,128)S(1)} %get-tuple-element.11.ownrow, f32[4,128,128]{2,1,0:T(8,128)S(1)} %get-tuple-element.12.owncol, f32[14,8,128]{2,1,0:T(8,128)S(1)} %collective-permute-done.rowrecv, ...), custom_call_target="tpu_custom_call" | custom-call | tf_op jit(solution)/shard_map/merge/pallas_call | solution.py:264
  17.2 22.4 %all_to_all.10 = f32[32,49,1,128]{3,2,1,0:T(1,128)S(1)} all-to-all(f32[32,49,1,128]{3,2,1,0:T(1,128)S(1)} %bitcast.8), channel_id=1, replica_groups=mesh['mem'=32,'gx'=2,'gy'=2] {'mem'}, dimensions={0} | all-to-all | bytes 1605632 | tf_op jit(solution)/shard_map/all_to_all | solution.py:279
  39.6 0.0 copy-start.4
  39.6 0.7 %copy-done.4 = s32[1,1,64]{2,1,0:T(1,128)S(1)} copy-done((s32[1,1,64]{2,1,0:T(1,128)S(1)}, s32[1,1,64]{2,1,0:T(1,128)}, u32[]{:S(2)}) %copy-start.4) | copy-done | bytes 280
  40.3 1.5 %select.1 = (f32[64,24,128]{2,1,0:T(8,128)S(1)}, f32[1,1,4]{2,1,0:T(1,128)}) custom-call(s32[64]{0:T(128)S(1)} %bitcast.13, f32[1568,128]{1,0:T(8,128)S(1)} %bitcast.9), custom_call_target="tpu_custom_call" | custom-call | tf_op jit(solution)/shard_map/select/pallas_call | solution.py:280
  41.8 16.9 %all_to_all.11 = f32[32,2,24,128]{3,2,1,0:T(8,128)S(1)} all-to-all(f32[32,2,24,128]{3,2,1,0:T(8,128)S(1)} %bitcast.10), channel_id=1, replica_groups=mesh['mem'=32,'gx'=2,'gy'=2] {'mem'}, dimensions={0} | all-to-all | bytes 1572864 | tf_op jit(solution)/shard_map/all_to_all | solution.py:288
  58.7 0.9 %copy.10 = f32[2,32,24,128]{3,2,1,0:T(8,128)} copy(f32[2,32,24,128]{3,2,0,1:T(8,128)S(1)} %bitcast.14) | data formatting | bytes 1572864 | tf_op jit(solution)/shard_map/transpose | solution.py:289
Async XLA Ops:
  0.6 1.1 %copy-start = (f32[4,3,128,128]{3,2,1,0:T(8,128)S(1)}, f32[4,3,128,128]{3,2,1,0:T(8,128)}, u32[]{:S(2)}) copy-start(f32[4,3,128,128]{3,2,1,0:T(8,128)} %fields.3) | copy-start | bytes 2359300
  1.8 0.9 %copy-start.1 = (f32[2,128,128]{2,1,0:T(8,128)S(1)}, f32[2,128,128]{2,1,0:T(8,128)}, u32[]{:S(2)}) copy-start(f32[2,128,128]{2,1,0:T(8,128)} %noise.3) | copy-start | bytes 393220
  3.0 9.8 %collective-permute-start.1 = (f32[128,128]{1,0:T(8,128)S(1)}, f32[128,128]{1,0:T(8,128)S(1)}, u32[]{:S(2)}, u32[]{:S(2)}) collective-permute-start(f32[128,128]{1,0:T(8,128)S(1)} %get-tuple-element.14), channel_id=1, source_target_pairs={{0,1},{1,0},{2,3},{3,2},{4,5},{5,4},{6,7},{7,6},{8,9},{9,8},{10,11... | collective-permute-start | bytes 196616 | tf_op jit(solution)/shard_map/ppermute | solution.py:249
  7.0 5.7 %collective-permute-start = (f32[14,8,128]{2,1,0:T(8,128)S(1)}, f32[14,8,128]{2,1,0:T(8,128)S(1)}, u32[]{:S(2)}, u32[]{:S(2)}) collective-permute-start(f32[14,8,128]{2,1,0:T(8,128)S(1)} %get-tuple-element.13), channel_id=1, source_target_pairs={{0,2},{2,0},{1,3},{3,1},{4,6},{6,4},{5,7},{7,5},{8,10},{10,8},{9,1... | collective-permute-start | bytes 172040 | tf_op jit(solution)/shard_map/ppermute | solution.py:251
  7.0 5.7 %collective-permute-start.2 = (f32[8,128]{1,0:T(8,128)S(1)}, f32[8,128]{1,0:T(8,128)S(1)}, u32[]{:S(2)}, u32[]{:S(2)}) collective-permute-start(f32[8,128]{1,0:T(8,128)S(1)} %get-tuple-element.15), channel_id=1, source_target_pairs={{0,3},{1,2},{2,1},{3,0},{4,7},{5,6},{6,5},{7,4},{8,11},{9,10},{10,... | collective-permute-start | bytes 12296 | tf_op jit(solution)/shard_map/ppermute | solution.py:250
  7.3 5.5 %copy-start.3 = (f32[1,1,256]{2,1,0:T(1,128)S(1)}, f32[1,1,256]{2,1,0:T(1,128)}, u32[]{:S(2)}) copy-start(f32[1,1,256]{2,1,0:T(1,128)} %param.9) | copy-start | bytes 3076
  12.8 0.7 %copy-start.2 = (s32[1,1,256]{2,1,0:T(1,128)S(1)}, s32[1,1,256]{2,1,0:T(1,128)}, u32[]{:S(2)}) copy-start(s32[1,1,256]{2,1,0:T(1,128)} %param.8) | copy-start | bytes 3076
  39.6 0.7 %copy-start.4 = (s32[1,1,64]{2,1,0:T(1,128)S(1)}, s32[1,1,64]{2,1,0:T(1,128)}, u32[]{:S(2)}) copy-start(s32[1,1,64]{2,1,0:T(1,128)} %param.7) | copy-start | bytes 772

commit v3 on v2

--- a/solution.py
+++ b/solution.py
@@ -12,7 +12,7 @@
 OBS_VAR = 0.25
 T = 128
 F32 = jnp.float32
-CHUNK = 16
+CHUNK = 64
 
 
 def lanes(shape):
@@ -70,23 +70,28 @@
     return 0.1 + 0.2 * ((y.astype(F32) + 0.5) / total_y - 0.5)
 
 
-def pack_kernel(fields, noise, rowpack, colpack, cornpack):
+def pack_kernel(fields_hbm, noise_hbm, fields, noise, rowpack, colpack, cornpack, sems):
     members = fields.shape[0]
+    copies = [pltpu.make_async_copy(noise_hbm, noise, sems.at[members])]
+    for m in range(members):
+        copies.append(pltpu.make_async_copy(fields_hbm.at[m], fields.at[m], sems.at[m]))
+    for copy in copies:
+        copy.start()
+    copies[0].wait()
     top = subl((8, T)) < 4
-    for m in range(members):
+    ln = lanes((T, T)) // 8
+    for p in range(members // 2):
+        rowpack[3 * members + p] = jnp.where(top, noise[p, 0:8], noise[p, T - 8 : T])
+    acc = jnp.zeros((T, T), F32)
+    for m in range(members):
+        acc = jnp.where(ln == 4 * m + 3, lroll(noise[m // 2], 32 * m + 28), acc)
+    for m in range(members):
+        copies[1 + m].wait()
         for f in range(3):
             rowpack[3 * m + f] = jnp.where(top, fields[m, f, 0:8], fields[m, f, T - 8 : T])
-    for p in range(members // 2):
-        rowpack[3 * members + p] = jnp.where(top, noise[p, 0:8], noise[p, T - 8 : T])
-    for t in range(0, T, CHUNK):
-        ln = lanes((CHUNK, T)) // 8
-        acc = jnp.zeros((CHUNK, T), F32)
-        for m in range(members):
-            for f in range(4):
-                src = fields[m, f, t : t + CHUNK] if f < 3 else noise[m // 2, t : t + CHUNK]
-                acc = jnp.where(ln == 4 * m + f, lroll(src, 32 * m + 8 * f + 4), acc)
-        colpack[t : t + CHUNK] = acc
-    cornpack[...] = jnp.where(top, colpack[0:8], colpack[T - 8 : T])
+            acc = jnp.where(ln == 4 * m + f, lroll(fields[m, f], 32 * m + 8 * f + 4), acc)
+    colpack[...] = acc
+    cornpack[...] = jnp.where(top, acc[0:8], acc[T - 8 : T])
 
 
 def own_columns(tiles):
@@ -99,38 +104,43 @@
     return acc
 
 
-def interior_kernel(total_y, fields, noise, inner, ownrow, owncol, tmp):
+def interior_kernel(total_y, fields, noise, cells_hbm, values_hbm, inner, ownrow, owncol, pick_y, cell_x,
+                    values, tmp, cells, sems):
     members = fields.shape[0]
+    copies = [
+        pltpu.make_async_copy(cells_hbm, cells, sems.at[0]),
+        pltpu.make_async_copy(values_hbm, values, sems.at[1]),
+    ]
+    for copy in copies:
+        copy.start()
     cor = coriolis(lanes((1, T)), total_y)
-
-    def body(m, carry):
-        for r in range(0, T, CHUNK):
-            new = one_step(fields, (m,), r, CHUNK, T, noise[m // 2, pl.ds(r, CHUNK)], cor)
-            for f in range(3):
-                tmp[f, pl.ds(r, CHUNK)] = new[f]
-        for r in range(0, T, CHUNK):
-            new = one_step(tmp, (), r, CHUNK, T, noise[m // 2, pl.ds(r, CHUNK)], cor)
-            for f in range(3):
-                inner[m, f, pl.ds(r, CHUNK)] = new[f]
-        return carry
-
-    lax.fori_loop(0, members, body, 0)
+    for src, dst in ((fields, tmp), (tmp, inner)):
+        for m in range(members):
+            for r in range(0, T, CHUNK):
+                new = one_step(src, (m,), r, CHUNK, T, noise[m // 2, r : r + CHUNK], cor)
+                for f in range(3):
+                    dst[m, f, r : r + CHUNK] = new[f]
     for m in range(members):
         for f in range(4):
             src = fields.at[m, f] if f < 3 else noise.at[m // 2]
             ownrow[f, 2 * m] = src[0:8]
             ownrow[f, 2 * m + 1] = src[T - 8 : T]
     for f in range(4):
-        for t in range(0, T, CHUNK):
-            tiles = []
-            for m in range(members):
-                src = fields.at[m, f] if f < 3 else noise.at[m // 2]
-                tiles.append(src[t : t + CHUNK])
-            owncol[f, t : t + CHUNK] = own_columns(tiles)
-
-
-def merge_kernel(total_y, devices, inner, ownrow, owncol, rowrecv, colrecv, cornrecv, cells, values,
-                 out, rs, rs1, cs, cs1, eta_s):
+        tiles = []
+        for m in range(members):
+            src = fields.at[m, f] if f < 3 else noise.at[m // 2]
+            tiles.append(src[...])
+        owncol[f] = own_columns(tiles)
+    for copy in copies:
+        copy.wait()
+    cell = cells[...]
+    line_y = lax.broadcasted_iota(jnp.int32, pick_y.shape, 0)
+    pick_y[...] = jnp.where(line_y == lax.rem(cell, T), 1.0, 0.0).astype(pick_y.dtype)
+    cell_x[...] = cell // T
+
+
+def merge_kernel(total_y, devices, inner, ownrow, owncol, rowrecv, colrecv, cornrecv, pick_y, cell_x,
+                 values, out, rs, rs1, cs, cs1, eta_s):
     members = inner.shape[0]
     tall = T + 16
     l32 = lax.rem(lanes((1, T)), 32)
@@ -153,15 +163,15 @@
         ends = with_halo(own_columns(tiles), cornrecv[...])
         cs[f, 0:8] = ends
         cs[f, T + 8 : T + 16] = ends
-        for t in range(0, T, CHUNK):
-            cs[f, t + 8 : t + 8 + CHUNK] = with_halo(owncol[f, t : t + CHUNK], colrecv[t : t + CHUNK])
+        cs[f, 8 : T + 8] = with_halo(owncol[f], colrecv[...])
 
     def twice(a, a1, total, cor):
+        chunk = total // 2
         for src, dst in ((a, a1), (a1, a)):
-            for r in range(0, total, CHUNK):
-                new = one_step(src, (), r, CHUNK, total, a[3, r : r + CHUNK], cor)
+            for r in range(0, total, chunk):
+                new = one_step(src, (), r, chunk, total, a[3, r : r + chunk], cor)
                 for f in range(3):
-                    dst[f, r : r + CHUNK] = new[f]
+                    dst[f, r : r + chunk] = new[f]
 
     twice(rs, rs1, T, cor_row)
     twice(cs, cs1, tall, cor_col)
@@ -189,44 +199,53 @@
                 if f == 0:
                     eta_s[m * T + 8 * t : m * T + 8 * t + 8] = a
 
-    count = cells.shape[1]
-    cell = cells[...]
-    pick_y = (lax.broadcasted_iota(jnp.int32, (T, count), 0) == lax.rem(cell, T)).astype(F32)
-    pick_x = lax.broadcasted_iota(jnp.int32, (T, count), 0) == cell // T
+    eta = eta_s[...]
+    hi = eta.astype(jnp.bfloat16)
+    rest = eta - hi.astype(F32)
+    mid = rest.astype(jnp.bfloat16)
+    low = (rest - mid.astype(F32)).astype(jnp.bfloat16)
+    dot = lambda part: jnp.dot(part, pick_y[...], preferred_element_type=F32)
+    seen = dot(hi) + (dot(mid) + dot(low))
+    pick_x = lax.broadcasted_iota(jnp.int32, pick_y.shape, 0) == cell_x[...]
     logw = jnp.zeros((1, T), F32)
     for m in range(members):
-        seen = jnp.dot(eta_s[m * T : (m + 1) * T], pick_y, precision=lax.Precision.HIGHEST,
-                       preferred_element_type=F32)
-        seen = jnp.sum(jnp.where(pick_x, seen, 0.0), axis=0, keepdims=True)
-        miss = seen - values[...]
+        at = jnp.sum(jnp.where(pick_x, seen[m * T : (m + 1) * T], 0.0), axis=0, keepdims=True)
+        miss = at - values[...]
         total = jnp.sum(miss * miss, axis=1, keepdims=True)
         logw = jnp.where(lanes((1, T)) == m, -0.5 * total / OBS_VAR, logw)
     for j in range(devices):
         out[(j + 1) * stride - 1 : (j + 1) * stride] = logw
 
 
-def select_kernel(members, devices, lineage, recv, out, log_weights):
+def select_kernel(members, devices, lineage_hbm, recv, out, log_weights, lineage, sem):
+    copy = pltpu.make_async_copy(lineage_hbm, lineage, sem)
+    copy.start()
     pairs, rows = members // 2 * devices, out.shape[1]
     stride = members // 2 * rows + 1
-
-    def body(k, carry):
-        pair = lineage[k]
-        first = lax.div(pair, members // 2) * stride + lax.rem(pair, members // 2) * rows
-        out[k] = recv[pl.ds(first, rows)]
-        return carry
-
-    lax.fori_loop(0, pairs, body, 0, unroll=8)
     logw = recv[pl.ds(stride - 1, devices, stride)]
     logw = jnp.where(lanes(logw.shape) < members, logw, -jnp.inf)
     peak = jnp.max(jnp.max(logw, axis=1, keepdims=True), axis=0, keepdims=True)
     total = jnp.sum(jnp.sum(jnp.exp(logw - peak), axis=1, keepdims=True), axis=0, keepdims=True)
     own = recv[pl.ds(lax.axis_index("mem") * stride + stride - 1, 1)]
     log_weights[0] = (own - peak - jnp.log(total))[:, :members]
+    copy.wait()
+
+    def body(k, carry):
+        pair = lineage[0, k]
+        first = lax.div(pair, members // 2) * stride + lax.rem(pair, members // 2) * rows
+        out[k] = recv[pl.ds(first, rows)]
+        return carry
+
+    lax.fori_loop(0, pairs, body, 0, unroll=8)
 
 
 VM = pl.BlockSpec(memory_space=pltpu.VMEM)
-SM = pl.BlockSpec(memory_space=pltpu.SMEM)
+HB = pl.BlockSpec(memory_space=pltpu.MemorySpace.HBM)
 PARAMS = pltpu.CompilerParams(vmem_limit_bytes=24 << 20)
+
+
+def in_hbm(a):
+    return pltpu.with_memory_space_constraint(a, pltpu.MemorySpace.HBM)
 
 
 def sds(*shape):
@@ -237,34 +256,53 @@
     members = fields.shape[0]
     devices = lax.axis_size("mem")
     total_y = T * lax.axis_size("gy")
-    rowpack, colpack, cornpack = pl.pallas_call(
+    fields_vm, noise_vm, rowpack, colpack, cornpack = pl.pallas_call(
         pack_kernel,
-        out_shape=(sds(3 * members + members // 2, 8, T), sds(T, T), sds(8, T)),
-        in_specs=[VM] * 2,
-        out_specs=[VM] * 3,
+        out_shape=(
+            sds(*fields.shape),
+            sds(*noise.shape),
+            sds(3 * members + members // 2, 8, T),
+            sds(T, T),
+            sds(8, T),
+        ),
+        in_specs=[HB] * 2,
+        out_specs=[VM] * 5,
+        scratch_shapes=[pltpu.SemaphoreType.DMA((members + 1,))],
         compiler_params=PARAMS,
         name="pack",
-    )(fields, noise)
+    )(in_hbm(fields), in_hbm(noise))
     swap = [(0, 1), (1, 0)]
     colrecv = lax.ppermute(colpack, "gy", swap)
     cornrecv = lax.ppermute(cornpack, ("gx", "gy"), [(0, 3), (1, 2), (2, 1), (3, 0)])
     rowrecv = lax.ppermute(rowpack, "gx", swap)
-    inner, ownrow, owncol = pl.pallas_call(
+    count = obs_cells.shape[-1]
+    inner, ownrow, owncol, pick_y, cell_x, values = pl.pallas_call(
         functools.partial(interior_kernel, total_y),
-        out_shape=(sds(members, 3, T, T), sds(4, 2 * members, 8, T), sds(4, T, T)),
-        in_specs=[VM] * 2,
-        out_specs=[VM] * 3,
-        scratch_shapes=[pltpu.VMEM((3, T, T), F32)],
+        out_shape=(
+            sds(members, 3, T, T),
+            sds(4, 2 * members, 8, T),
+            sds(4, T, T),
+            jax.ShapeDtypeStruct((T, count), jnp.bfloat16),
+            jax.ShapeDtypeStruct((1, count), jnp.int32),
+            sds(1, count),
+        ),
+        in_specs=[VM] * 2 + [HB] * 2,
+        out_specs=[VM] * 6,
+        scratch_shapes=[
+            pltpu.VMEM((members, 3, T, T), F32),
+            pltpu.VMEM((1, count), jnp.int32),
+            pltpu.SemaphoreType.DMA((2,)),
+        ],
         compiler_params=PARAMS,
         cost_estimate=pl.CostEstimate(flops=50_000_000, bytes_accessed=2_500_000, transcendentals=0),
         name="interior",
-    )(fields, noise)
+    )(fields_vm, noise_vm, in_hbm(obs_cells.reshape(1, -1)), in_hbm(obs_values.reshape(1, -1)))
     rows = 768 // devices
     stride = members // 2 * rows + 1
     pieces = pl.pallas_call(
         functools.partial(merge_kernel, total_y, devices),
         out_shape=sds(devices * stride, T),
-        in_specs=[VM] * 8,
+        in_specs=[VM] * 9,
         out_specs=VM,
         scratch_shapes=[
             pltpu.VMEM((4, T, T), F32),
@@ -275,16 +313,17 @@
         ],
         compiler_params=PARAMS,
         name="merge",
-    )(inner, ownrow, owncol, rowrecv, colrecv, cornrecv, obs_cells.reshape(1, -1), obs_values.reshape(1, -1))
+    )(inner, ownrow, owncol, rowrecv, colrecv, cornrecv, pick_y, cell_x, values)
     held = lax.all_to_all(pieces.reshape(devices, stride, 1, T), "mem", 0, 0).reshape(devices * stride, T)
     picked, log_weights = pl.pallas_call(
         functools.partial(select_kernel, members, devices),
         out_shape=(sds(devices * members // 2, rows, T), sds(1, 1, members)),
-        in_specs=[SM, VM],
+        in_specs=[HB, VM],
         out_specs=[VM] * 2,
+        scratch_shapes=[pltpu.SMEM((1, devices * members // 2), jnp.int32), pltpu.SemaphoreType.DMA],
         compiler_params=PARAMS,
         name="select",
-    )(ancestors.reshape(-1), held)
+    )(in_hbm(ancestors.reshape(1, -1)), held)
     back = lax.all_to_all(picked.reshape(devices, members // 2, rows, T), "mem", 0, 0)
     resampled = back.transpose(1, 0, 2, 3).reshape(fields.shape)
     return (resampled, log_weights)

time: 59.9 us -> 55.2 us (0.922)
  local copies, waits for them, and re-layouts: 4.28 us -> 0.93 us
  Pallas kernels: 11.1 us -> 8.38 us
  waiting for transfers between devices: 0.01 us -> 0.84 us
  blocking collectives: 39.3 us -> 39.9 us
    unnamed x10 -> x0, local copies, waits for them, and re-layouts: 3.35 us -> none
    pallas_call x1, Pallas kernels: 5.48 us -> 3.48 us  [shards(): pl.pallas_call(functools.partial(interior_kernel, total_y), out_shape=(sd...]
    pallas_call x1, Pallas kernels: 3.75 us -> 1.87 us  [shards(): pl.pallas_call(functools.partial(merge_kernel, total_y, devices), out_sha...]
    pallas_call x1, Pallas kernels: 0.33 us -> 1.56 us  [shards(): pl.pallas_call(pack_kernel, out_shape=(sds(*fields.shape), sds(*noise.sha...]
    ppermute x1, waiting for transfers between devices: 0.01 us -> 0.83 us  [shards(): lax.ppermute(cornpack, ('gx', 'gy'), [(0, 3), (1, 2), (2, 1), (3, 0)])]
  transfers between devices with their start and end apart: 3 -> 3, of which waited for: 0 -> 1; matrix products, arithmetic and copies ran while one was open for 0% -> 0% of each run, Pallas kernels for 9% -> 6%
where the time goes in v3:
time: 55.2 us; the launch traced here: 55 us
  blocking collectives  39.9 us (72%)
  Pallas kernels  8.38 us (15%)
  starting transfers between devices  4.26 us (8%)
  local copies, waits for them, and re-layouts  0.93 us (2%)
  waiting for transfers between devices  0.84 us (2%)
  between operations  0.66 us (1%)
    all_to_all x1, blocking collectives, shards(): lax.all_to_all(pieces.reshape(devices, stride, 1, T), 'mem', 0, 0)  22.5 us
    all_to_all x1, blocking collectives, shards(): lax.all_to_all(picked.reshape(devices, members // 2, rows, T), 'mem', 0, 0)  17.4 us
    ppermute x1, starting transfers between devices, shards(): colrecv = lax.ppermute(colpack, 'gy', swap)  4.04 us
    pallas_call x1, Pallas kernels, shards(): pl.pallas_call(functools.partial(interior_kernel, total_y), out_shape=(sd...  3.48 us
    pallas_call x1, Pallas kernels, shards(): pl.pallas_call(functools.partial(merge_kernel, total_y, devices), out_sha...  1.87 us
    pallas_call x1, Pallas kernels, shards(): pl.pallas_call(pack_kernel, out_shape=(sds(*fields.shape), sds(*noise.sha...  1.56 us
    pallas_call x1, Pallas kernels, shards(): pl.pallas_call(functools.partial(select_kernel, members, devices), out_sh...  1.47 us
  transfers between devices with their start and end apart: 3, of which 1 were waited for; matrix products, arithmetic and copies ran while one was open for 0% of the time, Pallas kernels for 6%

profile of v3, /device:TPU:0, one launch (start us, length us, event | category | flops | bytes accessed | tf_op | source)
XLA Modules:
  0.0 55.0 jit_solution(13141357597646591585)
XLA Ops:
  0.6 1.6 %pack.1 = (f32[4,3,128,128]{3,2,1,0:T(8,128)S(1)}, f32[2,128,128]{2,1,0:T(8,128)S(1)}, f32[14,8,128]{2,1,0:T(8,128)S(1)}, f32[128,128]{1,0:T(8,128)S(1)}, f32[8,128]{1,0:T(8,128)S(1)}) custom-call(f32[4,3,128,128]{3,2,1,0:T(8,128)} %fields_hbm.1, f32[2,128,128]{2,1,0:T(8,128)} %noise_hbm.1), custom_call_target="tpu_custom_call" | custom-call | tf_op jit(solution)/shard_map/pack/pallas_call | solution.py:259
  2.2 4.0 %collective-permute-start.1 = (f32[128,128]{1,0:T(8,128)S(1)}, f32[128,128]{1,0:T(8,128)S(1)}, u32[]{:S(2)}, u32[]{:S(2)}) collective-permute-start(f32[128,128]{1,0:T(8,128)S(1)} %get-tuple-element.21), channel_id=1, source_target_pairs={{0,1},{1,0},{2,3},{3,2},{4,5},{5,4},{6,7},{7,6},{8,9},{9,8},{10,11... | collective-permute-start | bytes 196616 | tf_op jit(solution)/shard_map/ppermute | solution.py:275
  6.2 0.0 collective-permute-start
  6.2 0.2 collective-permute-start.2
  6.5 3.5 %interior.1 = (f32[4,3,128,128]{3,2,1,0:T(8,128)S(1)}, f32[4,8,8,128]{3,2,1,0:T(8,128)S(1)}, f32[4,128,128]{2,1,0:T(8,128)S(1)}, bf16[128,256]{1,0:T(8,128)(2,1)...) custom-call(f32[4,3,128,128]{3,2,1,0:T(8,128)S(1)} %get-tuple-element.15.fields, ...), custom_call_target="tpu_custom_call" | custom-call | flops 50000000 | bytes 2500000 | tf_op jit(solution)/shard_map/interior/pallas_call | solution.py:279
  9.9 0.8 %collective-permute-done.2.cornrecv = f32[8,128]{1,0:T(8,128)S(1)} collective-permute-done((f32[8,128]{1,0:T(8,128)S(1)}, f32[8,128]{1,0:T(8,128)S(1)}, u32[]{:S(2)}, u32[]{:S(2)}) %collective-permute-start.2) | collective-permute-done | bytes 4128 | tf_op jit(solution)/shard_map/ppermute | solution.py:276
  10.8 0.0 collective-permute-done.rowrecv
  10.8 0.0 collective-permute-done.1.colrecv
  10.8 1.9 %merge.1 = f32[1568,128]{1,0:T(8,128)S(1)} custom-call(f32[4,3,128,128]{3,2,1,0:T(8,128)S(1)} %get-tuple-element.17.inner, f32[4,8,8,128]{3,2,1,0:T(8,128)S(1)} %get-tuple-element.18.ownrow, f32[4,128,128]{2,1,0:T(8,128)S(1)} %get-tuple-element.19.owncol, f32[14,8,128]{2,1,0:T(8,128)S(1)} %collective-permute-done.rowrecv, ...), custom_call_target="tpu_custom_call" | custom-call | tf_op jit(solution)/shard_map/merge/pallas_call | solution.py:302
  12.7 22.5 %all_to_all.10 = f32[32,49,1,128]{3,2,1,0:T(1,128)S(1)} all-to-all(f32[32,49,1,128]{3,2,1,0:T(1,128)S(1)} %bitcast.8), channel_id=1, replica_groups=mesh['mem'=32,'gx'=2,'gy'=2] {'mem'}, dimensions={0} | all-to-all | bytes 1605632 | tf_op jit(solution)/shard_map/all_to_all | solution.py:317
  35.1 1.5 %select.1 = (f32[64,24,128]{2,1,0:T(8,128)S(1)}, f32[1,1,4]{2,1,0:T(1,128)}) custom-call(s32[1,64]{1,0:T(1,128)} %bitcast.15, f32[1568,128]{1,0:T(8,128)S(1)} %bitcast.9), custom_call_target="tpu_custom_call" | custom-call | tf_op jit(solution)/shard_map/select/pallas_call | solution.py:318
  36.6 17.4 %all_to_all.11 = f32[32,2,24,128]{3,2,1,0:T(8,128)S(1)} all-to-all(f32[32,2,24,128]{3,2,1,0:T(8,128)S(1)} %bitcast.10), channel_id=1, replica_groups=mesh['mem'=32,'gx'=2,'gy'=2] {'mem'}, dimensions={0} | all-to-all | bytes 1572864 | tf_op jit(solution)/shard_map/all_to_all | solution.py:327
  54.0 0.9 %copy.10 = f32[2,32,24,128]{3,2,1,0:T(8,128)} copy(f32[2,32,24,128]{3,2,0,1:T(8,128)S(1)} %bitcast.11) | data formatting | bytes 1572864 | tf_op jit(solution)/shard_map/transpose | solution.py:328
Async XLA Ops:
  2.2 8.6 %collective-permute-start.1 = (f32[128,128]{1,0:T(8,128)S(1)}, f32[128,128]{1,0:T(8,128)S(1)}, u32[]{:S(2)}, u32[]{:S(2)}) collective-permute-start(f32[128,128]{1,0:T(8,128)S(1)} %get-tuple-element.21), channel_id=1, source_target_pairs={{0,1},{1,0},{2,3},{3,2},{4,5},{5,4},{6,7},{7,6},{8,9},{9,8},{10,11... | collective-permute-start | bytes 196616 | tf_op jit(solution)/shard_map/ppermute | solution.py:275
  6.2 4.5 %collective-permute-start = (f32[14,8,128]{2,1,0:T(8,128)S(1)}, f32[14,8,128]{2,1,0:T(8,128)S(1)}, u32[]{:S(2)}, u32[]{:S(2)}) collective-permute-start(f32[14,8,128]{2,1,0:T(8,128)S(1)} %get-tuple-element.20), channel_id=1, source_target_pairs={{0,2},{2,0},{1,3},{3,1},{4,6},{6,4},{5,7},{7,5},{8,10},{10,8},{9,1... | collective-permute-start | bytes 172040 | tf_op jit(solution)/shard_map/ppermute | solution.py:277
  6.2 4.5 %collective-permute-start.2 = (f32[8,128]{1,0:T(8,128)S(1)}, f32[8,128]{1,0:T(8,128)S(1)}, u32[]{:S(2)}, u32[]{:S(2)}) collective-permute-start(f32[8,128]{1,0:T(8,128)S(1)} %get-tuple-element.22), channel_id=1, source_target_pairs={{0,3},{1,2},{2,1},{3,0},{4,7},{5,6},{6,5},{7,4},{8,11},{9,10},{10,... | collective-permute-start | bytes 12296 | tf_op jit(solution)/shard_map/ppermute | solution.py:276

commit v4 on v3

--- a/solution.py
+++ b/solution.py
@@ -70,7 +70,7 @@
     return 0.1 + 0.2 * ((y.astype(F32) + 0.5) / total_y - 0.5)
 
 
-def pack_kernel(fields_hbm, noise_hbm, fields, noise, rowpack, colpack, cornpack, sems):
+def pack_kernel(fields_hbm, noise_hbm, fields, noise, rowpack, colpack, cornpack, allpack, sems):
     members = fields.shape[0]
     copies = [pltpu.make_async_copy(noise_hbm, noise, sems.at[members])]
     for m in range(members):
@@ -90,8 +90,11 @@
         for f in range(3):
             rowpack[3 * m + f] = jnp.where(top, fields[m, f, 0:8], fields[m, f, T - 8 : T])
             acc = jnp.where(ln == 4 * m + f, lroll(fields[m, f], 32 * m + 8 * f + 4), acc)
+    corn = jnp.where(top, acc[0:8], acc[T - 8 : T])
     colpack[...] = acc
-    cornpack[...] = jnp.where(top, acc[0:8], acc[T - 8 : T])
+    cornpack[...] = corn
+    allpack[0:8] = corn
+    allpack[8 : T + 8] = acc
 
 
 def own_columns(tiles):
@@ -139,8 +142,8 @@
     cell_x[...] = cell // T
 
 
-def merge_kernel(total_y, devices, inner, ownrow, owncol, rowrecv, colrecv, cornrecv, pick_y, cell_x,
-                 values, out, rs, rs1, cs, cs1, eta_s):
+def merge_kernel(total_y, devices, inner, ownrow, owncol, rowrecv, col_down, col_up, corn_down, corn_up,
+                 pick_y, cell_x, values, out, rs, rs1, cs, cs1, eta_s):
     members = inner.shape[0]
     tall = T + 16
     l32 = lax.rem(lanes((1, T)), 32)
@@ -149,6 +152,8 @@
     is_low = (l32 >= 20) & (l32 < 24)
     is_high = (l32 >= 8) & (l32 < 12)
 
+    colrecv = col_down[8 : T + 8] + col_up[...]
+    cornrecv = corn_down[0:8] + corn_up[...]
     for f in range(4):
         for m in range(members):
             halo = rowrecv[3 * m + f] if f < 3 else rowrecv[3 * members + m // 2]
@@ -160,10 +165,10 @@
             is_low, lroll(recv, 20 - 8 * f), jnp.where(is_high, lroll(recv, 4 - 8 * f), own)
         )
         tiles = [rowrecv[3 * m + f] if f < 3 else rowrecv[3 * members + m // 2] for m in range(members)]
-        ends = with_halo(own_columns(tiles), cornrecv[...])
+        ends = with_halo(own_columns(tiles), cornrecv)
         cs[f, 0:8] = ends
         cs[f, T + 8 : T + 16] = ends
-        cs[f, 8 : T + 8] = with_halo(owncol[f], colrecv[...])
+        cs[f, 8 : T + 8] = with_halo(owncol[f], colrecv)
 
     def twice(a, a1, total, cor):
         chunk = total // 2
@@ -256,7 +261,7 @@
     members = fields.shape[0]
     devices = lax.axis_size("mem")
     total_y = T * lax.axis_size("gy")
-    fields_vm, noise_vm, rowpack, colpack, cornpack = pl.pallas_call(
+    fields_vm, noise_vm, rowpack, colpack, cornpack, allpack = pl.pallas_call(
         pack_kernel,
         out_shape=(
             sds(*fields.shape),
@@ -264,17 +269,20 @@
             sds(3 * members + members // 2, 8, T),
             sds(T, T),
             sds(8, T),
+            sds(T + 8, T),
         ),
         in_specs=[HB] * 2,
-        out_specs=[VM] * 5,
+        out_specs=[VM] * 6,
         scratch_shapes=[pltpu.SemaphoreType.DMA((members + 1,))],
         compiler_params=PARAMS,
         name="pack",
     )(in_hbm(fields), in_hbm(noise))
-    swap = [(0, 1), (1, 0)]
-    colrecv = lax.ppermute(colpack, "gy", swap)
-    cornrecv = lax.ppermute(cornpack, ("gx", "gy"), [(0, 3), (1, 2), (2, 1), (3, 0)])
-    rowrecv = lax.ppermute(rowpack, "gx", swap)
+    grid = ("gx", "gy")
+    col_down = lax.ppermute(allpack, "gy", [(1, 0)])
+    corn_down = lax.ppermute(allpack, grid, [(1, 2), (3, 0)])
+    rowrecv = lax.ppermute(rowpack, "gx", [(0, 1), (1, 0)])
+    col_up = lax.ppermute(colpack, "gy", [(0, 1)])
+    corn_up = lax.ppermute(cornpack, grid, [(2, 1), (0, 3)])
     count = obs_cells.shape[-1]
     inner, ownrow, owncol, pick_y, cell_x, values = pl.pallas_call(
         functools.partial(interior_kernel, total_y),
@@ -302,7 +310,7 @@
     pieces = pl.pallas_call(
         functools.partial(merge_kernel, total_y, devices),
         out_shape=sds(devices * stride, T),
-        in_specs=[VM] * 9,
+        in_specs=[VM] * 11,
         out_specs=VM,
         scratch_shapes=[
             pltpu.VMEM((4, T, T), F32),
@@ -313,7 +321,7 @@
         ],
         compiler_params=PARAMS,
         name="merge",
-    )(inner, ownrow, owncol, rowrecv, colrecv, cornrecv, pick_y, cell_x, values)
+    )(inner, ownrow, owncol, rowrecv, col_down, col_up, corn_down, corn_up, pick_y, cell_x, values)
     held = lax.all_to_all(pieces.reshape(devices, stride, 1, T), "mem", 0, 0).reshape(devices * stride, T)
     picked, log_weights = pl.pallas_call(
         functools.partial(select_kernel, members, devices),

time: 55.2 us -> 61 us (1.11)
  starting transfers between devices: 4.26 us -> 10.1 us
  waiting for transfers between devices: 0.84 us -> 0.01 us
    ppermute x3 -> x5, starting transfers between devices: 4.26 us -> 10.1 us  [the longest x1 6.08 us: shards(): col_up = lax.ppermute(colpack, 'gy', [(0, 1)])]
    all_to_all x1, blocking collectives: 22.5 us -> 23.3 us  [shards(): lax.all_to_all(pieces.reshape(devices, stride, 1, T), 'mem', 0, 0)]
    ppermute x3 -> x5, waiting for transfers between devices: 0.84 us -> 0.01 us  [the longest x1 0.01 us: shards(): corn_up = lax.ppermute(cornpack, grid, [(2, 1), (0, 3)])]
  transfers between devices with their start and end apart: 3 -> 5, of which waited for: 1 -> 0; matrix products, arithmetic and copies ran while one was open for 0% -> 0% of each run, Pallas kernels for 6% -> 6%
where the time goes in v4:
time: 61 us; the launch traced here: 60.7 us
  blocking collectives  40.5 us (66%)
  starting transfers between devices  10.1 us (17%)
  Pallas kernels  8.37 us (14%)
  local copies, waits for them, and re-layouts  0.93 us (2%)
  between operations  0.74 us (1%)
    all_to_all x1, blocking collectives, shards(): lax.all_to_all(pieces.reshape(devices, stride, 1, T), 'mem', 0, 0)  23.3 us
    all_to_all x1, blocking collectives, shards(): lax.all_to_all(picked.reshape(devices, members // 2, rows, T), 'mem', 0, 0)  17.2 us
    ppermute x1, starting transfers between devices, shards(): col_up = lax.ppermute(colpack, 'gy', [(0, 1)])  6.08 us
    pallas_call x1, Pallas kernels, shards(): pl.pallas_call(functools.partial(interior_kernel, total_y), out_shape=(sd...  3.48 us
    pallas_call x1, Pallas kernels, shards(): pl.pallas_call(functools.partial(merge_kernel, total_y, devices), out_sha...  1.86 us
    pallas_call x1, Pallas kernels, shards(): pl.pallas_call(pack_kernel, out_shape=(sds(*fields.shape), sds(*noise.sha...  1.56 us
    pallas_call x1, Pallas kernels, shards(): pl.pallas_call(functools.partial(select_kernel, members, devices), out_sh...  1.47 us
    ppermute x1, starting transfers between devices, shards(): corn_up = lax.ppermute(cornpack, grid, [(2, 1), (0, 3)])  1.39 us
  transfers between devices with their start and end apart: 5, of which 0 were waited for; matrix products, arithmetic and copies ran while one was open for 0% of the time, Pallas kernels for 6%

profile of v4, /device:TPU:0, one launch (start us, length us, event | category | flops | bytes accessed | tf_op | source)
XLA Modules:
  0.0 60.7 jit_solution(18125289039347458610)
XLA Ops:
  0.6 1.6 %pack.1 = (f32[4,3,128,128]{3,2,1,0:T(8,128)S(1)}, f32[2,128,128]{2,1,0:T(8,128)S(1)}, f32[14,8,128]{2,1,0:T(8,128)S(1)}, f32[128,128]{1,0:T(8,128)S(1)}, f32[8,128]{1,0:T(8,128)S(1)}, /*index=5*/f32[136,128]{1,0:T(8,128)S(1)}) custom-call(f32[4,3,128,128]{3,2,1,0:T(8,128)} %fields_hbm.1, f32[2,128,128]{2,1,0:T(8,128)} %noise_hbm.1), custom_call_target="tpu_custom_call" | custom-call | tf_op jit(solution)/shard_map/pack/pallas_call | solution.py:264
  2.2 1.3 %collective-permute-start.1 = (f32[136,128]{1,0:T(8,128)S(1)}, f32[136,128]{1,0:T(8,128)S(1)}, u32[]{:S(2)}, u32[]{:S(2)}) collective-permute-start(f32[136,128]{1,0:T(8,128)S(1)} %get-tuple-element.22), channel_id=1, source_target_pairs={{1,0},{3,2},{5,4},{7,6},{9,8},{11,10},{13,12},{15,14},{17,16},{19,... | collective-permute-start | bytes 208904 | tf_op jit(solution)/shard_map/ppermute | solution.py:281
  3.5 1.3 %collective-permute-start.3 = (f32[136,128]{1,0:T(8,128)S(1)}, f32[136,128]{1,0:T(8,128)S(1)}, u32[]{:S(2)}, u32[]{:S(2)}) collective-permute-start(f32[136,128]{1,0:T(8,128)S(1)} %get-tuple-element.22), channel_id=1, source_target_pairs={{1,2},{3,0},{5,6},{7,4},{9,10},{11,8},{13,14},{15,12},{17,18},{19,... | collective-permute-start | bytes 208904 | tf_op jit(solution)/shard_map/ppermute | solution.py:282
  4.8 6.1 %collective-permute-start.2 = (f32[128,128]{1,0:T(8,128)S(1)}, f32[128,128]{1,0:T(8,128)S(1)}, u32[]{:S(2)}, u32[]{:S(2)}) collective-permute-start(f32[128,128]{1,0:T(8,128)S(1)} %get-tuple-element.23), channel_id=1, source_target_pairs={{0,1},{2,3},{4,5},{6,7},{8,9},{10,11},{12,13},{14,15},{16,17},{18,... | collective-permute-start | bytes 196616 | tf_op jit(solution)/shard_map/ppermute | solution.py:284
  10.9 0.1 collective-permute-start
  11.0 1.4 %collective-permute-start.4 = (f32[8,128]{1,0:T(8,128)S(1)}, f32[8,128]{1,0:T(8,128)S(1)}, u32[]{:S(2)}, u32[]{:S(2)}) collective-permute-start(f32[8,128]{1,0:T(8,128)S(1)} %get-tuple-element.24), channel_id=1, source_target_pairs={{2,1},{0,3},{6,5},{4,7},{10,9},{8,11},{14,13},{12,15},{18,17},{16,... | collective-permute-start | bytes 12296 | tf_op jit(solution)/shard_map/ppermute | solution.py:285
  12.4 3.5 %interior.1 = (f32[4,3,128,128]{3,2,1,0:T(8,128)S(1)}, f32[4,8,8,128]{3,2,1,0:T(8,128)S(1)}, f32[4,128,128]{2,1,0:T(8,128)S(1)}, bf16[128,256]{1,0:T(8,128)(2,1)...) custom-call(f32[4,3,128,128]{3,2,1,0:T(8,128)S(1)} %get-tuple-element.16.fields, ...), custom_call_target="tpu_custom_call" | custom-call | flops 50000000 | bytes 2500000 | tf_op jit(solution)/shard_map/interior/pallas_call | solution.py:287
  15.9 0.0 collective-permute-done.4.corn_up
  15.9 0.0 collective-permute-done.rowrecv
  15.9 0.0 collective-permute-done.2.col_up
  15.9 0.0 collective-permute-done.1.col_down
  15.9 0.0 collective-permute-done.3.corn_down
  15.9 1.9 %merge.1 = f32[1568,128]{1,0:T(8,128)S(1)} custom-call(f32[4,3,128,128]{3,2,1,0:T(8,128)S(1)} %get-tuple-element.18.inner, f32[4,8,8,128]{3,2,1,0:T(8,128)S(1)} %get-tuple-element.19.ownrow, f32[4,128,128]{2,1,0:T(8,128)S(1)} %get-tuple-element.20.owncol, f32[14,8,128]{2,1,0:T(8,128)S(1)} %collective-permute-done.rowrecv, ...), custom_call_target="tpu_custom_call" | custom-call | tf_op jit(solution)/shard_map/merge/pallas_call | solution.py:310
  17.8 23.3 %all_to_all.10 = f32[32,49,1,128]{3,2,1,0:T(1,128)S(1)} all-to-all(f32[32,49,1,128]{3,2,1,0:T(1,128)S(1)} %bitcast.8), channel_id=1, replica_groups=mesh['mem'=32,'gx'=2,'gy'=2] {'mem'}, dimensions={0} | all-to-all | bytes 1605632 | tf_op jit(solution)/shard_map/all_to_all | solution.py:325
  41.1 1.5 %select.1 = (f32[64,24,128]{2,1,0:T(8,128)S(1)}, f32[1,1,4]{2,1,0:T(1,128)}) custom-call(s32[1,64]{1,0:T(1,128)} %bitcast.15, f32[1568,128]{1,0:T(8,128)S(1)} %bitcast.9), custom_call_target="tpu_custom_call" | custom-call | tf_op jit(solution)/shard_map/select/pallas_call | solution.py:326
  42.6 17.2 %all_to_all.11 = f32[32,2,24,128]{3,2,1,0:T(8,128)S(1)} all-to-all(f32[32,2,24,128]{3,2,1,0:T(8,128)S(1)} %bitcast.10), channel_id=1, replica_groups=mesh['mem'=32,'gx'=2,'gy'=2] {'mem'}, dimensions={0} | all-to-all | bytes 1572864 | tf_op jit(solution)/shard_map/all_to_all | solution.py:335
  59.8 0.9 %copy.10 = f32[2,32,24,128]{3,2,1,0:T(8,128)} copy(f32[2,32,24,128]{3,2,0,1:T(8,128)S(1)} %bitcast.11) | data formatting | bytes 1572864 | tf_op jit(solution)/shard_map/transpose | solution.py:336
Async XLA Ops:
  2.2 13.7 %collective-permute-start.1 = (f32[136,128]{1,0:T(8,128)S(1)}, f32[136,128]{1,0:T(8,128)S(1)}, u32[]{:S(2)}, u32[]{:S(2)}) collective-permute-start(f32[136,128]{1,0:T(8,128)S(1)} %get-tuple-element.22), channel_id=1, source_target_pairs={{1,0},{3,2},{5,4},{7,6},{9,8},{11,10},{13,12},{15,14},{17,16},{19,... | collective-permute-start | bytes 208904 | tf_op jit(solution)/shard_map/ppermute | solution.py:281
  3.5 12.4 %collective-permute-start.3 = (f32[136,128]{1,0:T(8,128)S(1)}, f32[136,128]{1,0:T(8,128)S(1)}, u32[]{:S(2)}, u32[]{:S(2)}) collective-permute-start(f32[136,128]{1,0:T(8,128)S(1)} %get-tuple-element.22), channel_id=1, source_target_pairs={{1,2},{3,0},{5,6},{7,4},{9,10},{11,8},{13,14},{15,12},{17,18},{19,... | collective-permute-start | bytes 208904 | tf_op jit(solution)/shard_map/ppermute | solution.py:282
  4.8 11.1 %collective-permute-start.2 = (f32[128,128]{1,0:T(8,128)S(1)}, f32[128,128]{1,0:T(8,128)S(1)}, u32[]{:S(2)}, u32[]{:S(2)}) collective-permute-start(f32[128,128]{1,0:T(8,128)S(1)} %get-tuple-element.23), channel_id=1, source_target_pairs={{0,1},{2,3},{4,5},{6,7},{8,9},{10,11},{12,13},{14,15},{16,17},{18,... | collective-permute-start | bytes 196616 | tf_op jit(solution)/shard_map/ppermute | solution.py:284
  10.9 5.0 %collective-permute-start = (f32[14,8,128]{2,1,0:T(8,128)S(1)}, f32[14,8,128]{2,1,0:T(8,128)S(1)}, u32[]{:S(2)}, u32[]{:S(2)}) collective-permute-start(f32[14,8,128]{2,1,0:T(8,128)S(1)} %get-tuple-element.21), channel_id=1, source_target_pairs={{0,2},{2,0},{1,3},{3,1},{4,6},{6,4},{5,7},{7,5},{8,10},{10,8},{9,1... | collective-permute-start | bytes 172040 | tf_op jit(solution)/shard_map/ppermute | solution.py:283
  11.0 4.9 %collective-permute-start.4 = (f32[8,128]{1,0:T(8,128)S(1)}, f32[8,128]{1,0:T(8,128)S(1)}, u32[]{:S(2)}, u32[]{:S(2)}) collective-permute-start(f32[8,128]{1,0:T(8,128)S(1)} %get-tuple-element.24), channel_id=1, source_target_pairs={{2,1},{0,3},{6,5},{4,7},{10,9},{8,11},{14,13},{12,15},{18,17},{16,... | collective-permute-start | bytes 12296 | tf_op jit(solution)/shard_map/ppermute | solution.py:285

commit v5 on v3

--- a/solution.py
+++ b/solution.py
@@ -70,28 +70,33 @@
     return 0.1 + 0.2 * ((y.astype(F32) + 0.5) / total_y - 0.5)
 
 
-def pack_kernel(fields_hbm, noise_hbm, fields, noise, rowpack, colpack, cornpack, sems):
+def pack_kernel(fields_hbm, noise_hbm, fields, noise, slots, sems):
     members = fields.shape[0]
     copies = [pltpu.make_async_copy(noise_hbm, noise, sems.at[members])]
     for m in range(members):
         copies.append(pltpu.make_async_copy(fields_hbm.at[m], fields.at[m], sems.at[m]))
     for copy in copies:
         copy.start()
+    own = 2 * lax.axis_index("gx") + lax.axis_index("gy")
+    own_y, own_x, own_xy = own ^ 1, own ^ 2, own ^ 3
     copies[0].wait()
     top = subl((8, T)) < 4
     ln = lanes((T, T)) // 8
+    slots[own] = jnp.zeros((T, T), F32)
     for p in range(members // 2):
-        rowpack[3 * members + p] = jnp.where(top, noise[p, 0:8], noise[p, T - 8 : T])
+        k = 8 * (3 * members + p)
+        slots[own_x, k : k + 8] = jnp.where(top, noise[p, 0:8], noise[p, T - 8 : T])
     acc = jnp.zeros((T, T), F32)
     for m in range(members):
         acc = jnp.where(ln == 4 * m + 3, lroll(noise[m // 2], 32 * m + 28), acc)
     for m in range(members):
         copies[1 + m].wait()
         for f in range(3):
-            rowpack[3 * m + f] = jnp.where(top, fields[m, f, 0:8], fields[m, f, T - 8 : T])
+            k = 8 * (3 * m + f)
+            slots[own_x, k : k + 8] = jnp.where(top, fields[m, f, 0:8], fields[m, f, T - 8 : T])
             acc = jnp.where(ln == 4 * m + f, lroll(fields[m, f], 32 * m + 8 * f + 4), acc)
-    colpack[...] = acc
-    cornpack[...] = jnp.where(top, acc[0:8], acc[T - 8 : T])
+    slots[own_y] = acc
+    slots[own_xy, 0:8] = jnp.where(top, acc[0:8], acc[T - 8 : T])
 
 
 def own_columns(tiles):
@@ -139,8 +144,7 @@
     cell_x[...] = cell // T
 
 
-def merge_kernel(total_y, devices, inner, ownrow, owncol, rowrecv, colrecv, cornrecv, pick_y, cell_x,
-                 values, out, rs, rs1, cs, cs1, eta_s):
+def merge_kernel(total_y, devices, inner, ownrow, owncol, slots, pick_y, cell_x, values, out, rs, rs1, cs, cs1, eta_s):
     members = inner.shape[0]
     tall = T + 16
     l32 = lax.rem(lanes((1, T)), 32)
@@ -149,9 +153,12 @@
     is_low = (l32 >= 20) & (l32 < 24)
     is_high = (l32 >= 8) & (l32 < 12)
 
+    own = 2 * lax.axis_index("gx") + lax.axis_index("gy")
+    own_y, own_x, own_xy = own ^ 1, own ^ 2, own ^ 3
+    row_of = lambda m, f: pl.ds(8 * (3 * m + f if f < 3 else 3 * members + m // 2), 8)
     for f in range(4):
         for m in range(members):
-            halo = rowrecv[3 * m + f] if f < 3 else rowrecv[3 * members + m // 2]
+            halo = slots[own_x, row_of(m, f)]
             rs[f, 32 * m : 32 * m + 8] = halo
             rs[f, 32 * m + 8 : 32 * m + 16] = ownrow[f, 2 * m]
             rs[f, 32 * m + 16 : 32 * m + 24] = ownrow[f, 2 * m + 1]
@@ -159,11 +166,11 @@
         with_halo = lambda own, recv: jnp.where(
             is_low, lroll(recv, 20 - 8 * f), jnp.where(is_high, lroll(recv, 4 - 8 * f), own)
         )
-        tiles = [rowrecv[3 * m + f] if f < 3 else rowrecv[3 * members + m // 2] for m in range(members)]
-        ends = with_halo(own_columns(tiles), cornrecv[...])
+        tiles = [slots[own_x, row_of(m, f)] for m in range(members)]
+        ends = with_halo(own_columns(tiles), slots[own_xy, 0:8])
         cs[f, 0:8] = ends
         cs[f, T + 8 : T + 16] = ends
-        cs[f, 8 : T + 8] = with_halo(owncol[f], colrecv[...])
+        cs[f, 8 : T + 8] = with_halo(owncol[f], slots[own_y])
 
     def twice(a, a1, total, cor):
         chunk = total // 2
@@ -256,25 +263,16 @@
     members = fields.shape[0]
     devices = lax.axis_size("mem")
     total_y = T * lax.axis_size("gy")
-    fields_vm, noise_vm, rowpack, colpack, cornpack = pl.pallas_call(
+    fields_vm, noise_vm, slots = pl.pallas_call(
         pack_kernel,
-        out_shape=(
-            sds(*fields.shape),
-            sds(*noise.shape),
-            sds(3 * members + members // 2, 8, T),
-            sds(T, T),
-            sds(8, T),
-        ),
+        out_shape=(sds(*fields.shape), sds(*noise.shape), sds(4, T, T)),
         in_specs=[HB] * 2,
-        out_specs=[VM] * 5,
+        out_specs=[VM] * 3,
         scratch_shapes=[pltpu.SemaphoreType.DMA((members + 1,))],
         compiler_params=PARAMS,
         name="pack",
     )(in_hbm(fields), in_hbm(noise))
-    swap = [(0, 1), (1, 0)]
-    colrecv = lax.ppermute(colpack, "gy", swap)
-    cornrecv = lax.ppermute(cornpack, ("gx", "gy"), [(0, 3), (1, 2), (2, 1), (3, 0)])
-    rowrecv = lax.ppermute(rowpack, "gx", swap)
+    recv = lax.all_to_all(slots, ("gx", "gy"), 0, 0)
     count = obs_cells.shape[-1]
     inner, ownrow, owncol, pick_y, cell_x, values = pl.pallas_call(
         functools.partial(interior_kernel, total_y),
@@ -302,7 +300,7 @@
     pieces = pl.pallas_call(
         functools.partial(merge_kernel, total_y, devices),
         out_shape=sds(devices * stride, T),
-        in_specs=[VM] * 9,
+        in_specs=[VM] * 7,
         out_specs=VM,
         scratch_shapes=[
             pltpu.VMEM((4, T, T), F32),
@@ -313,7 +311,7 @@
         ],
         compiler_params=PARAMS,
         name="merge",
-    )(inner, ownrow, owncol, rowrecv, colrecv, cornrecv, pick_y, cell_x, values)
+    )(inner, ownrow, owncol, recv, pick_y, cell_x, values)
     held = lax.all_to_all(pieces.reshape(devices, stride, 1, T), "mem", 0, 0).reshape(devices * stride, T)
     picked, log_weights = pl.pallas_call(
         functools.partial(select_kernel, members, devices),

time: 55.2 us -> 58.4 us (1.058)
  waiting for transfers between devices: 0.84 us -> 4.06 us
  blocking collectives: 39.9 us -> 38.2 us
  starting transfers between devices: 4.26 us -> 5.24 us
  Pallas kernels: 8.38 us -> 9.07 us
    all_to_all x0 -> x1, starting transfers between devices: none -> 5.24 us  [shards(): recv = lax.all_to_all(slots, ('gx', 'gy'), 0, 0)]
    ppermute x3 -> x0, starting transfers between devices: 4.26 us -> none  [the longest x1 4.04 us: shards(): colrecv = lax.ppermute(colpack, 'gy', swap)]
    all_to_all x0 -> x1, waiting for transfers between devices: none -> 4.06 us  [shards(): recv = lax.all_to_all(slots, ('gx', 'gy'), 0, 0)]
    all_to_all x1, blocking collectives: 22.5 us -> 21.4 us  [shards(): lax.all_to_all(pieces.reshape(devices, stride, 1, T), 'mem', 0, 0)]
    ppermute x3 -> x0, waiting for transfers between devices: 0.84 us -> none  [the longest x1 0.83 us: shards(): lax.ppermute(cornpack, ('gx', 'gy'), [(0, 3), (1, 2), (2, 1), (3, 0)])]
    pallas_call x1, Pallas kernels: 1.56 us -> 2.26 us  [shards(): pl.pallas_call(pack_kernel, out_shape=(sds(*fields.shape), sds(*noise.sha...]
    all_to_all x1, blocking collectives: 17.4 us -> 16.8 us  [shards(): lax.all_to_all(picked.reshape(devices, members // 2, rows, T), 'mem', 0, 0)]
  transfers between devices with their start and end apart: 3 -> 1, of which waited for: 1 -> 1; matrix products, arithmetic and copies ran while one was open for 0% -> 0% of each run, Pallas kernels for 6% -> 6%
where the time goes in v5:
time: 58.4 us; the launch traced here: 58.1 us
  blocking collectives  38.2 us (65%)
  Pallas kernels  9.07 us (16%)
  starting transfers between devices  5.24 us (9%)
  waiting for transfers between devices  4.06 us (7%)
  local copies, waits for them, and re-layouts  0.93 us (2%)
  between operations  0.66 us (1%)
    all_to_all x1, blocking collectives, shards(): lax.all_to_all(pieces.reshape(devices, stride, 1, T), 'mem', 0, 0)  21.4 us
    all_to_all x1, blocking collectives, shards(): lax.all_to_all(picked.reshape(devices, members // 2, rows, T), 'mem', 0, 0)  16.8 us
    all_to_all x1, starting transfers between devices, shards(): recv = lax.all_to_all(slots, ('gx', 'gy'), 0, 0)  5.24 us
    all_to_all x1, waiting for transfers between devices, shards(): recv = lax.all_to_all(slots, ('gx', 'gy'), 0, 0)  4.06 us
    pallas_call x1, Pallas kernels, shards(): pl.pallas_call(functools.partial(interior_kernel, total_y), out_shape=(sd...  3.48 us
    pallas_call x1, Pallas kernels, shards(): pl.pallas_call(pack_kernel, out_shape=(sds(*fields.shape), sds(*noise.sha...  2.26 us
    pallas_call x1, Pallas kernels, shards(): pl.pallas_call(functools.partial(merge_kernel, total_y, devices), out_sha...  1.86 us
    pallas_call x1, Pallas kernels, shards(): pl.pallas_call(functools.partial(select_kernel, members, devices), out_sh...  1.47 us
  transfers between devices with their start and end apart: 1, of which 1 were waited for; matrix products, arithmetic and copies ran while one was open for 0% of the time, Pallas kernels for 6%

profile of v5, /device:TPU:0, one launch (start us, length us, event | category | flops | bytes accessed | tf_op | source)
XLA Modules:
  0.0 58.1 jit_solution(2866247184800137292)
XLA Ops:
  0.6 2.3 %pack.1 = (f32[4,3,128,128]{3,2,1,0:T(8,128)S(1)}, f32[2,128,128]{2,1,0:T(8,128)S(1)}, f32[4,128,128]{2,1,0:T(8,128)}) custom-call(f32[4,3,128,128]{3,2,1,0:T(8,128)} %fields_hbm.1, f32[2,128,128]{2,1,0:T(8,128)} %noise_hbm.1), custom_call_target="tpu_custom_call" | custom-call | tf_op jit(solution)/shard_map/pack/pallas_call | solution.py:266
  2.9 5.2 %all-to-all-start = ((f32[4,128,128]{2,1,0:T(8,128)}), f32[4,128,128]{2,1,0:T(8,128)S(1)}, u32[]{:S(2)}, u32[]{:S(2)}) async-start(f32[4,128,128]{2,1,0:T(8,128)} %get-tuple-element.18), calls=%async_computation | async-start | bytes 524288 | tf_op jit(solution)/shard_map/all_to_all | solution.py:275
  8.1 3.5 %interior.1 = (f32[4,3,128,128]{3,2,1,0:T(8,128)S(1)}, f32[4,8,8,128]{3,2,1,0:T(8,128)S(1)}, f32[4,128,128]{2,1,0:T(8,128)S(1)}, bf16[128,256]{1,0:T(8,128)(2,1)...) custom-call(f32[4,3,128,128]{3,2,1,0:T(8,128)S(1)} %get-tuple-element.13.fields, ...), custom_call_target="tpu_custom_call" | custom-call | flops 50000000 | bytes 2500000 | tf_op jit(solution)/shard_map/interior/pallas_call | solution.py:277
  11.6 4.1 %all-to-all-done.slots = f32[4,128,128]{2,1,0:T(8,128)S(1)} async-done(((f32[4,128,128]{2,1,0:T(8,128)}), f32[4,128,128]{2,1,0:T(8,128)S(1)}, u32[]{:S(2)}, u32[]{:S(2)}) %all-to-all-start) | async-done | bytes 262176 | tf_op jit(solution)/shard_map/all_to_all | solution.py:275
  15.7 1.9 %merge.1 = f32[1568,128]{1,0:T(8,128)S(1)} custom-call(f32[4,3,128,128]{3,2,1,0:T(8,128)S(1)} %get-tuple-element.15.inner, f32[4,8,8,128]{3,2,1,0:T(8,128)S(1)} %get-tuple-element.16.ownrow, f32[4,128,128]{2,1,0:T(8,128)S(1)} %get-tuple-element.17.owncol, f32[4,128,128]{2,1,0:T(8,128)S(1)} %all-to-all-done.slots, ...), custom_call_target="tpu_custom_call" | custom-call | tf_op jit(solution)/shard_map/merge/pallas_call | solution.py:300
  17.5 21.4 %all_to_all.15 = f32[32,49,1,128]{3,2,1,0:T(1,128)S(1)} all-to-all(f32[32,49,1,128]{3,2,1,0:T(1,128)S(1)} %bitcast.8), channel_id=1, replica_groups=mesh['mem'=32,'gx'=2,'gy'=2] {'mem'}, dimensions={0} | all-to-all | bytes 1605632 | tf_op jit(solution)/shard_map/all_to_all | solution.py:315
  39.0 1.5 %select.1 = (f32[64,24,128]{2,1,0:T(8,128)S(1)}, f32[1,1,4]{2,1,0:T(1,128)}) custom-call(s32[1,64]{1,0:T(1,128)} %bitcast.15, f32[1568,128]{1,0:T(8,128)S(1)} %bitcast.9), custom_call_target="tpu_custom_call" | custom-call | tf_op jit(solution)/shard_map/select/pallas_call | solution.py:316
  40.4 16.8 %all_to_all.16 = f32[32,2,24,128]{3,2,1,0:T(8,128)S(1)} all-to-all(f32[32,2,24,128]{3,2,1,0:T(8,128)S(1)} %bitcast.10), channel_id=1, replica_groups=mesh['mem'=32,'gx'=2,'gy'=2] {'mem'}, dimensions={0} | all-to-all | bytes 1572864 | tf_op jit(solution)/shard_map/all_to_all | solution.py:325
  57.2 0.9 %copy.10 = f32[2,32,24,128]{3,2,1,0:T(8,128)} copy(f32[2,32,24,128]{3,2,0,1:T(8,128)S(1)} %bitcast.11) | data formatting | bytes 1572864 | tf_op jit(solution)/shard_map/transpose | solution.py:326
Async XLA Ops:
  2.9 12.8 %all-to-all-start = ((f32[4,128,128]{2,1,0:T(8,128)}), f32[4,128,128]{2,1,0:T(8,128)S(1)}, u32[]{:S(2)}, u32[]{:S(2)}) async-start(f32[4,128,128]{2,1,0:T(8,128)} %get-tuple-element.18), calls=%async_computation | async-start | bytes 524288 | tf_op jit(solution)/shard_map/all_to_all | solution.py:275

commit v6 on v3

--- a/solution.py
+++ b/solution.py
@@ -70,7 +70,7 @@
     return 0.1 + 0.2 * ((y.astype(F32) + 0.5) / total_y - 0.5)
 
 
-def pack_kernel(fields_hbm, noise_hbm, fields, noise, rowpack, colpack, cornpack, sems):
+def pack_kernel(fields_hbm, noise_hbm, fields, noise, rowpack, colpack, sems):
     members = fields.shape[0]
     copies = [pltpu.make_async_copy(noise_hbm, noise, sems.at[members])]
     for m in range(members):
@@ -91,7 +91,6 @@
             rowpack[3 * m + f] = jnp.where(top, fields[m, f, 0:8], fields[m, f, T - 8 : T])
             acc = jnp.where(ln == 4 * m + f, lroll(fields[m, f], 32 * m + 8 * f + 4), acc)
     colpack[...] = acc
-    cornpack[...] = jnp.where(top, acc[0:8], acc[T - 8 : T])
 
 
 def own_columns(tiles):
@@ -139,16 +138,17 @@
     cell_x[...] = cell // T
 
 
-def merge_kernel(total_y, devices, inner, ownrow, owncol, rowrecv, colrecv, cornrecv, pick_y, cell_x,
-                 values, out, rs, rs1, cs, cs1, eta_s):
-    members = inner.shape[0]
-    tall = T + 16
-    l32 = lax.rem(lanes((1, T)), 32)
-    cor_row = coriolis(lanes((1, T)), total_y)
-    cor_col = coriolis(jnp.where(l32 < 16, l32 + 120, l32 - 24), total_y)
-    is_low = (l32 >= 20) & (l32 < 24)
-    is_high = (l32 >= 8) & (l32 < 12)
-
+def twice(a, a1, total, cor):
+    chunk = total // 2
+    for src, dst in ((a, a1), (a1, a)):
+        for r in range(0, total, chunk):
+            new = one_step(src, (), r, chunk, total, a[3, r : r + chunk], cor)
+            for f in range(3):
+                dst[f, r : r + chunk] = new[f]
+
+
+def rows_kernel(total_y, ownrow, rowrecv, edge, rs, rs1):
+    members = ownrow.shape[1] // 2
     for f in range(4):
         for m in range(members):
             halo = rowrecv[3 * m + f] if f < 3 else rowrecv[3 * members + m // 2]
@@ -156,24 +156,32 @@
             rs[f, 32 * m + 8 : 32 * m + 16] = ownrow[f, 2 * m]
             rs[f, 32 * m + 16 : 32 * m + 24] = ownrow[f, 2 * m + 1]
             rs[f, 32 * m + 24 : 32 * m + 32] = halo
+    twice(rs, rs1, T, coriolis(lanes((1, T)), total_y))
+    for f in range(3):
+        for m in range(members):
+            edge[f, 2 * m] = rs[f, 32 * m + 8 : 32 * m + 16]
+            edge[f, 2 * m + 1] = rs[f, 32 * m + 16 : 32 * m + 24]
+
+
+def merge_kernel(total_y, devices, inner, edge, owncol, rowrecv, colrecv, cornrecv, pick_y, cell_x,
+                 values, out, cs, cs1, eta_s):
+    members = inner.shape[0]
+    tall = T + 16
+    l32 = lax.rem(lanes((1, T)), 32)
+    cor_col = coriolis(jnp.where(l32 < 16, l32 + 120, l32 - 24), total_y)
+    is_low = (l32 >= 20) & (l32 < 24)
+    is_high = (l32 >= 8) & (l32 < 12)
+    corn = jnp.where(subl((8, T)) < 4, cornrecv[0:8], cornrecv[T - 8 : T])
+
+    for f in range(4):
         with_halo = lambda own, recv: jnp.where(
             is_low, lroll(recv, 20 - 8 * f), jnp.where(is_high, lroll(recv, 4 - 8 * f), own)
         )
         tiles = [rowrecv[3 * m + f] if f < 3 else rowrecv[3 * members + m // 2] for m in range(members)]
-        ends = with_halo(own_columns(tiles), cornrecv[...])
+        ends = with_halo(own_columns(tiles), corn)
         cs[f, 0:8] = ends
         cs[f, T + 8 : T + 16] = ends
         cs[f, 8 : T + 8] = with_halo(owncol[f], colrecv[...])
-
-    def twice(a, a1, total, cor):
-        chunk = total // 2
-        for src, dst in ((a, a1), (a1, a)):
-            for r in range(0, total, chunk):
-                new = one_step(src, (), r, chunk, total, a[3, r : r + chunk], cor)
-                for f in range(3):
-                    dst[f, r : r + chunk] = new[f]
-
-    twice(rs, rs1, T, cor_row)
     twice(cs, cs1, tall, cor_col)
 
     per = 96 // devices
@@ -187,9 +195,9 @@
             for t in range(T // 8):
                 a = inner[m, f, 8 * t : 8 * t + 8]
                 if t == 0:
-                    a = jnp.where(top, rs[f, 32 * m + 8 : 32 * m + 16], a)
+                    a = jnp.where(top, edge[f, 2 * m], a)
                 if t == T // 8 - 1:
-                    a = jnp.where(top, a, rs[f, 32 * m + 16 : 32 * m + 24])
+                    a = jnp.where(top, a, edge[f, 2 * m + 1])
                 col = cs[f, 8 * t + 8 : 8 * t + 16]
                 a = jnp.where(left, lroll(col, 104 - 32 * m), a)
                 a = jnp.where(right, lroll(col, 120 - 32 * m), a)
@@ -256,24 +264,22 @@
     members = fields.shape[0]
     devices = lax.axis_size("mem")
     total_y = T * lax.axis_size("gy")
-    fields_vm, noise_vm, rowpack, colpack, cornpack = pl.pallas_call(
+    fields_vm, noise_vm, rowpack, colpack = pl.pallas_call(
         pack_kernel,
         out_shape=(
             sds(*fields.shape),
             sds(*noise.shape),
             sds(3 * members + members // 2, 8, T),
             sds(T, T),
-            sds(8, T),
         ),
         in_specs=[HB] * 2,
-        out_specs=[VM] * 5,
+        out_specs=[VM] * 4,
         scratch_shapes=[pltpu.SemaphoreType.DMA((members + 1,))],
         compiler_params=PARAMS,
         name="pack",
     )(in_hbm(fields), in_hbm(noise))
     swap = [(0, 1), (1, 0)]
     colrecv = lax.ppermute(colpack, "gy", swap)
-    cornrecv = lax.ppermute(cornpack, ("gx", "gy"), [(0, 3), (1, 2), (2, 1), (3, 0)])
     rowrecv = lax.ppermute(rowpack, "gx", swap)
     count = obs_cells.shape[-1]
     inner, ownrow, owncol, pick_y, cell_x, values = pl.pallas_call(
@@ -297,6 +303,18 @@
         cost_estimate=pl.CostEstimate(flops=50_000_000, bytes_accessed=2_500_000, transcendentals=0),
         name="interior",
     )(fields_vm, noise_vm, in_hbm(obs_cells.reshape(1, -1)), in_hbm(obs_values.reshape(1, -1)))
+    colrecv, rowrecv, inner = lax.optimization_barrier((colrecv, rowrecv, inner))
+    cornrecv = lax.ppermute(colrecv, "gx", swap)
+    edge = pl.pallas_call(
+        functools.partial(rows_kernel, total_y),
+        out_shape=sds(3, 2 * members, 8, T),
+        in_specs=[VM] * 2,
+        out_specs=VM,
+        scratch_shapes=[pltpu.VMEM((4, T, T), F32), pltpu.VMEM((3, T, T), F32)],
+        compiler_params=PARAMS,
+        cost_estimate=pl.CostEstimate(flops=12_000_000, bytes_accessed=250_000, transcendentals=0),
+        name="rows",
+    )(ownrow, rowrecv)
     rows = 768 // devices
     stride = members // 2 * rows + 1
     pieces = pl.pallas_call(
@@ -305,15 +323,13 @@
         in_specs=[VM] * 9,
         out_specs=VM,
         scratch_shapes=[
-            pltpu.VMEM((4, T, T), F32),
-            pltpu.VMEM((3, T, T), F32),
             pltpu.VMEM((4, T + 16, T), F32),
             pltpu.VMEM((3, T + 16, T), F32),
             pltpu.VMEM((members * T, T), F32),
         ],
         compiler_params=PARAMS,
         name="merge",
-    )(inner, ownrow, owncol, rowrecv, colrecv, cornrecv, pick_y, cell_x, values)
+    )(inner, edge, owncol, rowrecv, colrecv, cornrecv, pick_y, cell_x, values)
     held = lax.all_to_all(pieces.reshape(devices, stride, 1, T), "mem", 0, 0).reshape(devices * stride, T)
     picked, log_weights = pl.pallas_call(
         functools.partial(select_kernel, members, devices),

time: 55.2 us -> 54.8 us (level)
  waiting for transfers between devices: 0.84 us -> 0.26 us
    pallas_call x0 -> x1, Pallas kernels: none -> 0.64 us  [shards(): pl.pallas_call(functools.partial(rows_kernel, total_y), out_shape=sds(3,...]
    ppermute x1, waiting for transfers between devices: 0.83 us -> 0.26 us  [shards(): cornrecv = lax.ppermute(colrecv, 'gx', swap)]
    pallas_call x1, Pallas kernels: 1.87 us -> 1.31 us  [shards(): pl.pallas_call(functools.partial(merge_kernel, total_y, devices), out_sha...]
  transfers between devices with their start and end apart: 3 -> 3, of which waited for: 1 -> 1; matrix products, arithmetic and copies ran while one was open for 0% -> 0% of each run, Pallas kernels for 6% -> 8%
where the time goes in v6:
time: 54.8 us; the launch traced here: 54.5 us
  blocking collectives  39.6 us (72%)
  Pallas kernels  8.46 us (15%)
  starting transfers between devices  4.63 us (8%)
  local copies, waits for them, and re-layouts  0.93 us (2%)
  between operations  0.68 us (1%)
    all_to_all x1, blocking collectives, shards(): lax.all_to_all(pieces.reshape(devices, stride, 1, T), 'mem', 0, 0)  22.3 us
    all_to_all x1, blocking collectives, shards(): lax.all_to_all(picked.reshape(devices, members // 2, rows, T), 'mem', 0, 0)  17.2 us
    ppermute x1, starting transfers between devices, shards(): colrecv = lax.ppermute(colpack, 'gy', swap)  4.04 us
    pallas_call x1, Pallas kernels, shards(): pl.pallas_call(functools.partial(interior_kernel, total_y), out_shape=(sd...  3.48 us
    pallas_call x1, Pallas kernels, shards(): pl.pallas_call(pack_kernel, out_shape=(sds(*fields.shape), sds(*noise.sha...  1.56 us
    pallas_call x1, Pallas kernels, shards(): pl.pallas_call(functools.partial(select_kernel, members, devices), out_sh...  1.47 us
    pallas_call x1, Pallas kernels, shards(): pl.pallas_call(functools.partial(merge_kernel, total_y, devices), out_sha...  1.31 us
  transfers between devices with their start and end apart: 3, of which 1 were waited for; matrix products, arithmetic and copies ran while one was open for 0% of the time, Pallas kernels for 8%

profile of v6, /device:TPU:0, one launch (start us, length us, event | category | flops | bytes accessed | tf_op | source)
XLA Modules:
  0.0 54.5 jit_solution(6169052308354726524)
XLA Ops:
  0.6 1.6 %pack.1 = (f32[4,3,128,128]{3,2,1,0:T(8,128)S(1)}, f32[2,128,128]{2,1,0:T(8,128)S(1)}, f32[14,8,128]{2,1,0:T(8,128)S(1)}, f32[128,128]{1,0:T(8,128)S(1)}) custom-call(f32[4,3,128,128]{3,2,1,0:T(8,128)} %fields_hbm.1, f32[2,128,128]{2,1,0:T(8,128)} %noise_hbm.1), custom_call_target="tpu_custom_call" | custom-call | tf_op jit(solution)/shard_map/pack/pallas_call | solution.py:267
  2.2 4.0 %collective-permute-start = (f32[128,128]{1,0:T(8,128)S(1)}, f32[128,128]{1,0:T(8,128)S(1)}, u32[]{:S(2)}, u32[]{:S(2)}) collective-permute-start(f32[128,128]{1,0:T(8,128)S(1)} %get-tuple-element.17), channel_id=1, source_target_pairs={{0,1},{1,0},{2,3},{3,2},{4,5},{5,4},{6,7},{7,6},{8,9},{9,8},{10,11... | collective-permute-start | bytes 196616 | tf_op jit(solution)/shard_map/ppermute | solution.py:282
  6.2 0.0 collective-permute-start.1
  6.2 3.5 %interior.1 = (f32[4,3,128,128]{3,2,1,0:T(8,128)S(1)}, f32[4,8,8,128]{3,2,1,0:T(8,128)S(1)}, f32[4,128,128]{2,1,0:T(8,128)S(1)}, bf16[128,256]{1,0:T(8,128)(2,1)...) custom-call(f32[4,3,128,128]{3,2,1,0:T(8,128)S(1)} %get-tuple-element.19.fields, ...), custom_call_target="tpu_custom_call" | custom-call | flops 50000000 | bytes 2500000 | tf_op jit(solution)/shard_map/interior/pallas_call | solution.py:285
  9.7 0.0 collective-permute-done.1.rowrecv
  9.7 0.0 collective-permute-done.colrecv
  9.7 0.6 %collective-permute-start.2 = (f32[128,128]{1,0:T(8,128)S(1)}, f32[128,128]{1,0:T(8,128)S(1)}, u32[]{:S(2)}, u32[]{:S(2)}) collective-permute-start(f32[128,128]{1,0:T(8,128)S(1)} %collective-permute-done.colrecv), channel_id=1, source_target_pairs={{0,2},{2,0},{1,3},{3,1},{4,6},{6,4},{5,7},{7,5},{8,10},{10,8},{9,1... | collective-permute-start | bytes 196616 | tf_op jit(solution)/shard_map/ppermute | solution.py:307
  10.3 0.6 %rows.1.edge = f32[3,8,8,128]{3,2,1,0:T(8,128)S(1)} custom-call(f32[4,8,8,128]{3,2,1,0:T(8,128)S(1)} %get-tuple-element.23.ownrow, f32[14,8,128]{2,1,0:T(8,128)S(1)} %collective-permute-done.1.rowrecv), custom_call_target="tpu_custom_call" | custom-call | flops 12000000 | bytes 250000 | tf_op jit(solution)/shard_map/rows/pallas_call | solution.py:308
  11.0 0.3 collective-permute-done.2.cornrecv
  11.2 1.3 %merge.1 = f32[1568,128]{1,0:T(8,128)S(1)} custom-call(f32[4,3,128,128]{3,2,1,0:T(8,128)S(1)} %get-tuple-element.22.inner, f32[3,8,8,128]{3,2,1,0:T(8,128)S(1)} %rows.1.edge, f32[4,128,128]{2,1,0:T(8,128)S(1)} %get-tuple-element.25.owncol, f32[14,8,128]{2,1,0:T(8,128)S(1)} %collective-permute-done.1.rowrecv, f32[128,128]{1,0:T(8,128)S(1)} %collective-permute-done.colrecv, ...), custom_call_target="tpu_custom_call" | custom-call | tf_op jit(solution)/shard_map/merge/pallas_call | solution.py:320
  12.6 22.3 %all_to_all.10 = f32[32,49,1,128]{3,2,1,0:T(1,128)S(1)} all-to-all(f32[32,49,1,128]{3,2,1,0:T(1,128)S(1)} %bitcast.8), channel_id=1, replica_groups=mesh['mem'=32,'gx'=2,'gy'=2] {'mem'}, dimensions={0} | all-to-all | bytes 1605632 | tf_op jit(solution)/shard_map/all_to_all | solution.py:333
  34.9 1.5 %select.1 = (f32[64,24,128]{2,1,0:T(8,128)S(1)}, f32[1,1,4]{2,1,0:T(1,128)}) custom-call(s32[1,64]{1,0:T(1,128)} %bitcast.15, f32[1568,128]{1,0:T(8,128)S(1)} %bitcast.9), custom_call_target="tpu_custom_call" | custom-call | tf_op jit(solution)/shard_map/select/pallas_call | solution.py:334
  36.4 17.2 %all_to_all.11 = f32[32,2,24,128]{3,2,1,0:T(8,128)S(1)} all-to-all(f32[32,2,24,128]{3,2,1,0:T(8,128)S(1)} %bitcast.10), channel_id=1, replica_groups=mesh['mem'=32,'gx'=2,'gy'=2] {'mem'}, dimensions={0} | all-to-all | bytes 1572864 | tf_op jit(solution)/shard_map/all_to_all | solution.py:343
  53.6 0.9 %copy.10 = f32[2,32,24,128]{3,2,1,0:T(8,128)} copy(f32[2,32,24,128]{3,2,0,1:T(8,128)S(1)} %bitcast.11) | data formatting | bytes 1572864 | tf_op jit(solution)/shard_map/transpose | solution.py:344
Async XLA Ops:
  2.2 7.5 %collective-permute-start = (f32[128,128]{1,0:T(8,128)S(1)}, f32[128,128]{1,0:T(8,128)S(1)}, u32[]{:S(2)}, u32[]{:S(2)}) collective-permute-start(f32[128,128]{1,0:T(8,128)S(1)} %get-tuple-element.17), channel_id=1, source_target_pairs={{0,1},{1,0},{2,3},{3,2},{4,5},{5,4},{6,7},{7,6},{8,9},{9,8},{10,11... | collective-permute-start | bytes 196616 | tf_op jit(solution)/shard_map/ppermute | solution.py:282
  6.2 3.5 %collective-permute-start.1 = (f32[14,8,128]{2,1,0:T(8,128)S(1)}, f32[14,8,128]{2,1,0:T(8,128)S(1)}, u32[]{:S(2)}, u32[]{:S(2)}) collective-permute-start(f32[14,8,128]{2,1,0:T(8,128)S(1)} %get-tuple-element.18), channel_id=1, source_target_pairs={{0,2},{2,0},{1,3},{3,1},{4,6},{6,4},{5,7},{7,5},{8,10},{10,8},{9,1... | collective-permute-start | bytes 172040 | tf_op jit(solution)/shard_map/ppermute | solution.py:283
  9.7 1.5 %collective-permute-start.2 = (f32[128,128]{1,0:T(8,128)S(1)}, f32[128,128]{1,0:T(8,128)S(1)}, u32[]{:S(2)}, u32[]{:S(2)}) collective-permute-start(f32[128,128]{1,0:T(8,128)S(1)} %collective-permute-done.colrecv), channel_id=1, source_target_pairs={{0,2},{2,0},{1,3},{3,1},{4,6},{6,4},{5,7},{7,5},{8,10},{10,8},{9,1... | collective-permute-start | bytes 196616 | tf_op jit(solution)/shard_map/ppermute | solution.py:307

commit v7 on v6

--- a/solution.py
+++ b/solution.py
@@ -70,7 +70,7 @@
     return 0.1 + 0.2 * ((y.astype(F32) + 0.5) / total_y - 0.5)
 
 
-def pack_kernel(fields_hbm, noise_hbm, fields, noise, rowpack, colpack, sems):
+def pack_kernel(total_y, fields_hbm, noise_hbm, fields, noise, rowpack, colpack, inner, tmp, sems):
     members = fields.shape[0]
     copies = [pltpu.make_async_copy(noise_hbm, noise, sems.at[members])]
     for m in range(members):
@@ -92,6 +92,10 @@
             acc = jnp.where(ln == 4 * m + f, lroll(fields[m, f], 32 * m + 8 * f + 4), acc)
     colpack[...] = acc
 
+    @pl.when(lax.axis_index("gy") == 0)
+    def _():
+        interior(total_y, fields, noise, inner, tmp)
+
 
 def own_columns(tiles):
     shape = tiles[0].shape
@@ -103,22 +107,31 @@
     return acc
 
 
-def interior_kernel(total_y, fields, noise, cells_hbm, values_hbm, inner, ownrow, owncol, pick_y, cell_x,
-                    values, tmp, cells, sems):
+def interior(total_y, fields, noise, inner, tmp):
+    cor = coriolis(lanes((1, T)), total_y)
+    for src, dst in ((fields, tmp), (tmp, inner)):
+        for m in range(fields.shape[0]):
+            for r in range(0, T, CHUNK):
+                new = one_step(src, (m,), r, CHUNK, T, noise[m // 2, r : r + CHUNK], cor)
+                for f in range(3):
+                    dst[m, f, r : r + CHUNK] = new[f]
+
+
+def interior_kernel(total_y, fields, noise, inner_in, cells_hbm, values_hbm, lineage_hbm, inner, ownrow, owncol,
+                    pick_y, cell_x, values, lineage, tmp, cells, sems):
     members = fields.shape[0]
     copies = [
         pltpu.make_async_copy(cells_hbm, cells, sems.at[0]),
         pltpu.make_async_copy(values_hbm, values, sems.at[1]),
+        pltpu.make_async_copy(lineage_hbm, lineage, sems.at[2]),
     ]
     for copy in copies:
         copy.start()
-    cor = coriolis(lanes((1, T)), total_y)
-    for src, dst in ((fields, tmp), (tmp, inner)):
-        for m in range(members):
-            for r in range(0, T, CHUNK):
-                new = one_step(src, (m,), r, CHUNK, T, noise[m // 2, r : r + CHUNK], cor)
-                for f in range(3):
-                    dst[m, f, r : r + CHUNK] = new[f]
+
+    @pl.when(lax.axis_index("gy") != 0)
+    def _():
+        interior(total_y, fields, noise, inner, tmp)
+
     for m in range(members):
         for f in range(4):
             src = fields.at[m, f] if f < 3 else noise.at[m // 2]
@@ -225,26 +238,34 @@
         out[(j + 1) * stride - 1 : (j + 1) * stride] = logw
 
 
-def select_kernel(members, devices, lineage_hbm, recv, out, log_weights, lineage, sem):
-    copy = pltpu.make_async_copy(lineage_hbm, lineage, sem)
+def select_kernel(members, lineage_vmem, recv, out, lineage, sem):
+    copy = pltpu.make_async_copy(lineage_vmem, lineage, sem)
     copy.start()
-    pairs, rows = members // 2 * devices, out.shape[1]
-    stride = members // 2 * rows + 1
+    pairs, rows = out.shape[0], out.shape[1]
+    per = members // 2
+    copy.wait()
+    for k in range(pairs):
+        pair = lineage[0, k]
+        out[k] = recv[pl.ds(lax.div(pair, per) * (per * rows + 1) + lax.rem(pair, per) * rows, rows)]
+
+
+def finish_kernel(members, back, recv, out, log_weights, result, sems):
+    devices = back.shape[0]
+    copies = [pltpu.make_async_copy(back.at[:, p], out.at[p], sems.at[p]) for p in range(members // 2)]
+    for copy in copies:
+        copy.start()
+    stride = recv.shape[0] // devices
     logw = recv[pl.ds(stride - 1, devices, stride)]
     logw = jnp.where(lanes(logw.shape) < members, logw, -jnp.inf)
     peak = jnp.max(jnp.max(logw, axis=1, keepdims=True), axis=0, keepdims=True)
     total = jnp.sum(jnp.sum(jnp.exp(logw - peak), axis=1, keepdims=True), axis=0, keepdims=True)
     own = recv[pl.ds(lax.axis_index("mem") * stride + stride - 1, 1)]
-    log_weights[0] = (own - peak - jnp.log(total))[:, :members]
-    copy.wait()
-
-    def body(k, carry):
-        pair = lineage[0, k]
-        first = lax.div(pair, members // 2) * stride + lax.rem(pair, members // 2) * rows
-        out[k] = recv[pl.ds(first, rows)]
-        return carry
-
-    lax.fori_loop(0, pairs, body, 0, unroll=8)
+    result[0] = (own - peak - jnp.log(total))[:, :members]
+    last = pltpu.make_async_copy(result, log_weights, sems.at[members // 2])
+    last.start()
+    for copy in copies:
+        copy.wait()
+    last.wait()
 
 
 VM = pl.BlockSpec(memory_space=pltpu.VMEM)
@@ -264,25 +285,26 @@
     members = fields.shape[0]
     devices = lax.axis_size("mem")
     total_y = T * lax.axis_size("gy")
-    fields_vm, noise_vm, rowpack, colpack = pl.pallas_call(
-        pack_kernel,
+    fields_vm, noise_vm, rowpack, colpack, inner = pl.pallas_call(
+        functools.partial(pack_kernel, total_y),
         out_shape=(
             sds(*fields.shape),
             sds(*noise.shape),
             sds(3 * members + members // 2, 8, T),
             sds(T, T),
+            sds(members, 3, T, T),
         ),
         in_specs=[HB] * 2,
-        out_specs=[VM] * 4,
-        scratch_shapes=[pltpu.SemaphoreType.DMA((members + 1,))],
+        out_specs=[VM] * 5,
+        scratch_shapes=[pltpu.VMEM((members, 3, T, T), F32), pltpu.SemaphoreType.DMA((members + 1,))],
         compiler_params=PARAMS,
         name="pack",
     )(in_hbm(fields), in_hbm(noise))
     swap = [(0, 1), (1, 0)]
     colrecv = lax.ppermute(colpack, "gy", swap)
     rowrecv = lax.ppermute(rowpack, "gx", swap)
-    count = obs_cells.shape[-1]
-    inner, ownrow, owncol, pick_y, cell_x, values = pl.pallas_call(
+    count, pairs = obs_cells.shape[-1], ancestors.shape[-1]
+    inner, ownrow, owncol, pick_y, cell_x, values, lineage = pl.pallas_call(
         functools.partial(interior_kernel, total_y),
         out_shape=(
             sds(members, 3, T, T),
@@ -291,18 +313,27 @@
             jax.ShapeDtypeStruct((T, count), jnp.bfloat16),
             jax.ShapeDtypeStruct((1, count), jnp.int32),
             sds(1, count),
+            jax.ShapeDtypeStruct((1, pairs), jnp.int32),
         ),
-        in_specs=[VM] * 2 + [HB] * 2,
-        out_specs=[VM] * 6,
+        in_specs=[VM] * 3 + [HB] * 3,
+        out_specs=[VM] * 7,
+        input_output_aliases={2: 0},
         scratch_shapes=[
             pltpu.VMEM((members, 3, T, T), F32),
             pltpu.VMEM((1, count), jnp.int32),
-            pltpu.SemaphoreType.DMA((2,)),
+            pltpu.SemaphoreType.DMA((3,)),
         ],
         compiler_params=PARAMS,
         cost_estimate=pl.CostEstimate(flops=50_000_000, bytes_accessed=2_500_000, transcendentals=0),
         name="interior",
-    )(fields_vm, noise_vm, in_hbm(obs_cells.reshape(1, -1)), in_hbm(obs_values.reshape(1, -1)))
+    )(
+        fields_vm,
+        noise_vm,
+        inner,
+        in_hbm(obs_cells.reshape(1, -1)),
+        in_hbm(obs_values.reshape(1, -1)),
+        in_hbm(ancestors.reshape(1, -1)),
+    )
     colrecv, rowrecv, inner = lax.optimization_barrier((colrecv, rowrecv, inner))
     cornrecv = lax.ppermute(colrecv, "gx", swap)
     edge = pl.pallas_call(
@@ -331,18 +362,26 @@
         name="merge",
     )(inner, edge, owncol, rowrecv, colrecv, cornrecv, pick_y, cell_x, values)
     held = lax.all_to_all(pieces.reshape(devices, stride, 1, T), "mem", 0, 0).reshape(devices * stride, T)
-    picked, log_weights = pl.pallas_call(
-        functools.partial(select_kernel, members, devices),
-        out_shape=(sds(devices * members // 2, rows, T), sds(1, 1, members)),
-        in_specs=[HB, VM],
-        out_specs=[VM] * 2,
-        scratch_shapes=[pltpu.SMEM((1, devices * members // 2), jnp.int32), pltpu.SemaphoreType.DMA],
+    picked = pl.pallas_call(
+        functools.partial(select_kernel, members),
+        out_shape=sds(pairs, rows, T),
+        in_specs=[VM, VM],
+        out_specs=VM,
+        scratch_shapes=[pltpu.SMEM((1, pairs), jnp.int32), pltpu.SemaphoreType.DMA],
         compiler_params=PARAMS,
         name="select",
-    )(in_hbm(ancestors.reshape(1, -1)), held)
+    )(lineage, held)
     back = lax.all_to_all(picked.reshape(devices, members // 2, rows, T), "mem", 0, 0)
-    resampled = back.transpose(1, 0, 2, 3).reshape(fields.shape)
-    return (resampled, log_weights)
+    resampled, log_weights = pl.pallas_call(
+        functools.partial(finish_kernel, members),
+        out_shape=(sds(members // 2, devices, rows, T), sds(1, 1, members)),
+        in_specs=[VM, VM],
+        out_specs=[HB, HB],
+        scratch_shapes=[pltpu.VMEM((1, 1, members), F32), pltpu.SemaphoreType.DMA((members // 2 + 1,))],
+        compiler_params=PARAMS,
+        name="finish",
+    )(back, held)
+    return (resampled.reshape(fields.shape), log_weights)
 
 
 def solution(mesh):

time: 54.8 us -> 54.9 us (level)
  waiting for transfers between devices: 0.26 us -> 3.93 us
  starting transfers between devices: 4.63 us -> 1.77 us
  local copies, waits for them, and re-layouts: 0.93 us -> 0 us
    ppermute x1, waiting for transfers between devices: 0.01 us -> 2.84 us  [shards(): colrecv = lax.ppermute(colpack, 'gy', swap)]
    pallas_call x1, Pallas kernels: 3.48 us -> 0.74 us  [shards(): pl.pallas_call(functools.partial(interior_kernel, total_y), out_shape=(sd...]
    pallas_call x2 -> x3, Pallas kernels: 3.03 us -> 5.52 us  [the longest x1 3.83 us: shards(): pl.pallas_call(functools.partial(pack_kernel, total_y), out_shape=(sds(*f...]
    ppermute x1, starting transfers between devices: 4.04 us -> 1.77 us  [shards(): colrecv = lax.ppermute(colpack, 'gy', swap)]
    transpose x1 -> x0, local copies, waits for them, and re-layouts: 0.93 us -> none  [shards(): resampled = back.transpose(1, 0, 2, 3).reshape(fields.shape)]
    all_to_all x1, blocking collectives: 22.3 us -> 23.1 us  [shards(): lax.all_to_all(pieces.reshape(devices, stride, 1, T), 'mem', 0, 0)]
    ppermute x1, starting transfers between devices: 0.59 us -> 0.01 us  [shards(): cornrecv = lax.ppermute(colrecv, 'gx', swap)]
  transfers between devices with their start and end apart: 3 -> 3, of which waited for: 1 -> 3; matrix products, arithmetic and copies ran while one was open for 0% -> 0% of each run, Pallas kernels for 8% -> 3%
where the time goes in v7:
time: 54.9 us; the launch traced here: 54.7 us
  blocking collectives  40.1 us (73%)
  Pallas kernels  8.22 us (15%)
  waiting for transfers between devices  3.93 us (7%)
  starting transfers between devices  1.77 us (3%)
  between operations  0.67 us (1%)
    all_to_all x1, blocking collectives, shards(): lax.all_to_all(pieces.reshape(devices, stride, 1, T), 'mem', 0, 0)  23.1 us
    all_to_all x1, blocking collectives, shards(): lax.all_to_all(picked.reshape(devices, members // 2, rows, T), 'mem', 0, 0)  17 us
    pallas_call x1, Pallas kernels, shards(): pl.pallas_call(functools.partial(pack_kernel, total_y), out_shape=(sds(*f...  3.83 us
    ppermute x1, waiting for transfers between devices, shards(): colrecv = lax.ppermute(colpack, 'gy', swap)  2.84 us
    ppermute x1, starting transfers between devices, shards(): colrecv = lax.ppermute(colpack, 'gy', swap)  1.77 us
    pallas_call x1, Pallas kernels, shards(): pl.pallas_call(functools.partial(merge_kernel, total_y, devices), out_sha...  1.32 us
  transfers between devices with their start and end apart: 3, of which 3 were waited for; matrix products, arithmetic and copies ran while one was open for 0% of the time, Pallas kernels for 3%

profile of v7, /device:TPU:0, one launch (start us, length us, event | category | flops | bytes accessed | tf_op | source)
XLA Modules:
  0.0 54.7 jit_solution(3842598113847775216)
XLA Ops:
  0.6 3.8 %pack.1 = (f32[4,3,128,128]{3,2,1,0:T(8,128)S(1)}, f32[2,128,128]{2,1,0:T(8,128)S(1)}, f32[14,8,128]{2,1,0:T(8,128)S(1)}, f32[128,128]{1,0:T(8,128)S(1)}, f32[4,3,128,128]{3,2,1,0:T(8,128)S(1)}) custom-call(f32[4,3,128,128]{3,2,1,0:T(8,128)} %fields_hbm.1, f32[2,128,128]{2,1,0:T(8,128)} %noise_hbm.1), custom_call_target="tpu_custom_call" | custom-call | tf_op jit(solution)/shard_map/pack/pallas_call | solution.py:288
  4.5 1.8 %collective-permute-start = (f32[128,128]{1,0:T(8,128)S(1)}, f32[128,128]{1,0:T(8,128)S(1)}, u32[]{:S(2)}, u32[]{:S(2)}) collective-permute-start(f32[128,128]{1,0:T(8,128)S(1)} %get-tuple-element.23), channel_id=1, source_target_pairs={{0,1},{1,0},{2,3},{3,2},{4,5},{5,4},{6,7},{7,6},{8,9},{9,8},{10,11... | collective-permute-start | bytes 196616 | tf_op jit(solution)/shard_map/ppermute | solution.py:304
  6.2 0.0 collective-permute-start.1
  6.2 0.7 %interior.1 = (f32[4,3,128,128]{3,2,1,0:T(8,128)S(1)}, f32[4,8,8,128]{3,2,1,0:T(8,128)S(1)}, f32[4,128,128]{2,1,0:T(8,128)S(1)}, bf16[128,256]{1,0:T(8,128)(2,1)...) custom-call(f32[4,3,128,128]{3,2,1,0:T(8,128)S(1)} %get-tuple-elemen, ...), custom_call_target="tpu_custom_call", output_to_operand_aliasing={{0}: (2, {})} | custom-call | flops 50000000 | bytes 2500000 | tf_op jit(solution)/shard_map/interior/pallas_call | solution.py:307
  7.0 0.5 collective-permute-done.1.rowrecv
  7.5 2.8 %collective-permute-done.colrecv = f32[128,128]{1,0:T(8,128)S(1)} collective-permute-done((f32[128,128]{1,0:T(8,128)S(1)}, f32[128,128]{1,0:T(8,128)S(1)}, u32[]{:S(2)}, u32[]{:S(2)}) %collective-permute-start) | collective-permute-done | bytes 65568 | tf_op jit(solution)/shard_map/ppermute | solution.py:304
  10.3 0.0 collective-permute-start.2
  10.3 0.6 %rows.1.edge = f32[3,8,8,128]{3,2,1,0:T(8,128)S(1)} custom-call(f32[4,8,8,128]{3,2,1,0:T(8,128)S(1)} %get-tuple-element.27.ownrow, f32[14,8,128]{2,1,0:T(8,128)S(1)} %collective-permute-done.1.rowrecv), custom_call_target="tpu_custom_call" | custom-call | flops 12000000 | bytes 250000 | tf_op jit(solution)/shard_map/rows/pallas_call | solution.py:339
  11.0 0.6 %collective-permute-done.2.cornrecv = f32[128,128]{1,0:T(8,128)S(1)} collective-permute-done((f32[128,128]{1,0:T(8,128)S(1)}, f32[128,128]{1,0:T(8,128)S(1)}, u32[]{:S(2)}, u32[]{:S(2)}) %collective-permute-start.2) | collective-permute-done | bytes 65568 | tf_op jit(solution)/shard_map/ppermute | solution.py:338
  11.6 1.3 %merge.1 = f32[1568,128]{1,0:T(8,128)S(1)} custom-call(f32[4,3,128,128]{3,2,1,0:T(8,128)S(1)} %get-tuple-element.26.inner, f32[3,8,8,128]{3,2,1,0:T(8,128)S(1)} %rows.1.edge, f32[4,128,128]{2,1,0:T(8,128)S(1)} %get-tuple-element.29.owncol, f32[14,8,128]{2,1,0:T(8,128)S(1)} %collective-permute-done.1.rowrecv, f32[128,128]{1,0:T(8,128)S(1)} %collective-permute-done.colrecv, ...), custom_call_target="tpu_custom_call" | custom-call | tf_op jit(solution)/shard_map/merge/pallas_call | solution.py:351
  12.9 23.1 %all_to_all.10 = f32[32,49,1,128]{3,2,1,0:T(1,128)S(1)} all-to-all(f32[32,49,1,128]{3,2,1,0:T(1,128)S(1)} %bitcast.9), channel_id=1, replica_groups=mesh['mem'=32,'gx'=2,'gy'=2] {'mem'}, dimensions={0} | all-to-all | bytes 1605632 | tf_op jit(solution)/shard_map/all_to_all | solution.py:364
  36.0 0.8 %select.1 = f32[64,24,128]{2,1,0:T(8,128)S(1)} custom-call(s32[1,64]{1,0:T(1,128)S(1)} %get-tuple-element.22.lineage_vmem, f32[1568,128]{1,0:T(8,128)S(1)} %bitcast.7), custom_call_target="tpu_custom_call" | custom-call | tf_op jit(solution)/shard_map/select/pallas_call | solution.py:365
  36.8 17.0 %all_to_all.11.back = f32[32,2,24,128]{3,2,1,0:T(8,128)S(1)} all-to-all(f32[32,2,24,128]{3,2,1,0:T(8,128)S(1)} %bitcast.10), channel_id=1, replica_groups=mesh['mem'=32,'gx'=2,'gy'=2] {'mem'}, dimensions={0} | all-to-all | bytes 1572864 | tf_op jit(solution)/shard_map/all_to_all | solution.py:374
  53.8 0.9 %finish.1 = (f32[2,32,24,128]{3,2,1,0:T(8,128)}, f32[1,1,4]{2,1,0:T(1,128)}) custom-call(f32[32,2,24,128]{3,2,1,0:T(8,128)S(1)} %all_to_all.11.back, f32[1568,128]{1,0:T(8,128)S(1)} %bitcast.8), custom_call_target="tpu_custom_call" | custom-call | tf_op jit(solution)/shard_map/finish/pallas_call | solution.py:375
Async XLA Ops:
  4.5 5.8 %collective-permute-start = (f32[128,128]{1,0:T(8,128)S(1)}, f32[128,128]{1,0:T(8,128)S(1)}, u32[]{:S(2)}, u32[]{:S(2)}) collective-permute-start(f32[128,128]{1,0:T(8,128)S(1)} %get-tuple-element.23), channel_id=1, source_target_pairs={{0,1},{1,0},{2,3},{3,2},{4,5},{5,4},{6,7},{7,6},{8,9},{9,8},{10,11... | collective-permute-start | bytes 196616 | tf_op jit(solution)/shard_map/ppermute | solution.py:304
  6.2 1.2 %collective-permute-start.1 = (f32[14,8,128]{2,1,0:T(8,128)S(1)}, f32[14,8,128]{2,1,0:T(8,128)S(1)}, u32[]{:S(2)}, u32[]{:S(2)}) collective-permute-start(f32[14,8,128]{2,1,0:T(8,128)S(1)} %get-tuple-element.24), channel_id=1, source_target_pairs={{0,2},{2,0},{1,3},{3,1},{4,6},{6,4},{5,7},{7,5},{8,10},{10,8},{9,1... | collective-permute-start | bytes 172040 | tf_op jit(solution)/shard_map/ppermute | solution.py:305
  10.3 1.3 %collective-permute-start.2 = (f32[128,128]{1,0:T(8,128)S(1)}, f32[128,128]{1,0:T(8,128)S(1)}, u32[]{:S(2)}, u32[]{:S(2)}) collective-permute-start(f32[128,128]{1,0:T(8,128)S(1)} %collective-permute-done.colrecv), channel_id=1, source_target_pairs={{0,2},{2,0},{1,3},{3,1},{4,6},{6,4},{5,7},{7,5},{8,10},{10,8},{9,1... | collective-permute-start | bytes 196616 | tf_op jit(solution)/shard_map/ppermute | solution.py:338

commit v8 on v7

--- a/solution.py
+++ b/solution.py
@@ -12,7 +12,7 @@
 OBS_VAR = 0.25
 T = 128
 F32 = jnp.float32
-CHUNK = 64
+CHUNK = 128
 
 
 def lanes(shape):
@@ -70,7 +70,7 @@
     return 0.1 + 0.2 * ((y.astype(F32) + 0.5) / total_y - 0.5)
 
 
-def pack_kernel(total_y, fields_hbm, noise_hbm, fields, noise, rowpack, colpack, inner, tmp, sems):
+def pack_kernel(fields_hbm, noise_hbm, fields, noise, rowpack, colpack, ownrow, owncol, sems):
     members = fields.shape[0]
     copies = [pltpu.make_async_copy(noise_hbm, noise, sems.at[members])]
     for m in range(members):
@@ -94,7 +94,7 @@
 
     @pl.when(lax.axis_index("gy") == 0)
     def _():
-        interior(total_y, fields, noise, inner, tmp)
+        own_strips(fields, noise, ownrow, owncol)
 
 
 def own_columns(tiles):
@@ -107,6 +107,16 @@
     return acc
 
 
+def own_strips(fields, noise, ownrow, owncol):
+    members = fields.shape[0]
+    for f in range(4):
+        tiles = [fields[m, f] if f < 3 else noise[m // 2] for m in range(members)]
+        for m, a in enumerate(tiles):
+            ownrow[f, 2 * m] = a[0:8]
+            ownrow[f, 2 * m + 1] = a[T - 8 : T]
+        owncol[f] = own_columns(tiles)
+
+
 def interior(total_y, fields, noise, inner, tmp):
     cor = coriolis(lanes((1, T)), total_y)
     for src, dst in ((fields, tmp), (tmp, inner)):
@@ -117,8 +127,8 @@
                     dst[m, f, r : r + CHUNK] = new[f]
 
 
-def interior_kernel(total_y, fields, noise, inner_in, cells_hbm, values_hbm, lineage_hbm, inner, ownrow, owncol,
-                    pick_y, cell_x, values, lineage, tmp, cells, sems):
+def interior_kernel(total_y, fields, noise, ownrow_in, owncol_in, cells_hbm, values_hbm, lineage_hbm,
+                    ownrow, owncol, inner, pick_y, cell_x, values, lineage, tmp, cells, sems):
     members = fields.shape[0]
     copies = [
         pltpu.make_async_copy(cells_hbm, cells, sems.at[0]),
@@ -130,19 +140,9 @@
 
     @pl.when(lax.axis_index("gy") != 0)
     def _():
-        interior(total_y, fields, noise, inner, tmp)
-
-    for m in range(members):
-        for f in range(4):
-            src = fields.at[m, f] if f < 3 else noise.at[m // 2]
-            ownrow[f, 2 * m] = src[0:8]
-            ownrow[f, 2 * m + 1] = src[T - 8 : T]
-    for f in range(4):
-        tiles = []
-        for m in range(members):
-            src = fields.at[m, f] if f < 3 else noise.at[m // 2]
-            tiles.append(src[...])
-        owncol[f] = own_columns(tiles)
+        own_strips(fields, noise, ownrow, owncol)
+
+    interior(total_y, fields, noise, inner, tmp)
     for copy in copies:
         copy.wait()
     cell = cells[...]
@@ -152,12 +152,10 @@
 
 
 def twice(a, a1, total, cor):
-    chunk = total // 2
     for src, dst in ((a, a1), (a1, a)):
-        for r in range(0, total, chunk):
-            new = one_step(src, (), r, chunk, total, a[3, r : r + chunk], cor)
-            for f in range(3):
-                dst[f, r : r + chunk] = new[f]
+        new = one_step(src, (), 0, total, total, a[3], cor)
+        for f in range(3):
+            dst[f, 0:total] = new[f]
 
 
 def rows_kernel(total_y, ownrow, rowrecv, edge, rs, rs1):
@@ -285,18 +283,19 @@
     members = fields.shape[0]
     devices = lax.axis_size("mem")
     total_y = T * lax.axis_size("gy")
-    fields_vm, noise_vm, rowpack, colpack, inner = pl.pallas_call(
-        functools.partial(pack_kernel, total_y),
+    fields_vm, noise_vm, rowpack, colpack, ownrow, owncol = pl.pallas_call(
+        pack_kernel,
         out_shape=(
             sds(*fields.shape),
             sds(*noise.shape),
             sds(3 * members + members // 2, 8, T),
             sds(T, T),
-            sds(members, 3, T, T),
+            sds(4, 2 * members, 8, T),
+            sds(4, T, T),
         ),
         in_specs=[HB] * 2,
-        out_specs=[VM] * 5,
-        scratch_shapes=[pltpu.VMEM((members, 3, T, T), F32), pltpu.SemaphoreType.DMA((members + 1,))],
+        out_specs=[VM] * 6,
+        scratch_shapes=[pltpu.SemaphoreType.DMA((members + 1,))],
         compiler_params=PARAMS,
         name="pack",
     )(in_hbm(fields), in_hbm(noise))
@@ -304,20 +303,20 @@
     colrecv = lax.ppermute(colpack, "gy", swap)
     rowrecv = lax.ppermute(rowpack, "gx", swap)
     count, pairs = obs_cells.shape[-1], ancestors.shape[-1]
-    inner, ownrow, owncol, pick_y, cell_x, values, lineage = pl.pallas_call(
+    ownrow, owncol, inner, pick_y, cell_x, values, lineage = pl.pallas_call(
         functools.partial(interior_kernel, total_y),
         out_shape=(
-            sds(members, 3, T, T),
             sds(4, 2 * members, 8, T),
             sds(4, T, T),
+            sds(members, 3, T, T),
             jax.ShapeDtypeStruct((T, count), jnp.bfloat16),
             jax.ShapeDtypeStruct((1, count), jnp.int32),
             sds(1, count),
             jax.ShapeDtypeStruct((1, pairs), jnp.int32),
         ),
-        in_specs=[VM] * 3 + [HB] * 3,
+        in_specs=[VM] * 4 + [HB] * 3,
         out_specs=[VM] * 7,
-        input_output_aliases={2: 0},
+        input_output_aliases={2: 0, 3: 1},
         scratch_shapes=[
             pltpu.VMEM((members, 3, T, T), F32),
             pltpu.VMEM((1, count), jnp.int32),
@@ -329,7 +328,8 @@
     )(
         fields_vm,
         noise_vm,
-        inner,
+        ownrow,
+        owncol,
         in_hbm(obs_cells.reshape(1, -1)),
         in_hbm(obs_values.reshape(1, -1)),
         in_hbm(ancestors.reshape(1, -1)),

time: 54.9 us -> 53.2 us (0.969)
  waiting for transfers between devices: 3.93 us -> 0.95 us
  starting transfers between devices: 1.77 us -> 3.65 us
  Pallas kernels: 8.22 us -> 7.59 us
    ppermute x1, waiting for transfers between devices: 2.84 us -> 0.38 us  [shards(): colrecv = lax.ppermute(colpack, 'gy', swap)]
    ppermute x1, starting transfers between devices: 1.77 us -> 3.43 us  [shards(): colrecv = lax.ppermute(colpack, 'gy', swap)]
    pallas_call x1, Pallas kernels: 3.83 us -> 2.17 us  [shards(): pl.pallas_call(pack_kernel, out_shape=(sds(*fields.shape), sds(*noise.sha...]
    pallas_call x1, Pallas kernels: 0.74 us -> 2.02 us  [shards(): pl.pallas_call(functools.partial(interior_kernel, total_y), out_shape=(sd...]
  transfers between devices with their start and end apart: 3 -> 3, of which waited for: 3 -> 2; matrix products, arithmetic and copies ran while one was open for 0% -> 0% of each run, Pallas kernels for 3% -> 5%
where the time goes in v8:
time: 53.2 us; the launch traced here: 53 us
  blocking collectives  40.1 us (75%)
  Pallas kernels  7.59 us (14%)
  starting transfers between devices  3.65 us (7%)
  waiting for transfers between devices  0.95 us (2%)
  between operations  0.68 us (1%)
    all_to_all x1, blocking collectives, shards(): lax.all_to_all(pieces.reshape(devices, stride, 1, T), 'mem', 0, 0)  23.1 us
    all_to_all x1, blocking collectives, shards(): lax.all_to_all(picked.reshape(devices, members // 2, rows, T), 'mem', 0, 0)  17 us
    ppermute x1, starting transfers between devices, shards(): colrecv = lax.ppermute(colpack, 'gy', swap)  3.43 us
    pallas_call x1, Pallas kernels, shards(): pl.pallas_call(pack_kernel, out_shape=(sds(*fields.shape), sds(*noise.sha...  2.17 us
    pallas_call x1, Pallas kernels, shards(): pl.pallas_call(functools.partial(interior_kernel, total_y), out_shape=(sd...  2.02 us
    pallas_call x1, Pallas kernels, shards(): pl.pallas_call(functools.partial(merge_kernel, total_y, devices), out_sha...  1.25 us
  transfers between devices with their start and end apart: 3, of which 2 were waited for; matrix products, arithmetic and copies ran while one was open for 0% of the time, Pallas kernels for 5%

profile of v8, /device:TPU:0, one launch (start us, length us, event | category | flops | bytes accessed | tf_op | source)
XLA Modules:
  0.0 53.0 jit_solution(14301791483061190432)
XLA Ops:
  0.6 2.2 %pack.1 = (f32[4,3,128,128]{3,2,1,0:T(8,128)S(1)}, f32[2,128,128]{2,1,0:T(8,128)S(1)}, f32[14,8,128]{2,1,0:T(8,128)S(1)}, f32[128,128]{1,0:T(8,128)S(1)}, f32[4,...) custom-call(f32[4,3,128,128]{3,2,1,0:T(8,128)} %fields_hbm.1, f32[2,128,128]{2,1,0:T(8,128)} %noise_hbm.1), custom_call_target="tpu_custom_call" | custom-call | tf_op jit(solution)/shard_map/pack/pallas_call | solution.py:286
  2.8 3.4 %collective-permute-start = (f32[128,128]{1,0:T(8,128)S(1)}, f32[128,128]{1,0:T(8,128)S(1)}, u32[]{:S(2)}, u32[]{:S(2)}) collective-permute-start(f32[128,128]{1,0:T(8,128)S(1)} %get-tuple-element.25), channel_id=1, source_target_pairs={{0,1},{1,0},{2,3},{3,2},{4,5},{5,4},{6,7},{7,6},{8,9},{9,8},{10,11... | collective-permute-start | bytes 196616 | tf_op jit(solution)/shard_map/ppermute | solution.py:303
  6.2 0.0 collective-permute-start.1
  6.2 2.0 %interior.1 = (f32[4,8,8,128]{3,2,1,0:T(8,128)S(1)}, f32[4,128,128]{2,1,0:T(8,128)S(1)}, f32[4,3,128,128]{3,2,1,0:T(8,128)S(1)}, bf16[128,256]{1,0:T(8,128)(2,1)...) custom-call(f32[4,3,128,128]{3,2,1,0:T(8,128)S(1)} %get-tuple-elemen, ...), custom_call_target="tpu_custom_call", output_to_operand_aliasing={{0}: (2, {}), {1}: (3, {})} | custom-call | flops 50000000 | bytes 2500000 | tf_op jit(solution)/shard_map/interior/pallas_call | solution.py:306
  8.3 0.0 collective-permute-done.1.rowrecv
  8.3 0.4 collective-permute-done.colrecv
  8.7 0.2 collective-permute-start.2
  8.9 0.5 rows.1.edge
  9.3 0.6 %collective-permute-done.2.cornrecv = f32[128,128]{1,0:T(8,128)S(1)} collective-permute-done((f32[128,128]{1,0:T(8,128)S(1)}, f32[128,128]{1,0:T(8,128)S(1)}, u32[]{:S(2)}, u32[]{:S(2)}) %collective-permute-start.2) | collective-permute-done | bytes 65568 | tf_op jit(solution)/shard_map/ppermute | solution.py:338
  9.9 1.2 %merge.1 = f32[1568,128]{1,0:T(8,128)S(1)} custom-call(f32[4,3,128,128]{3,2,1,0:T(8,128)S(1)} %get-tuple-element.28.inner, f32[3,8,8,128]{3,2,1,0:T(8,128)S(1)} %rows.1.edge, f32[4,128,128]{2,1,0:T(8,128)S(1)} %get-tuple-element.31.owncol, f32[14,8,128]{2,1,0:T(8,128)S(1)} %collective-permute-done.1.rowrecv, f32[128,128]{1,0:T(8,128)S(1)} %collective-permute-done.colrecv, ...), custom_call_target="tpu_custom_call" | custom-call | tf_op jit(solution)/shard_map/merge/pallas_call | solution.py:351
  11.2 23.1 %all_to_all.10 = f32[32,49,1,128]{3,2,1,0:T(1,128)S(1)} all-to-all(f32[32,49,1,128]{3,2,1,0:T(1,128)S(1)} %bitcast.9), channel_id=1, replica_groups=mesh['mem'=32,'gx'=2,'gy'=2] {'mem'}, dimensions={0} | all-to-all | bytes 1605632 | tf_op jit(solution)/shard_map/all_to_all | solution.py:364
  34.3 0.8 %select.1 = f32[64,24,128]{2,1,0:T(8,128)S(1)} custom-call(s32[1,64]{1,0:T(1,128)S(1)} %get-tuple-element.24.lineage_vmem, f32[1568,128]{1,0:T(8,128)S(1)} %bitcast.7), custom_call_target="tpu_custom_call" | custom-call | tf_op jit(solution)/shard_map/select/pallas_call | solution.py:365
  35.1 17.0 %all_to_all.11.back = f32[32,2,24,128]{3,2,1,0:T(8,128)S(1)} all-to-all(f32[32,2,24,128]{3,2,1,0:T(8,128)S(1)} %bitcast.10), channel_id=1, replica_groups=mesh['mem'=32,'gx'=2,'gy'=2] {'mem'}, dimensions={0} | all-to-all | bytes 1572864 | tf_op jit(solution)/shard_map/all_to_all | solution.py:374
  52.1 0.9 %finish.1 = (f32[2,32,24,128]{3,2,1,0:T(8,128)}, f32[1,1,4]{2,1,0:T(1,128)}) custom-call(f32[32,2,24,128]{3,2,1,0:T(8,128)S(1)} %all_to_all.11.back, f32[1568,128]{1,0:T(8,128)S(1)} %bitcast.8), custom_call_target="tpu_custom_call" | custom-call | tf_op jit(solution)/shard_map/finish/pallas_call | solution.py:375
Async XLA Ops:
  2.8 5.8 %collective-permute-start = (f32[128,128]{1,0:T(8,128)S(1)}, f32[128,128]{1,0:T(8,128)S(1)}, u32[]{:S(2)}, u32[]{:S(2)}) collective-permute-start(f32[128,128]{1,0:T(8,128)S(1)} %get-tuple-element.25), channel_id=1, source_target_pairs={{0,1},{1,0},{2,3},{3,2},{4,5},{5,4},{6,7},{7,6},{8,9},{9,8},{10,11... | collective-permute-start | bytes 196616 | tf_op jit(solution)/shard_map/ppermute | solution.py:303
  6.2 2.0 %collective-permute-start.1 = (f32[14,8,128]{2,1,0:T(8,128)S(1)}, f32[14,8,128]{2,1,0:T(8,128)S(1)}, u32[]{:S(2)}, u32[]{:S(2)}) collective-permute-start(f32[14,8,128]{2,1,0:T(8,128)S(1)} %get-tuple-element.26), channel_id=1, source_target_pairs={{0,2},{2,0},{1,3},{3,1},{4,6},{6,4},{5,7},{7,5},{8,10},{10,8},{9,1... | collective-permute-start | bytes 172040 | tf_op jit(solution)/shard_map/ppermute | solution.py:304
  8.7 1.3 %collective-permute-start.2 = (f32[128,128]{1,0:T(8,128)S(1)}, f32[128,128]{1,0:T(8,128)S(1)}, u32[]{:S(2)}, u32[]{:S(2)}) collective-permute-start(f32[128,128]{1,0:T(8,128)S(1)} %collective-permute-done.colrecv), channel_id=1, source_target_pairs={{0,2},{2,0},{1,3},{3,1},{4,6},{6,4},{5,7},{7,5},{8,10},{10,8},{9,1... | collective-permute-start | bytes 196616 | tf_op jit(solution)/shard_map/ppermute | solution.py:338

commit v9 on v8

--- a/solution.py
+++ b/solution.py
@@ -158,15 +158,35 @@
             dst[f, 0:total] = new[f]
 
 
-def rows_kernel(total_y, ownrow, rowrecv, edge, rs, rs1):
+def column_masks():
+    l32 = lax.rem(lanes((1, T)), 32)
+    cols = jnp.where(l32 < 16, l32 + 120, l32 - 24)
+    return cols, (l32 >= 20) & (l32 < 24), (l32 >= 8) & (l32 < 12)
+
+
+def with_halo(own, recv, f, is_low, is_high):
+    return jnp.where(is_low, lroll(recv, 20 - 8 * f), jnp.where(is_high, lroll(recv, 4 - 8 * f), own))
+
+
+def some_rows(src, dst, first, count, cor, force):
+    new = one_step(src, (), first, count, T + 16, force[3, first : first + count], cor)
+    for f in range(3):
+        dst[f, first : first + count] = new[f]
+
+
+def strips_kernel(total_y, ownrow, rowrecv, owncol, colrecv, edge, cs, cs1, rs, rs1):
     members = ownrow.shape[1] // 2
+    cols, is_low, is_high = column_masks()
+    halo = lambda m, f: rowrecv[3 * m + f] if f < 3 else rowrecv[3 * members + m // 2]
     for f in range(4):
         for m in range(members):
-            halo = rowrecv[3 * m + f] if f < 3 else rowrecv[3 * members + m // 2]
-            rs[f, 32 * m : 32 * m + 8] = halo
+            rs[f, 32 * m : 32 * m + 8] = halo(m, f)
             rs[f, 32 * m + 8 : 32 * m + 16] = ownrow[f, 2 * m]
             rs[f, 32 * m + 16 : 32 * m + 24] = ownrow[f, 2 * m + 1]
-            rs[f, 32 * m + 24 : 32 * m + 32] = halo
+            rs[f, 32 * m + 24 : 32 * m + 32] = halo(m, f)
+        cs[f, 0:8] = own_columns([halo(m, f) for m in range(members)])
+        cs[f, 8 : T + 8] = with_halo(owncol[f], colrecv[...], f, is_low, is_high)
+    some_rows(cs, cs1, 16, T - 16, coriolis(cols, total_y), cs)
     twice(rs, rs1, T, coriolis(lanes((1, T)), total_y))
     for f in range(3):
         for m in range(members):
@@ -174,26 +194,18 @@
             edge[f, 2 * m + 1] = rs[f, 32 * m + 16 : 32 * m + 24]
 
 
-def merge_kernel(total_y, devices, inner, edge, owncol, rowrecv, colrecv, cornrecv, pick_y, cell_x,
-                 values, out, cs, cs1, eta_s):
+def merge_kernel(total_y, devices, inner, edge, cs_in, cs1_in, cornrecv, pick_y, cell_x, values, cs, cs1, out, eta_s):
     members = inner.shape[0]
-    tall = T + 16
-    l32 = lax.rem(lanes((1, T)), 32)
-    cor_col = coriolis(jnp.where(l32 < 16, l32 + 120, l32 - 24), total_y)
-    is_low = (l32 >= 20) & (l32 < 24)
-    is_high = (l32 >= 8) & (l32 < 12)
+    cols, is_low, is_high = column_masks()
+    cor_col = coriolis(cols, total_y)
     corn = jnp.where(subl((8, T)) < 4, cornrecv[0:8], cornrecv[T - 8 : T])
-
     for f in range(4):
-        with_halo = lambda own, recv: jnp.where(
-            is_low, lroll(recv, 20 - 8 * f), jnp.where(is_high, lroll(recv, 4 - 8 * f), own)
-        )
-        tiles = [rowrecv[3 * m + f] if f < 3 else rowrecv[3 * members + m // 2] for m in range(members)]
-        ends = with_halo(own_columns(tiles), corn)
+        ends = with_halo(cs[f, 0:8], corn, f, is_low, is_high)
         cs[f, 0:8] = ends
         cs[f, T + 8 : T + 16] = ends
-        cs[f, 8 : T + 8] = with_halo(owncol[f], colrecv[...])
-    twice(cs, cs1, tall, cor_col)
+    some_rows(cs, cs1, 0, 16, cor_col, cs)
+    some_rows(cs, cs1, T, 16, cor_col, cs)
+    some_rows(cs1, cs, 8, T, cor_col, cs)
 
     per = 96 // devices
     stride = members // 2 * 8 * per + 1
@@ -336,31 +348,28 @@
     )
     colrecv, rowrecv, inner = lax.optimization_barrier((colrecv, rowrecv, inner))
     cornrecv = lax.ppermute(colrecv, "gx", swap)
-    edge = pl.pallas_call(
-        functools.partial(rows_kernel, total_y),
-        out_shape=sds(3, 2 * members, 8, T),
-        in_specs=[VM] * 2,
-        out_specs=VM,
+    edge, cs, cs1 = pl.pallas_call(
+        functools.partial(strips_kernel, total_y),
+        out_shape=(sds(3, 2 * members, 8, T), sds(4, T + 16, T), sds(3, T + 16, T)),
+        in_specs=[VM] * 4,
+        out_specs=[VM] * 3,
         scratch_shapes=[pltpu.VMEM((4, T, T), F32), pltpu.VMEM((3, T, T), F32)],
         compiler_params=PARAMS,
-        cost_estimate=pl.CostEstimate(flops=12_000_000, bytes_accessed=250_000, transcendentals=0),
-        name="rows",
-    )(ownrow, rowrecv)
+        cost_estimate=pl.CostEstimate(flops=18_000_000, bytes_accessed=700_000, transcendentals=0),
+        name="strips",
+    )(ownrow, rowrecv, owncol, colrecv)
     rows = 768 // devices
     stride = members // 2 * rows + 1
-    pieces = pl.pallas_call(
+    _, _, pieces = pl.pallas_call(
         functools.partial(merge_kernel, total_y, devices),
-        out_shape=sds(devices * stride, T),
-        in_specs=[VM] * 9,
-        out_specs=VM,
-        scratch_shapes=[
-            pltpu.VMEM((4, T + 16, T), F32),
-            pltpu.VMEM((3, T + 16, T), F32),
-            pltpu.VMEM((members * T, T), F32),
-        ],
+        out_shape=(sds(4, T + 16, T), sds(3, T + 16, T), sds(devices * stride, T)),
+        in_specs=[VM] * 8,
+        out_specs=[VM] * 3,
+        input_output_aliases={2: 0, 3: 1},
+        scratch_shapes=[pltpu.VMEM((members * T, T), F32)],
         compiler_params=PARAMS,
         name="merge",
-    )(inner, edge, owncol, rowrecv, colrecv, cornrecv, pick_y, cell_x, values)
+    )(inner, edge, cs, cs1, cornrecv, pick_y, cell_x, values)
     held = lax.all_to_all(pieces.reshape(devices, stride, 1, T), "mem", 0, 0).reshape(devices * stride, T)
     picked = pl.pallas_call(
         functools.partial(select_kernel, members),

time: 53.2 us -> 52.9 us (level)
  no operation moved by 1% of the time
where the time goes in v9:
time: 52.9 us; the launch traced here: 52.7 us
  blocking collectives  40.1 us (76%)
  Pallas kernels  7.7 us (15%)
  starting transfers between devices  3.65 us (7%)
  between operations  0.68 us (1%)
  waiting for transfers between devices  0.55 us (1%)
    all_to_all x1, blocking collectives, shards(): lax.all_to_all(pieces.reshape(devices, stride, 1, T), 'mem', 0, 0)  23.1 us
    all_to_all x1, blocking collectives, shards(): lax.all_to_all(picked.reshape(devices, members // 2, rows, T), 'mem', 0, 0)  17 us
    ppermute x1, starting transfers between devices, shards(): colrecv = lax.ppermute(colpack, 'gy', swap)  3.43 us
    pallas_call x1, Pallas kernels, shards(): pl.pallas_call(pack_kernel, out_shape=(sds(*fields.shape), sds(*noise.sha...  2.17 us
    pallas_call x1, Pallas kernels, shards(): pl.pallas_call(functools.partial(interior_kernel, total_y), out_shape=(sd...  2.02 us
  transfers between devices with their start and end apart: 3, of which 2 were waited for; matrix products, arithmetic and copies ran while one was open for 0% of the time, Pallas kernels for 5%

profile of v9, /device:TPU:0, one launch (start us, length us, event | category | flops | bytes accessed | tf_op | source)
XLA Modules:
  0.0 52.7 jit_solution(11727419902421758701)
XLA Ops:
  0.6 2.2 %pack.1 = (f32[4,3,128,128]{3,2,1,0:T(8,128)S(1)}, f32[2,128,128]{2,1,0:T(8,128)S(1)}, f32[14,8,128]{2,1,0:T(8,128)S(1)}, f32[128,128]{1,0:T(8,128)S(1)}, f32[4,...) custom-call(f32[4,3,128,128]{3,2,1,0:T(8,128)} %fields_hbm.1, f32[2,128,128]{2,1,0:T(8,128)} %noise_hbm.1), custom_call_target="tpu_custom_call" | custom-call | tf_op jit(solution)/shard_map/pack/pallas_call | solution.py:298
  2.8 3.4 %collective-permute-start = (f32[128,128]{1,0:T(8,128)S(1)}, f32[128,128]{1,0:T(8,128)S(1)}, u32[]{:S(2)}, u32[]{:S(2)}) collective-permute-start(f32[128,128]{1,0:T(8,128)S(1)} %get-tuple-element.29), channel_id=1, source_target_pairs={{0,1},{1,0},{2,3},{3,2},{4,5},{5,4},{6,7},{7,6},{8,9},{9,8},{10,11... | collective-permute-start | bytes 196616 | tf_op jit(solution)/shard_map/ppermute | solution.py:315
  6.2 0.0 collective-permute-start.1
  6.2 2.0 %interior.1 = (f32[4,8,8,128]{3,2,1,0:T(8,128)S(1)}, f32[4,128,128]{2,1,0:T(8,128)S(1)}, f32[4,3,128,128]{3,2,1,0:T(8,128)S(1)}, bf16[128,256]{1,0:T(8,128)(2,1)...) custom-call(f32[4,3,128,128]{3,2,1,0:T(8,128)S(1)} %get-tuple-elemen, ...), custom_call_target="tpu_custom_call", output_to_operand_aliasing={{0}: (2, {}), {1}: (3, {})} | custom-call | flops 50000000 | bytes 2500000 | tf_op jit(solution)/shard_map/interior/pallas_call | solution.py:318
  8.3 0.0 collective-permute-done.1.rowrecv
  8.3 0.4 collective-permute-done.colrecv
  8.7 0.2 collective-permute-start.2
  8.9 0.9 %strips.1 = (f32[3,8,8,128]{3,2,1,0:T(8,128)S(1)}, f32[4,144,128]{2,1,0:T(8,128)S(1)}, f32[3,144,128]{2,1,0:T(8,128)S(1)}) custom-call(f32[4,8,8,128]{3,2,1,0:T(8,128)S(1)} %get-tuple-element.33.ownrow, f32[14,8,128]{2,1,0:T(8,128)S(1)} %collective-permute-done.1.rowrecv, f32[4,128,128]{2,1,0:T(8,128)S(1)} %get-tuple-element.35.owncol, ...), custom_call_target="tpu_custom_call" | custom-call | flops 18000000 | bytes 700000 | tf_op jit(solution)/shard_map/strips/pallas_call | solution.py:351
  9.7 0.2 collective-permute-done.2.cornrecv
  9.9 1.0 %merge.1 = (f32[4,144,128]{2,1,0:T(8,128)S(1)}, f32[3,144,128]{2,1,0:T(8,128)S(1)}, f32[1568,128]{1,0:T(8,128)S(1)}) custom-call(f32[4,3,128,128]{3,2,1,0:T(8,128)S(1)} %get-tuple-element.32.inner, f32[3,8,8,128]{3,2,1,0:T(8,128)S(1)} %get-tuple-element.37.edge, ...), custom_call_target="tpu_custom_call", output_to_operand_aliasing={{0}: (2, {}), {1}: (3, {})} | custom-call | tf_op jit(solution)/shard_map/merge/pallas_call | solution.py:363
  10.9 23.1 %all_to_all.10 = f32[32,49,1,128]{3,2,1,0:T(1,128)S(1)} all-to-all(f32[32,49,1,128]{3,2,1,0:T(1,128)S(1)} %bitcast.10), channel_id=1, replica_groups=mesh['mem'=32,'gx'=2,'gy'=2] {'mem'}, dimensions={0} | all-to-all | bytes 1605632 | tf_op jit(solution)/shard_map/all_to_all | solution.py:373
  34.0 0.8 %select.1 = f32[64,24,128]{2,1,0:T(8,128)S(1)} custom-call(s32[1,64]{1,0:T(1,128)S(1)} %get-tuple-element.28.lineage_vmem, f32[1568,128]{1,0:T(8,128)S(1)} %bitcast.7), custom_call_target="tpu_custom_call" | custom-call | tf_op jit(solution)/shard_map/select/pallas_call | solution.py:374
  34.8 17.0 %all_to_all.11.back = f32[32,2,24,128]{3,2,1,0:T(8,128)S(1)} all-to-all(f32[32,2,24,128]{3,2,1,0:T(8,128)S(1)} %bitcast.9), channel_id=1, replica_groups=mesh['mem'=32,'gx'=2,'gy'=2] {'mem'}, dimensions={0} | all-to-all | bytes 1572864 | tf_op jit(solution)/shard_map/all_to_all | solution.py:383
  51.8 0.9 %finish.1 = (f32[2,32,24,128]{3,2,1,0:T(8,128)}, f32[1,1,4]{2,1,0:T(1,128)}) custom-call(f32[32,2,24,128]{3,2,1,0:T(8,128)S(1)} %all_to_all.11.back, f32[1568,128]{1,0:T(8,128)S(1)} %bitcast.8), custom_call_target="tpu_custom_call" | custom-call | tf_op jit(solution)/shard_map/finish/pallas_call | solution.py:384
Async XLA Ops:
  2.8 5.8 %collective-permute-start = (f32[128,128]{1,0:T(8,128)S(1)}, f32[128,128]{1,0:T(8,128)S(1)}, u32[]{:S(2)}, u32[]{:S(2)}) collective-permute-start(f32[128,128]{1,0:T(8,128)S(1)} %get-tuple-element.29), channel_id=1, source_target_pairs={{0,1},{1,0},{2,3},{3,2},{4,5},{5,4},{6,7},{7,6},{8,9},{9,8},{10,11... | collective-permute-start | bytes 196616 | tf_op jit(solution)/shard_map/ppermute | solution.py:315
  6.2 2.0 %collective-permute-start.1 = (f32[14,8,128]{2,1,0:T(8,128)S(1)}, f32[14,8,128]{2,1,0:T(8,128)S(1)}, u32[]{:S(2)}, u32[]{:S(2)}) collective-permute-start(f32[14,8,128]{2,1,0:T(8,128)S(1)} %get-tuple-element.30), channel_id=1, source_target_pairs={{0,2},{2,0},{1,3},{3,1},{4,6},{6,4},{5,7},{7,5},{8,10},{10,8},{9,1... | collective-permute-start | bytes 172040 | tf_op jit(solution)/shard_map/ppermute | solution.py:316
  8.7 1.3 %collective-permute-start.2 = (f32[128,128]{1,0:T(8,128)S(1)}, f32[128,128]{1,0:T(8,128)S(1)}, u32[]{:S(2)}, u32[]{:S(2)}) collective-permute-start(f32[128,128]{1,0:T(8,128)S(1)} %collective-permute-done.colrecv), channel_id=1, source_target_pairs={{0,2},{2,0},{1,3},{3,1},{4,6},{6,4},{5,7},{7,5},{8,10},{10,8},{9,1... | collective-permute-start | bytes 196616 | tf_op jit(solution)/shard_map/ppermute | solution.py:350

commit v10 on v9

--- a/solution.py
+++ b/solution.py
@@ -248,12 +248,9 @@
         out[(j + 1) * stride - 1 : (j + 1) * stride] = logw
 
 
-def select_kernel(members, lineage_vmem, recv, out, lineage, sem):
-    copy = pltpu.make_async_copy(lineage_vmem, lineage, sem)
-    copy.start()
+def select_kernel(members, lineage, recv, out):
     pairs, rows = out.shape[0], out.shape[1]
     per = members // 2
-    copy.wait()
     for k in range(pairs):
         pair = lineage[0, k]
         out[k] = recv[pl.ds(lax.div(pair, per) * (per * rows + 1) + lax.rem(pair, per) * rows, rows)]
@@ -376,7 +373,6 @@
         out_shape=sds(pairs, rows, T),
         in_specs=[VM, VM],
         out_specs=VM,
-        scratch_shapes=[pltpu.SMEM((1, pairs), jnp.int32), pltpu.SemaphoreType.DMA],
         compiler_params=PARAMS,
         name="select",
     )(lineage, held)

time: 52.9 us -> 52.5 us (level)
  transfers between devices with their start and end apart: 3 -> 3, of which waited for: 2 -> 2; matrix products, arithmetic and copies ran while one was open for 0% -> 0% of each run, Pallas kernels for 5% -> 6%
where the time goes in v10:
time: 52.5 us; the launch traced here: 52.3 us
  blocking collectives  40.1 us (76%)
  Pallas kernels  7.25 us (14%)
  starting transfers between devices  3.65 us (7%)
  between operations  0.68 us (1%)
  waiting for transfers between devices  0.55 us (1%)
    all_to_all x1, blocking collectives, shards(): lax.all_to_all(pieces.reshape(devices, stride, 1, T), 'mem', 0, 0)  23.1 us
    all_to_all x1, blocking collectives, shards(): lax.all_to_all(picked.reshape(devices, members // 2, rows, T), 'mem', 0, 0)  17 us
    ppermute x1, starting transfers between devices, shards(): colrecv = lax.ppermute(colpack, 'gy', swap)  3.43 us
    pallas_call x1, Pallas kernels, shards(): pl.pallas_call(pack_kernel, out_shape=(sds(*fields.shape), sds(*noise.sha...  2.17 us
    pallas_call x1, Pallas kernels, shards(): pl.pallas_call(functools.partial(interior_kernel, total_y), out_shape=(sd...  2.02 us
  transfers between devices with their start and end apart: 3, of which 2 were waited for; matrix products, arithmetic and copies ran while one was open for 0% of the time, Pallas kernels for 6%

profile of v10, /device:TPU:0, one launch (start us, length us, event | category | flops | bytes accessed | tf_op | source)
XLA Modules:
  0.0 52.3 jit_solution(11828281278109275400)
XLA Ops:
  0.6 2.2 %pack.1 = (f32[4,3,128,128]{3,2,1,0:T(8,128)S(1)}, f32[2,128,128]{2,1,0:T(8,128)S(1)}, f32[14,8,128]{2,1,0:T(8,128)S(1)}, f32[128,128]{1,0:T(8,128)S(1)}, f32[4,...) custom-call(f32[4,3,128,128]{3,2,1,0:T(8,128)} %fields_hbm.1, f32[2,128,128]{2,1,0:T(8,128)} %noise_hbm.1), custom_call_target="tpu_custom_call" | custom-call | tf_op jit(solution)/shard_map/pack/pallas_call | solution.py:295
  2.8 3.4 %collective-permute-start = (f32[128,128]{1,0:T(8,128)S(1)}, f32[128,128]{1,0:T(8,128)S(1)}, u32[]{:S(2)}, u32[]{:S(2)}) collective-permute-start(f32[128,128]{1,0:T(8,128)S(1)} %get-tuple-element.29), channel_id=1, source_target_pairs={{0,1},{1,0},{2,3},{3,2},{4,5},{5,4},{6,7},{7,6},{8,9},{9,8},{10,11... | collective-permute-start | bytes 196616 | tf_op jit(solution)/shard_map/ppermute | solution.py:312
  6.2 0.0 collective-permute-start.1
  6.2 2.0 %interior.1 = (f32[4,8,8,128]{3,2,1,0:T(8,128)S(1)}, f32[4,128,128]{2,1,0:T(8,128)S(1)}, f32[4,3,128,128]{3,2,1,0:T(8,128)S(1)}, bf16[128,256]{1,0:T(8,128)(2,1)...) custom-call(f32[4,3,128,128]{3,2,1,0:T(8,128)S(1)} %get-tuple-elemen, ...), custom_call_target="tpu_custom_call", output_to_operand_aliasing={{0}: (2, {}), {1}: (3, {})} | custom-call | flops 50000000 | bytes 2500000 | tf_op jit(solution)/shard_map/interior/pallas_call | solution.py:315
  8.3 0.0 collective-permute-done.1.rowrecv
  8.3 0.4 collective-permute-done.colrecv
  8.7 0.2 collective-permute-start.2
  8.9 0.9 %strips.1 = (f32[3,8,8,128]{3,2,1,0:T(8,128)S(1)}, f32[4,144,128]{2,1,0:T(8,128)S(1)}, f32[3,144,128]{2,1,0:T(8,128)S(1)}) custom-call(f32[4,8,8,128]{3,2,1,0:T(8,128)S(1)} %get-tuple-element.33.ownrow, f32[14,8,128]{2,1,0:T(8,128)S(1)} %collective-permute-done.1.rowrecv, f32[4,128,128]{2,1,0:T(8,128)S(1)} %get-tuple-element.35.owncol, ...), custom_call_target="tpu_custom_call" | custom-call | flops 18000000 | bytes 700000 | tf_op jit(solution)/shard_map/strips/pallas_call | solution.py:348
  9.7 0.2 collective-permute-done.2.cornrecv
  9.9 1.0 %merge.1 = (f32[4,144,128]{2,1,0:T(8,128)S(1)}, f32[3,144,128]{2,1,0:T(8,128)S(1)}, f32[1568,128]{1,0:T(8,128)S(1)}) custom-call(f32[4,3,128,128]{3,2,1,0:T(8,128)S(1)} %get-tuple-element.32.inner, f32[3,8,8,128]{3,2,1,0:T(8,128)S(1)} %get-tuple-element.37.edge, ...), custom_call_target="tpu_custom_call", output_to_operand_aliasing={{0}: (2, {}), {1}: (3, {})} | custom-call | tf_op jit(solution)/shard_map/merge/pallas_call | solution.py:360
  10.9 23.1 %all_to_all.10 = f32[32,49,1,128]{3,2,1,0:T(1,128)S(1)} all-to-all(f32[32,49,1,128]{3,2,1,0:T(1,128)S(1)} %bitcast.10), channel_id=1, replica_groups=mesh['mem'=32,'gx'=2,'gy'=2] {'mem'}, dimensions={0} | all-to-all | bytes 1605632 | tf_op jit(solution)/shard_map/all_to_all | solution.py:370
  34.0 0.3 select.1
  34.3 17.0 %all_to_all.11.back = f32[32,2,24,128]{3,2,1,0:T(8,128)S(1)} all-to-all(f32[32,2,24,128]{3,2,1,0:T(8,128)S(1)} %bitcast.9), channel_id=1, replica_groups=mesh['mem'=32,'gx'=2,'gy'=2] {'mem'}, dimensions={0} | all-to-all | bytes 1572864 | tf_op jit(solution)/shard_map/all_to_all | solution.py:379
  51.4 0.9 %finish.1 = (f32[2,32,24,128]{3,2,1,0:T(8,128)}, f32[1,1,4]{2,1,0:T(1,128)}) custom-call(f32[32,2,24,128]{3,2,1,0:T(8,128)S(1)} %all_to_all.11.back, f32[1568,128]{1,0:T(8,128)S(1)} %bitcast.8), custom_call_target="tpu_custom_call" | custom-call | tf_op jit(solution)/shard_map/finish/pallas_call | solution.py:380
Async XLA Ops:
  2.8 5.8 %collective-permute-start = (f32[128,128]{1,0:T(8,128)S(1)}, f32[128,128]{1,0:T(8,128)S(1)}, u32[]{:S(2)}, u32[]{:S(2)}) collective-permute-start(f32[128,128]{1,0:T(8,128)S(1)} %get-tuple-element.29), channel_id=1, source_target_pairs={{0,1},{1,0},{2,3},{3,2},{4,5},{5,4},{6,7},{7,6},{8,9},{9,8},{10,11... | collective-permute-start | bytes 196616 | tf_op jit(solution)/shard_map/ppermute | solution.py:312
  6.2 2.0 %collective-permute-start.1 = (f32[14,8,128]{2,1,0:T(8,128)S(1)}, f32[14,8,128]{2,1,0:T(8,128)S(1)}, u32[]{:S(2)}, u32[]{:S(2)}) collective-permute-start(f32[14,8,128]{2,1,0:T(8,128)S(1)} %get-tuple-element.30), channel_id=1, source_target_pairs={{0,2},{2,0},{1,3},{3,1},{4,6},{6,4},{5,7},{7,5},{8,10},{10,8},{9,1... | collective-permute-start | bytes 172040 | tf_op jit(solution)/shard_map/ppermute | solution.py:313
  8.7 1.3 %collective-permute-start.2 = (f32[128,128]{1,0:T(8,128)S(1)}, f32[128,128]{1,0:T(8,128)S(1)}, u32[]{:S(2)}, u32[]{:S(2)}) collective-permute-start(f32[128,128]{1,0:T(8,128)S(1)} %collective-permute-done.colrecv), channel_id=1, source_target_pairs={{0,2},{2,0},{1,3},{3,1},{4,6},{6,4},{5,7},{7,5},{8,10},{10,8},{9,1... | collective-permute-start | bytes 196616 | tf_op jit(solution)/shard_map/ppermute | solution.py:347

commit v11 on v10

--- a/solution.py
+++ b/solution.py
@@ -70,6 +70,30 @@
     return 0.1 + 0.2 * ((y.astype(F32) + 0.5) / total_y - 0.5)
 
 
+USED = (0, 1, 2, 4, 5, 6, 8, 9, 10, 12, 13, 14, 3)
+SPARE = (7, 11, 15)
+
+
+def fold(acc):
+    ln = lanes((8, T)) // 8
+    short = []
+    for i, group in enumerate(USED):
+        tile = acc[8 * i : 8 * i + 8]
+        for j, spare in enumerate(SPARE):
+            last = acc[8 * (len(USED) + j) : 8 * (len(USED) + j) + 8]
+            tile = jnp.where(ln == spare, lroll(last, 8 * (spare - group)), tile)
+        short.append(tile)
+    return short
+
+
+def unfold(ref, j):
+    ln = lanes((8, T)) // 8
+    tile = jnp.zeros((8, T), F32)
+    for i, group in enumerate(USED):
+        tile = jnp.where(ln == group, lroll(ref[8 * i : 8 * i + 8], 8 * (group - SPARE[j])), tile)
+    return tile
+
+
 def pack_kernel(fields_hbm, noise_hbm, fields, noise, rowpack, colpack, ownrow, owncol, sems):
     members = fields.shape[0]
     copies = [pltpu.make_async_copy(noise_hbm, noise, sems.at[members])]
@@ -80,17 +104,19 @@
     copies[0].wait()
     top = subl((8, T)) < 4
     ln = lanes((T, T)) // 8
-    for p in range(members // 2):
-        rowpack[3 * members + p] = jnp.where(top, noise[p, 0:8], noise[p, T - 8 : T])
-    acc = jnp.zeros((T, T), F32)
-    for m in range(members):
-        acc = jnp.where(ln == 4 * m + 3, lroll(noise[m // 2], 32 * m + 28), acc)
+    sub, lane = subl((8, T)), lanes((T, T))
+    near = jnp.where(sub < 2, noise[0, 0:8], pltpu.roll(noise[1, 0:8], 2, 0))
+    far = jnp.where(sub < 6, pltpu.roll(noise[1, T - 8 : T], 6, 0), noise[0, T - 8 : T])
+    rowpack[3 * members] = jnp.where(top, near, far)
+    acc = jnp.where((lane >= 24) & (lane < 28), lroll(noise[0], 26), 0.0)
+    acc = jnp.where((lane >= 28) & (lane < 32), lroll(noise[1], 30), acc)
     for m in range(members):
         copies[1 + m].wait()
         for f in range(3):
             rowpack[3 * m + f] = jnp.where(top, fields[m, f, 0:8], fields[m, f, T - 8 : T])
             acc = jnp.where(ln == 4 * m + f, lroll(fields[m, f], 32 * m + 8 * f + 4), acc)
-    colpack[...] = acc
+    for i, tile in enumerate(fold(acc)):
+        colpack[8 * i : 8 * i + 8] = tile
 
     @pl.when(lax.axis_index("gy") == 0)
     def _():
@@ -165,6 +191,13 @@
 
 
 def with_halo(own, recv, f, is_low, is_high):
+    if f == 3:
+        lane = lanes((1, T))
+        for m in range(4):
+            p = m // 2
+            own = jnp.where(lane // 2 == 16 * m + 11, lroll(recv, 32 * m - 2 - 4 * p), own)
+            own = jnp.where(lane // 2 == 16 * m + 4, lroll(recv, 32 * m - 18 - 4 * p), own)
+        return own
     return jnp.where(is_low, lroll(recv, 20 - 8 * f), jnp.where(is_high, lroll(recv, 4 - 8 * f), own))
 
 
@@ -177,7 +210,11 @@
 def strips_kernel(total_y, ownrow, rowrecv, owncol, colrecv, edge, cs, cs1, rs, rs1):
     members = ownrow.shape[1] // 2
     cols, is_low, is_high = column_masks()
-    halo = lambda m, f: rowrecv[3 * m + f] if f < 3 else rowrecv[3 * members + m // 2]
+    noise = rowrecv[3 * members]
+    inside = jnp.where(subl((8, T)) < 4, pltpu.roll(noise, 6, 0), pltpu.roll(noise, 2, 0))
+    halo = lambda m, f: rowrecv[3 * m + f] if f < 3 else (noise, inside)[m // 2]
+    held = 8 * len(USED)
+    last = [unfold(colrecv, j) for j in range(len(SPARE))]
     for f in range(4):
         for m in range(members):
             rs[f, 32 * m : 32 * m + 8] = halo(m, f)
@@ -185,7 +222,10 @@
             rs[f, 32 * m + 16 : 32 * m + 24] = ownrow[f, 2 * m + 1]
             rs[f, 32 * m + 24 : 32 * m + 32] = halo(m, f)
         cs[f, 0:8] = own_columns([halo(m, f) for m in range(members)])
-        cs[f, 8 : T + 8] = with_halo(owncol[f], colrecv[...], f, is_low, is_high)
+        cs[f, 8 : held + 8] = with_halo(owncol[f, 0:held], colrecv[...], f, is_low, is_high)
+        for j, tile in enumerate(last):
+            k = held + 8 * j
+            cs[f, k + 8 : k + 16] = with_halo(owncol[f, k : k + 8], tile, f, is_low, is_high)
     some_rows(cs, cs1, 16, T - 16, coriolis(cols, total_y), cs)
     twice(rs, rs1, T, coriolis(lanes((1, T)), total_y))
     for f in range(3):
@@ -198,7 +238,7 @@
     members = inner.shape[0]
     cols, is_low, is_high = column_masks()
     cor_col = coriolis(cols, total_y)
-    corn = jnp.where(subl((8, T)) < 4, cornrecv[0:8], cornrecv[T - 8 : T])
+    corn = jnp.where(subl((8, T)) < 4, cornrecv[0:8], unfold(cornrecv, len(SPARE) - 1))
     for f in range(4):
         ends = with_halo(cs[f, 0:8], corn, f, is_low, is_high)
         cs[f, 0:8] = ends
@@ -297,8 +337,8 @@
         out_shape=(
             sds(*fields.shape),
             sds(*noise.shape),
-            sds(3 * members + members // 2, 8, T),
-            sds(T, T),
+            sds(3 * members + 1, 8, T),
+            sds(8 * len(USED), T),
             sds(4, 2 * members, 8, T),
             sds(4, T, T),
         ),

time: 52.5 us -> 52.8 us (level)
  transfers between devices with their start and end apart: 3 -> 3, of which waited for: 2 -> 1; matrix products, arithmetic and copies ran while one was open for 0% -> 0% of each run, Pallas kernels for 6% -> 6%
where the time goes in v11:
time: 52.8 us; the launch traced here: 52.6 us
  blocking collectives  40.3 us (76%)
  Pallas kernels  7.56 us (14%)
  starting transfers between devices  3.78 us (7%)
  between operations  0.68 us (1%)
    all_to_all x1, blocking collectives, shards(): lax.all_to_all(pieces.reshape(devices, stride, 1, T), 'mem', 0, 0)  23.1 us
    all_to_all x1, blocking collectives, shards(): lax.all_to_all(picked.reshape(devices, members // 2, rows, T), 'mem', 0, 0)  17.2 us
    ppermute x1, starting transfers between devices, shards(): colrecv = lax.ppermute(colpack, 'gy', swap)  3.43 us
    pallas_call x1, Pallas kernels, shards(): pl.pallas_call(pack_kernel, out_shape=(sds(*fields.shape), sds(*noise.sha...  2.22 us
    pallas_call x1, Pallas kernels, shards(): pl.pallas_call(functools.partial(interior_kernel, total_y), out_shape=(sd...  2.02 us
  transfers between devices with their start and end apart: 3, of which 1 were waited for; matrix products, arithmetic and copies ran while one was open for 0% of the time, Pallas kernels for 6%

profile of v11, /device:TPU:0, one launch (start us, length us, event | category | flops | bytes accessed | tf_op | source)
XLA Modules:
  0.0 52.6 jit_solution(15794092647857694539)
XLA Ops:
  0.6 2.2 %pack.1 = (f32[4,3,128,128]{3,2,1,0:T(8,128)S(1)}, f32[2,128,128]{2,1,0:T(8,128)S(1)}, f32[13,8,128]{2,1,0:T(8,128)S(1)}, f32[104,128]{1,0:T(8,128)S(1)}, f32[4,...) custom-call(f32[4,3,128,128]{3,2,1,0:T(8,128)} %fields_hbm.1, f32[2,128,128]{2,1,0:T(8,128)} %noise_hbm.1), custom_call_target="tpu_custom_call" | custom-call | tf_op jit(solution)/shard_map/pack/pallas_call | solution.py:335
  2.9 3.4 %collective-permute-start = (f32[104,128]{1,0:T(8,128)S(1)}, f32[104,128]{1,0:T(8,128)S(1)}, u32[]{:S(2)}, u32[]{:S(2)}) collective-permute-start(f32[104,128]{1,0:T(8,128)S(1)} %get-tuple-element.29), channel_id=1, source_target_pairs={{0,1},{1,0},{2,3},{3,2},{4,5},{5,4},{6,7},{7,6},{8,9},{9,8},{10,11... | collective-permute-start | bytes 159752 | tf_op jit(solution)/shard_map/ppermute | solution.py:352
  6.3 0.0 collective-permute-start.1
  6.3 2.0 %interior.1 = (f32[4,8,8,128]{3,2,1,0:T(8,128)S(1)}, f32[4,128,128]{2,1,0:T(8,128)S(1)}, f32[4,3,128,128]{3,2,1,0:T(8,128)S(1)}, bf16[128,256]{1,0:T(8,128)(2,1)...) custom-call(f32[4,3,128,128]{3,2,1,0:T(8,128)S(1)} %get-tuple-elemen, ...), custom_call_target="tpu_custom_call", output_to_operand_aliasing={{0}: (2, {}), {1}: (3, {})} | custom-call | flops 50000000 | bytes 2500000 | tf_op jit(solution)/shard_map/interior/pallas_call | solution.py:355
  8.3 0.3 collective-permute-done.colrecv
  8.6 0.0 collective-permute-done.1.rowrecv
  8.6 0.3 collective-permute-start.2
  8.9 1.0 %strips.1 = (f32[3,8,8,128]{3,2,1,0:T(8,128)S(1)}, f32[4,144,128]{2,1,0:T(8,128)S(1)}, f32[3,144,128]{2,1,0:T(8,128)S(1)}) custom-call(f32[4,8,8,128]{3,2,1,0:T(8,128)S(1)} %get-tuple-element.33.ownrow, f32[13,8,128]{2,1,0:T(8,128)S(1)} %collective-permute-done.1.rowrecv, f32[4,128,128]{2,1,0:T(8,128)S(1)} %get-tuple-element.35.owncol, ...), custom_call_target="tpu_custom_call" | custom-call | flops 18000000 | bytes 700000 | tf_op jit(solution)/shard_map/strips/pallas_call | solution.py:388
  10.0 0.0 collective-permute-done.2.cornrecv
  10.0 1.0 %merge.1 = (f32[4,144,128]{2,1,0:T(8,128)S(1)}, f32[3,144,128]{2,1,0:T(8,128)S(1)}, f32[1568,128]{1,0:T(8,128)S(1)}) custom-call(f32[4,3,128,128]{3,2,1,0:T(8,128)S(1)} %get-tuple-element.32.inner, f32[3,8,8,128]{3,2,1,0:T(8,128)S(1)} %get-tuple-element.37.edge, ...), custom_call_target="tpu_custom_call", output_to_operand_aliasing={{0}: (2, {}), {1}: (3, {})} | custom-call | tf_op jit(solution)/shard_map/merge/pallas_call | solution.py:400
  11.0 23.1 %all_to_all.10 = f32[32,49,1,128]{3,2,1,0:T(1,128)S(1)} all-to-all(f32[32,49,1,128]{3,2,1,0:T(1,128)S(1)} %bitcast.10), channel_id=1, replica_groups=mesh['mem'=32,'gx'=2,'gy'=2] {'mem'}, dimensions={0} | all-to-all | bytes 1605632 | tf_op jit(solution)/shard_map/all_to_all | solution.py:410
  34.2 0.3 select.1
  34.5 17.2 %all_to_all.11.back = f32[32,2,24,128]{3,2,1,0:T(8,128)S(1)} all-to-all(f32[32,2,24,128]{3,2,1,0:T(8,128)S(1)} %bitcast.9), channel_id=1, replica_groups=mesh['mem'=32,'gx'=2,'gy'=2] {'mem'}, dimensions={0} | all-to-all | bytes 1572864 | tf_op jit(solution)/shard_map/all_to_all | solution.py:419
  51.7 0.9 %finish.1 = (f32[2,32,24,128]{3,2,1,0:T(8,128)}, f32[1,1,4]{2,1,0:T(1,128)}) custom-call(f32[32,2,24,128]{3,2,1,0:T(8,128)S(1)} %all_to_all.11.back, f32[1568,128]{1,0:T(8,128)S(1)} %bitcast.8), custom_call_target="tpu_custom_call" | custom-call | tf_op jit(solution)/shard_map/finish/pallas_call | solution.py:420
Async XLA Ops:
  2.9 5.7 %collective-permute-start = (f32[104,128]{1,0:T(8,128)S(1)}, f32[104,128]{1,0:T(8,128)S(1)}, u32[]{:S(2)}, u32[]{:S(2)}) collective-permute-start(f32[104,128]{1,0:T(8,128)S(1)} %get-tuple-element.29), channel_id=1, source_target_pairs={{0,1},{1,0},{2,3},{3,2},{4,5},{5,4},{6,7},{7,6},{8,9},{9,8},{10,11... | collective-permute-start | bytes 159752 | tf_op jit(solution)/shard_map/ppermute | solution.py:352
  6.3 2.3 %collective-permute-start.1 = (f32[13,8,128]{2,1,0:T(8,128)S(1)}, f32[13,8,128]{2,1,0:T(8,128)S(1)}, u32[]{:S(2)}, u32[]{:S(2)}) collective-permute-start(f32[13,8,128]{2,1,0:T(8,128)S(1)} %get-tuple-element.30), channel_id=1, source_target_pairs={{0,2},{2,0},{1,3},{3,1},{4,6},{6,4},{5,7},{7,5},{8,10},{10,8},{9,1... | collective-permute-start | bytes 159752 | tf_op jit(solution)/shard_map/ppermute | solution.py:353
  8.6 1.4 %collective-permute-start.2 = (f32[104,128]{1,0:T(8,128)S(1)}, f32[104,128]{1,0:T(8,128)S(1)}, u32[]{:S(2)}, u32[]{:S(2)}) collective-permute-start(f32[104,128]{1,0:T(8,128)S(1)} %collective-permute-done.colrecv), channel_id=1, source_target_pairs={{0,2},{2,0},{1,3},{3,1},{4,6},{6,4},{5,7},{7,5},{8,10},{10,8},{9,1... | collective-permute-start | bytes 159752 | tf_op jit(solution)/shard_map/ppermute | solution.py:387

commit v12 on v10

--- a/solution.py
+++ b/solution.py
@@ -70,7 +70,7 @@
     return 0.1 + 0.2 * ((y.astype(F32) + 0.5) / total_y - 0.5)
 
 
-def pack_kernel(fields_hbm, noise_hbm, fields, noise, rowpack, colpack, ownrow, owncol, sems):
+def pack_kernel(fields_hbm, noise_hbm, fields, noise, rowpack, colpack, sems):
     members = fields.shape[0]
     copies = [pltpu.make_async_copy(noise_hbm, noise, sems.at[members])]
     for m in range(members):
@@ -91,10 +91,6 @@
             rowpack[3 * m + f] = jnp.where(top, fields[m, f, 0:8], fields[m, f, T - 8 : T])
             acc = jnp.where(ln == 4 * m + f, lroll(fields[m, f], 32 * m + 8 * f + 4), acc)
     colpack[...] = acc
-
-    @pl.when(lax.axis_index("gy") == 0)
-    def _():
-        own_strips(fields, noise, ownrow, owncol)
 
 
 def own_columns(tiles):
@@ -127,7 +123,7 @@
                     dst[m, f, r : r + CHUNK] = new[f]
 
 
-def interior_kernel(total_y, fields, noise, ownrow_in, owncol_in, cells_hbm, values_hbm, lineage_hbm,
+def interior_kernel(total_y, fields, noise, cells_hbm, values_hbm, lineage_hbm,
                     ownrow, owncol, inner, pick_y, cell_x, values, lineage, tmp, cells, sems):
     members = fields.shape[0]
     copies = [
@@ -138,10 +134,7 @@
     for copy in copies:
         copy.start()
 
-    @pl.when(lax.axis_index("gy") != 0)
-    def _():
-        own_strips(fields, noise, ownrow, owncol)
-
+    own_strips(fields, noise, ownrow, owncol)
     interior(total_y, fields, noise, inner, tmp)
     for copy in copies:
         copy.wait()
@@ -292,18 +285,16 @@
     members = fields.shape[0]
     devices = lax.axis_size("mem")
     total_y = T * lax.axis_size("gy")
-    fields_vm, noise_vm, rowpack, colpack, ownrow, owncol = pl.pallas_call(
+    fields_vm, noise_vm, rowpack, colpack = pl.pallas_call(
         pack_kernel,
         out_shape=(
             sds(*fields.shape),
             sds(*noise.shape),
             sds(3 * members + members // 2, 8, T),
             sds(T, T),
-            sds(4, 2 * members, 8, T),
-            sds(4, T, T),
         ),
         in_specs=[HB] * 2,
-        out_specs=[VM] * 6,
+        out_specs=[VM] * 4,
         scratch_shapes=[pltpu.SemaphoreType.DMA((members + 1,))],
         compiler_params=PARAMS,
         name="pack",
@@ -323,9 +314,8 @@
             sds(1, count),
             jax.ShapeDtypeStruct((1, pairs), jnp.int32),
         ),
-        in_specs=[VM] * 4 + [HB] * 3,
+        in_specs=[VM] * 2 + [HB] * 3,
         out_specs=[VM] * 7,
-        input_output_aliases={2: 0, 3: 1},
         scratch_shapes=[
             pltpu.VMEM((members, 3, T, T), F32),
             pltpu.VMEM((1, count), jnp.int32),
@@ -337,8 +327,6 @@
     )(
         fields_vm,
         noise_vm,
-        ownrow,
-        owncol,
         in_hbm(obs_cells.reshape(1, -1)),
         in_hbm(obs_values.reshape(1, -1)),
         in_hbm(ancestors.reshape(1, -1)),

time: 52.5 us -> 52.3 us (level)
  starting transfers between devices: 3.65 us -> 4.63 us
    all_to_all x1, blocking collectives: 23.1 us -> 22.3 us  [shards(): lax.all_to_all(pieces.reshape(devices, stride, 1, T), 'mem', 0, 0)]
    pallas_call x1, Pallas kernels: 2.17 us -> 1.56 us  [shards(): pl.pallas_call(pack_kernel, out_shape=(sds(*fields.shape), sds(*noise.sha...]
    ppermute x1, starting transfers between devices: 3.43 us -> 4.04 us  [shards(): colrecv = lax.ppermute(colpack, 'gy', swap)]
    pallas_call x1, Pallas kernels: 2.02 us -> 2.57 us  [shards(): pl.pallas_call(functools.partial(interior_kernel, total_y), out_shape=(sd...]
  transfers between devices with their start and end apart: 3 -> 3, of which waited for: 2 -> 0; matrix products, arithmetic and copies ran while one was open for 0% -> 0% of each run, Pallas kernels for 6% -> 7%
where the time goes in v12:
time: 52.3 us; the launch traced here: 52.1 us
  blocking collectives  39.6 us (76%)
  Pallas kernels  7.12 us (14%)
  starting transfers between devices  4.63 us (9%)
  between operations  0.69 us (1%)
    all_to_all x1, blocking collectives, shards(): lax.all_to_all(pieces.reshape(devices, stride, 1, T), 'mem', 0, 0)  22.3 us
    all_to_all x1, blocking collectives, shards(): lax.all_to_all(picked.reshape(devices, members // 2, rows, T), 'mem', 0, 0)  17.2 us
    ppermute x1, starting transfers between devices, shards(): colrecv = lax.ppermute(colpack, 'gy', swap)  4.04 us
    pallas_call x1, Pallas kernels, shards(): pl.pallas_call(functools.partial(interior_kernel, total_y), out_shape=(sd...  2.57 us
    pallas_call x1, Pallas kernels, shards(): pl.pallas_call(pack_kernel, out_shape=(sds(*fields.shape), sds(*noise.sha...  1.56 us
  transfers between devices with their start and end apart: 3, of which 0 were waited for; matrix products, arithmetic and copies ran while one was open for 0% of the time, Pallas kernels for 7%

profile of v12, /device:TPU:0, one launch (start us, length us, event | category | flops | bytes accessed | tf_op | source)
XLA Modules:
  0.0 52.1 jit_solution(9616171206225676048)
XLA Ops:
  0.6 1.6 %pack.1 = (f32[4,3,128,128]{3,2,1,0:T(8,128)S(1)}, f32[2,128,128]{2,1,0:T(8,128)S(1)}, f32[14,8,128]{2,1,0:T(8,128)S(1)}, f32[128,128]{1,0:T(8,128)S(1)}) custom-call(f32[4,3,128,128]{3,2,1,0:T(8,128)} %fields_hbm.1, f32[2,128,128]{2,1,0:T(8,128)} %noise_hbm.1), custom_call_target="tpu_custom_call" | custom-call | tf_op jit(solution)/shard_map/pack/pallas_call | solution.py:288
  2.2 4.0 %collective-permute-start = (f32[128,128]{1,0:T(8,128)S(1)}, f32[128,128]{1,0:T(8,128)S(1)}, u32[]{:S(2)}, u32[]{:S(2)}) collective-permute-start(f32[128,128]{1,0:T(8,128)S(1)} %get-tuple-element.25), channel_id=1, source_target_pairs={{0,1},{1,0},{2,3},{3,2},{4,5},{5,4},{6,7},{7,6},{8,9},{9,8},{10,11... | collective-permute-start | bytes 196616 | tf_op jit(solution)/shard_map/ppermute | solution.py:303
  6.2 0.0 collective-permute-start.1
  6.2 2.6 %interior.1 = (f32[4,8,8,128]{3,2,1,0:T(8,128)S(1)}, f32[4,128,128]{2,1,0:T(8,128)S(1)}, f32[4,3,128,128]{3,2,1,0:T(8,128)S(1)}, bf16[128,256]{1,0:T(8,128)(2,1)...) custom-call(f32[4,3,128,128]{3,2,1,0:T(8,128)S(1)} %get-tuple-element.22.fields, ...), custom_call_target="tpu_custom_call" | custom-call | flops 50000000 | bytes 2500000 | tf_op jit(solution)/shard_map/interior/pallas_call | solution.py:306
  8.8 0.0 collective-permute-done.1.rowrecv
  8.8 0.0 collective-permute-done.colrecv
  8.8 0.6 %collective-permute-start.2 = (f32[128,128]{1,0:T(8,128)S(1)}, f32[128,128]{1,0:T(8,128)S(1)}, u32[]{:S(2)}, u32[]{:S(2)}) collective-permute-start(f32[128,128]{1,0:T(8,128)S(1)} %collective-permute-done.colrecv), channel_id=1, source_target_pairs={{0,2},{2,0},{1,3},{3,1},{4,6},{6,4},{5,7},{7,5},{8,10},{10,8},{9,1... | collective-permute-start | bytes 196616 | tf_op jit(solution)/shard_map/ppermute | solution.py:335
  9.4 0.8 %strips.1 = (f32[3,8,8,128]{3,2,1,0:T(8,128)S(1)}, f32[4,144,128]{2,1,0:T(8,128)S(1)}, f32[3,144,128]{2,1,0:T(8,128)S(1)}) custom-call(f32[4,8,8,128]{3,2,1,0:T(8,128)S(1)} %get-tuple-element.29.ownrow, f32[14,8,128]{2,1,0:T(8,128)S(1)} %collective-permute-done.1.rowrecv, f32[4,128,128]{2,1,0:T(8,128)S(1)} %get-tuple-element.31.owncol, ...), custom_call_target="tpu_custom_call" | custom-call | flops 18000000 | bytes 700000 | tf_op jit(solution)/shard_map/strips/pallas_call | solution.py:336
  10.3 0.0 collective-permute-done.2.cornrecv
  10.3 0.9 %merge.1 = (f32[4,144,128]{2,1,0:T(8,128)S(1)}, f32[3,144,128]{2,1,0:T(8,128)S(1)}, f32[1568,128]{1,0:T(8,128)S(1)}) custom-call(f32[4,3,128,128]{3,2,1,0:T(8,128)S(1)} %get-tuple-element.28.inner, f32[3,8,8,128]{3,2,1,0:T(8,128)S(1)} %get-tuple-element.33.edge, ...), custom_call_target="tpu_custom_call", output_to_operand_aliasing={{0}: (2, {}), {1}: (3, {})} | custom-call | tf_op jit(solution)/shard_map/merge/pallas_call | solution.py:348
  11.2 22.3 %all_to_all.10 = f32[32,49,1,128]{3,2,1,0:T(1,128)S(1)} all-to-all(f32[32,49,1,128]{3,2,1,0:T(1,128)S(1)} %bitcast.10), channel_id=1, replica_groups=mesh['mem'=32,'gx'=2,'gy'=2] {'mem'}, dimensions={0} | all-to-all | bytes 1605632 | tf_op jit(solution)/shard_map/all_to_all | solution.py:358
  33.6 0.3 select.1
  33.9 17.2 %all_to_all.11.back = f32[32,2,24,128]{3,2,1,0:T(8,128)S(1)} all-to-all(f32[32,2,24,128]{3,2,1,0:T(8,128)S(1)} %bitcast.9), channel_id=1, replica_groups=mesh['mem'=32,'gx'=2,'gy'=2] {'mem'}, dimensions={0} | all-to-all | bytes 1572864 | tf_op jit(solution)/shard_map/all_to_all | solution.py:367
  51.1 0.9 %finish.1 = (f32[2,32,24,128]{3,2,1,0:T(8,128)}, f32[1,1,4]{2,1,0:T(1,128)}) custom-call(f32[32,2,24,128]{3,2,1,0:T(8,128)S(1)} %all_to_all.11.back, f32[1568,128]{1,0:T(8,128)S(1)} %bitcast.8), custom_call_target="tpu_custom_call" | custom-call | tf_op jit(solution)/shard_map/finish/pallas_call | solution.py:368
Async XLA Ops:
  2.2 6.6 %collective-permute-start = (f32[128,128]{1,0:T(8,128)S(1)}, f32[128,128]{1,0:T(8,128)S(1)}, u32[]{:S(2)}, u32[]{:S(2)}) collective-permute-start(f32[128,128]{1,0:T(8,128)S(1)} %get-tuple-element.25), channel_id=1, source_target_pairs={{0,1},{1,0},{2,3},{3,2},{4,5},{5,4},{6,7},{7,6},{8,9},{9,8},{10,11... | collective-permute-start | bytes 196616 | tf_op jit(solution)/shard_map/ppermute | solution.py:303
  6.2 2.6 %collective-permute-start.1 = (f32[14,8,128]{2,1,0:T(8,128)S(1)}, f32[14,8,128]{2,1,0:T(8,128)S(1)}, u32[]{:S(2)}, u32[]{:S(2)}) collective-permute-start(f32[14,8,128]{2,1,0:T(8,128)S(1)} %get-tuple-element.26), channel_id=1, source_target_pairs={{0,2},{2,0},{1,3},{3,1},{4,6},{6,4},{5,7},{7,5},{8,10},{10,8},{9,1... | collective-permute-start | bytes 172040 | tf_op jit(solution)/shard_map/ppermute | solution.py:304
  8.8 1.5 %collective-permute-start.2 = (f32[128,128]{1,0:T(8,128)S(1)}, f32[128,128]{1,0:T(8,128)S(1)}, u32[]{:S(2)}, u32[]{:S(2)}) collective-permute-start(f32[128,128]{1,0:T(8,128)S(1)} %collective-permute-done.colrecv), channel_id=1, source_target_pairs={{0,2},{2,0},{1,3},{3,1},{4,6},{6,4},{5,7},{7,5},{8,10},{10,8},{9,1... | collective-permute-start | bytes 196616 | tf_op jit(solution)/shard_map/ppermute | solution.py:335

commit v13 on v12

--- a/solution.py
+++ b/solution.py
@@ -72,9 +72,11 @@
 
 def pack_kernel(fields_hbm, noise_hbm, fields, noise, rowpack, colpack, sems):
     members = fields.shape[0]
-    copies = [pltpu.make_async_copy(noise_hbm, noise, sems.at[members])]
-    for m in range(members):
-        copies.append(pltpu.make_async_copy(fields_hbm.at[m], fields.at[m], sems.at[m]))
+    half = members // 2
+    copies = [pltpu.make_async_copy(noise_hbm, noise, sems.at[2])]
+    for i in range(2):
+        part = slice(i * half, (i + 1) * half)
+        copies.append(pltpu.make_async_copy(fields_hbm.at[part], fields.at[part], sems.at[i]))
     for copy in copies:
         copy.start()
     copies[0].wait()
@@ -86,18 +88,20 @@
     for m in range(members):
         acc = jnp.where(ln == 4 * m + 3, lroll(noise[m // 2], 32 * m + 28), acc)
     for m in range(members):
-        copies[1 + m].wait()
+        if m % half == 0:
+            copies[1 + m // half].wait()
         for f in range(3):
             rowpack[3 * m + f] = jnp.where(top, fields[m, f, 0:8], fields[m, f, T - 8 : T])
             acc = jnp.where(ln == 4 * m + f, lroll(fields[m, f], 32 * m + 8 * f + 4), acc)
     colpack[...] = acc
 
 
-def own_columns(tiles):
+def own_columns(tiles, every=1):
     shape = tiles[0].shape
     ln = lanes(shape) // 8
     acc = jnp.zeros(shape, F32)
-    for m, a in enumerate(tiles):
+    for m in range(0, len(tiles), every):
+        a = tiles[m]
         acc = jnp.where(ln == 4 * m, lroll(a, 32 * m + 8), acc)
         acc = jnp.where(ln == 4 * m + 3, lroll(a, 32 * m + 24), acc)
     return acc
@@ -110,7 +114,11 @@
         for m, a in enumerate(tiles):
             ownrow[f, 2 * m] = a[0:8]
             ownrow[f, 2 * m + 1] = a[T - 8 : T]
-        owncol[f] = own_columns(tiles)
+        if f < 3:
+            owncol[f] = own_columns(tiles)
+        else:
+            even = own_columns(tiles, 2)
+            owncol[f] = even + lroll(even, 32)
 
 
 def interior(total_y, fields, noise, inner, tmp):
@@ -295,7 +303,7 @@
         ),
         in_specs=[HB] * 2,
         out_specs=[VM] * 4,
-        scratch_shapes=[pltpu.SemaphoreType.DMA((members + 1,))],
+        scratch_shapes=[pltpu.SemaphoreType.DMA((3,))],
         compiler_params=PARAMS,
         name="pack",
     )(in_hbm(fields), in_hbm(noise))

time: 52.3 us -> 52.1 us (level)
  no operation moved by 1% of the time
where the time goes in v13:
time: 52.1 us; the launch traced here: 51.9 us
  blocking collectives  39.6 us (76%)
  Pallas kernels  7 us (13%)
  starting transfers between devices  4.63 us (9%)
  between operations  0.69 us (1%)
    all_to_all x1, blocking collectives, shards(): lax.all_to_all(pieces.reshape(devices, stride, 1, T), 'mem', 0, 0)  22.3 us
    all_to_all x1, blocking collectives, shards(): lax.all_to_all(picked.reshape(devices, members // 2, rows, T), 'mem', 0, 0)  17.2 us
    ppermute x1, starting transfers between devices, shards(): colrecv = lax.ppermute(colpack, 'gy', swap)  4.04 us
    pallas_call x1, Pallas kernels, shards(): pl.pallas_call(functools.partial(interior_kernel, total_y), out_shape=(sd...  2.58 us
    pallas_call x1, Pallas kernels, shards(): pl.pallas_call(pack_kernel, out_shape=(sds(*fields.shape), sds(*noise.sha...  1.43 us
  transfers between devices with their start and end apart: 3, of which 0 were waited for; matrix products, arithmetic and copies ran while one was open for 0% of the time, Pallas kernels for 7%

profile of v13, /device:TPU:0, one launch (start us, length us, event | category | flops | bytes accessed | tf_op | source)
XLA Modules:
  0.0 51.9 jit_solution(6440299659171633416)
XLA Ops:
  0.6 1.4 %pack.1 = (f32[4,3,128,128]{3,2,1,0:T(8,128)S(1)}, f32[2,128,128]{2,1,0:T(8,128)S(1)}, f32[14,8,128]{2,1,0:T(8,128)S(1)}, f32[128,128]{1,0:T(8,128)S(1)}) custom-call(f32[4,3,128,128]{3,2,1,0:T(8,128)} %fields_hbm.1, f32[2,128,128]{2,1,0:T(8,128)} %noise_hbm.1), custom_call_target="tpu_custom_call" | custom-call | tf_op jit(solution)/shard_map/pack/pallas_call | solution.py:296
  2.1 4.0 %collective-permute-start = (f32[128,128]{1,0:T(8,128)S(1)}, f32[128,128]{1,0:T(8,128)S(1)}, u32[]{:S(2)}, u32[]{:S(2)}) collective-permute-start(f32[128,128]{1,0:T(8,128)S(1)} %get-tuple-element.25), channel_id=1, source_target_pairs={{0,1},{1,0},{2,3},{3,2},{4,5},{5,4},{6,7},{7,6},{8,9},{9,8},{10,11... | collective-permute-start | bytes 196616 | tf_op jit(solution)/shard_map/ppermute | solution.py:311
  6.1 0.0 collective-permute-start.1
  6.1 2.6 %interior.1 = (f32[4,8,8,128]{3,2,1,0:T(8,128)S(1)}, f32[4,128,128]{2,1,0:T(8,128)S(1)}, f32[4,3,128,128]{3,2,1,0:T(8,128)S(1)}, bf16[128,256]{1,0:T(8,128)(2,1)...) custom-call(f32[4,3,128,128]{3,2,1,0:T(8,128)S(1)} %get-tuple-element.22.fields, ...), custom_call_target="tpu_custom_call" | custom-call | flops 50000000 | bytes 2500000 | tf_op jit(solution)/shard_map/interior/pallas_call | solution.py:314
  8.7 0.0 collective-permute-done.1.rowrecv
  8.7 0.0 collective-permute-done.colrecv
  8.7 0.6 %collective-permute-start.2 = (f32[128,128]{1,0:T(8,128)S(1)}, f32[128,128]{1,0:T(8,128)S(1)}, u32[]{:S(2)}, u32[]{:S(2)}) collective-permute-start(f32[128,128]{1,0:T(8,128)S(1)} %collective-permute-done.colrecv), channel_id=1, source_target_pairs={{0,2},{2,0},{1,3},{3,1},{4,6},{6,4},{5,7},{7,5},{8,10},{10,8},{9,1... | collective-permute-start | bytes 196616 | tf_op jit(solution)/shard_map/ppermute | solution.py:343
  9.3 0.8 %strips.1 = (f32[3,8,8,128]{3,2,1,0:T(8,128)S(1)}, f32[4,144,128]{2,1,0:T(8,128)S(1)}, f32[3,144,128]{2,1,0:T(8,128)S(1)}) custom-call(f32[4,8,8,128]{3,2,1,0:T(8,128)S(1)} %get-tuple-element.29.ownrow, f32[14,8,128]{2,1,0:T(8,128)S(1)} %collective-permute-done.1.rowrecv, f32[4,128,128]{2,1,0:T(8,128)S(1)} %get-tuple-element.31.owncol, ...), custom_call_target="tpu_custom_call" | custom-call | flops 18000000 | bytes 700000 | tf_op jit(solution)/shard_map/strips/pallas_call | solution.py:344
  10.2 0.0 collective-permute-done.2.cornrecv
  10.2 0.9 %merge.1 = (f32[4,144,128]{2,1,0:T(8,128)S(1)}, f32[3,144,128]{2,1,0:T(8,128)S(1)}, f32[1568,128]{1,0:T(8,128)S(1)}) custom-call(f32[4,3,128,128]{3,2,1,0:T(8,128)S(1)} %get-tuple-element.28.inner, f32[3,8,8,128]{3,2,1,0:T(8,128)S(1)} %get-tuple-element.33.edge, ...), custom_call_target="tpu_custom_call", output_to_operand_aliasing={{0}: (2, {}), {1}: (3, {})} | custom-call | tf_op jit(solution)/shard_map/merge/pallas_call | solution.py:356
  11.1 22.3 %all_to_all.10 = f32[32,49,1,128]{3,2,1,0:T(1,128)S(1)} all-to-all(f32[32,49,1,128]{3,2,1,0:T(1,128)S(1)} %bitcast.10), channel_id=1, replica_groups=mesh['mem'=32,'gx'=2,'gy'=2] {'mem'}, dimensions={0} | all-to-all | bytes 1605632 | tf_op jit(solution)/shard_map/all_to_all | solution.py:366
  33.5 0.3 select.1
  33.8 17.2 %all_to_all.11.back = f32[32,2,24,128]{3,2,1,0:T(8,128)S(1)} all-to-all(f32[32,2,24,128]{3,2,1,0:T(8,128)S(1)} %bitcast.9), channel_id=1, replica_groups=mesh['mem'=32,'gx'=2,'gy'=2] {'mem'}, dimensions={0} | all-to-all | bytes 1572864 | tf_op jit(solution)/shard_map/all_to_all | solution.py:375
  51.0 0.9 %finish.1 = (f32[2,32,24,128]{3,2,1,0:T(8,128)}, f32[1,1,4]{2,1,0:T(1,128)}) custom-call(f32[32,2,24,128]{3,2,1,0:T(8,128)S(1)} %all_to_all.11.back, f32[1568,128]{1,0:T(8,128)S(1)} %bitcast.8), custom_call_target="tpu_custom_call" | custom-call | tf_op jit(solution)/shard_map/finish/pallas_call | solution.py:376
Async XLA Ops:
  2.1 6.6 %collective-permute-start = (f32[128,128]{1,0:T(8,128)S(1)}, f32[128,128]{1,0:T(8,128)S(1)}, u32[]{:S(2)}, u32[]{:S(2)}) collective-permute-start(f32[128,128]{1,0:T(8,128)S(1)} %get-tuple-element.25), channel_id=1, source_target_pairs={{0,1},{1,0},{2,3},{3,2},{4,5},{5,4},{6,7},{7,6},{8,9},{9,8},{10,11... | collective-permute-start | bytes 196616 | tf_op jit(solution)/shard_map/ppermute | solution.py:311
  6.1 2.6 %collective-permute-start.1 = (f32[14,8,128]{2,1,0:T(8,128)S(1)}, f32[14,8,128]{2,1,0:T(8,128)S(1)}, u32[]{:S(2)}, u32[]{:S(2)}) collective-permute-start(f32[14,8,128]{2,1,0:T(8,128)S(1)} %get-tuple-element.26), channel_id=1, source_target_pairs={{0,2},{2,0},{1,3},{3,1},{4,6},{6,4},{5,7},{7,5},{8,10},{10,8},{9,1... | collective-permute-start | bytes 172040 | tf_op jit(solution)/shard_map/ppermute | solution.py:312
  8.7 1.5 %collective-permute-start.2 = (f32[128,128]{1,0:T(8,128)S(1)}, f32[128,128]{1,0:T(8,128)S(1)}, u32[]{:S(2)}, u32[]{:S(2)}) collective-permute-start(f32[128,128]{1,0:T(8,128)S(1)} %collective-permute-done.colrecv), channel_id=1, source_target_pairs={{0,2},{2,0},{1,3},{3,1},{4,6},{6,4},{5,7},{7,5},{8,10},{10,8},{9,1... | collective-permute-start | bytes 196616 | tf_op jit(solution)/shard_map/ppermute | solution.py:343

commit v14 on v13

--- a/solution.py
+++ b/solution.py
@@ -70,7 +70,7 @@
     return 0.1 + 0.2 * ((y.astype(F32) + 0.5) / total_y - 0.5)
 
 
-def pack_kernel(fields_hbm, noise_hbm, fields, noise, rowpack, colpack, sems):
+def pack_kernel(fields_hbm, noise_hbm, fields, noise, rowpack, colpack, ownrow, owncol, sems):
     members = fields.shape[0]
     half = members // 2
     copies = [pltpu.make_async_copy(noise_hbm, noise, sems.at[2])]
@@ -95,6 +95,14 @@
             acc = jnp.where(ln == 4 * m + f, lroll(fields[m, f], 32 * m + 8 * f + 4), acc)
     colpack[...] = acc
 
+    @pl.when(strips_first())
+    def _():
+        own_strips(fields, noise, ownrow, owncol)
+
+
+def strips_first():
+    return (lax.axis_index("gx") != 0) & (lax.axis_index("gy") == 0)
+
 
 def own_columns(tiles, every=1):
     shape = tiles[0].shape
@@ -131,7 +139,7 @@
                     dst[m, f, r : r + CHUNK] = new[f]
 
 
-def interior_kernel(total_y, fields, noise, cells_hbm, values_hbm, lineage_hbm,
+def interior_kernel(total_y, fields, noise, ownrow_in, owncol_in, cells_hbm, values_hbm, lineage_hbm,
                     ownrow, owncol, inner, pick_y, cell_x, values, lineage, tmp, cells, sems):
     members = fields.shape[0]
     copies = [
@@ -142,7 +150,10 @@
     for copy in copies:
         copy.start()
 
-    own_strips(fields, noise, ownrow, owncol)
+    @pl.when(jnp.logical_not(strips_first()))
+    def _():
+        own_strips(fields, noise, ownrow, owncol)
+
     interior(total_y, fields, noise, inner, tmp)
     for copy in copies:
         copy.wait()
@@ -293,16 +304,18 @@
     members = fields.shape[0]
     devices = lax.axis_size("mem")
     total_y = T * lax.axis_size("gy")
-    fields_vm, noise_vm, rowpack, colpack = pl.pallas_call(
+    fields_vm, noise_vm, rowpack, colpack, ownrow, owncol = pl.pallas_call(
         pack_kernel,
         out_shape=(
             sds(*fields.shape),
             sds(*noise.shape),
             sds(3 * members + members // 2, 8, T),
             sds(T, T),
+            sds(4, 2 * members, 8, T),
+            sds(4, T, T),
         ),
         in_specs=[HB] * 2,
-        out_specs=[VM] * 4,
+        out_specs=[VM] * 6,
         scratch_shapes=[pltpu.SemaphoreType.DMA((3,))],
         compiler_params=PARAMS,
         name="pack",
@@ -322,8 +335,9 @@
             sds(1, count),
             jax.ShapeDtypeStruct((1, pairs), jnp.int32),
         ),
-        in_specs=[VM] * 2 + [HB] * 3,
+        in_specs=[VM] * 4 + [HB] * 3,
         out_specs=[VM] * 7,
+        input_output_aliases={2: 0, 3: 1},
         scratch_shapes=[
             pltpu.VMEM((members, 3, T, T), F32),
             pltpu.VMEM((1, count), jnp.int32),
@@ -335,6 +349,8 @@
     )(
         fields_vm,
         noise_vm,
+        ownrow,
+        owncol,
         in_hbm(obs_cells.reshape(1, -1)),
         in_hbm(obs_values.reshape(1, -1)),
         in_hbm(ancestors.reshape(1, -1)),

time: 52.1 us -> 51.9 us (level)
  transfers between devices with their start and end apart: 3 -> 3, of which waited for: 0 -> 1; matrix products, arithmetic and copies ran while one was open for 0% -> 0% of each run, Pallas kernels for 7% -> 7%
where the time goes in v14:
time: 51.9 us; the launch traced here: 51.7 us
  blocking collectives  39.4 us (76%)
  Pallas kernels  7.13 us (14%)
  starting transfers between devices  4.13 us (8%)
  between operations  0.69 us (1%)
    all_to_all x1, blocking collectives, shards(): lax.all_to_all(pieces.reshape(devices, stride, 1, T), 'mem', 0, 0)  22.4 us
    all_to_all x1, blocking collectives, shards(): lax.all_to_all(picked.reshape(devices, members // 2, rows, T), 'mem', 0, 0)  17 us
    ppermute x1, starting transfers between devices, shards(): colrecv = lax.ppermute(colpack, 'gy', swap)  4.04 us
    pallas_call x1, Pallas kernels, shards(): pl.pallas_call(functools.partial(interior_kernel, total_y), out_shape=(sd...  2.62 us
    pallas_call x1, Pallas kernels, shards(): pl.pallas_call(pack_kernel, out_shape=(sds(*fields.shape), sds(*noise.sha...  1.43 us
  transfers between devices with their start and end apart: 3, of which 1 were waited for; matrix products, arithmetic and copies ran while one was open for 0% of the time, Pallas kernels for 7%

profile of v14, /device:TPU:0, one launch (start us, length us, event | category | flops | bytes accessed | tf_op | source)
XLA Modules:
  0.0 51.7 jit_solution(16340995189490890378)
XLA Ops:
  0.6 1.4 %pack.1 = (f32[4,3,128,128]{3,2,1,0:T(8,128)S(1)}, f32[2,128,128]{2,1,0:T(8,128)S(1)}, f32[14,8,128]{2,1,0:T(8,128)S(1)}, f32[128,128]{1,0:T(8,128)S(1)}, f32[4,...) custom-call(f32[4,3,128,128]{3,2,1,0:T(8,128)} %fields_hbm.1, f32[2,128,128]{2,1,0:T(8,128)} %noise_hbm.1), custom_call_target="tpu_custom_call" | custom-call | tf_op jit(solution)/shard_map/pack/pallas_call | solution.py:307
  2.1 4.0 %collective-permute-start = (f32[128,128]{1,0:T(8,128)S(1)}, f32[128,128]{1,0:T(8,128)S(1)}, u32[]{:S(2)}, u32[]{:S(2)}) collective-permute-start(f32[128,128]{1,0:T(8,128)S(1)} %get-tuple-element.29), channel_id=1, source_target_pairs={{0,1},{1,0},{2,3},{3,2},{4,5},{5,4},{6,7},{7,6},{8,9},{9,8},{10,11... | collective-permute-start | bytes 196616 | tf_op jit(solution)/shard_map/ppermute | solution.py:324
  6.1 0.0 collective-permute-start.1
  6.1 2.6 %interior.1 = (f32[4,8,8,128]{3,2,1,0:T(8,128)S(1)}, f32[4,128,128]{2,1,0:T(8,128)S(1)}, f32[4,3,128,128]{3,2,1,0:T(8,128)S(1)}, bf16[128,256]{1,0:T(8,128)(2,1)...) custom-call(f32[4,3,128,128]{3,2,1,0:T(8,128)S(1)} %get-tuple-elemen, ...), custom_call_target="tpu_custom_call", output_to_operand_aliasing={{0}: (2, {}), {1}: (3, {})} | custom-call | flops 50000000 | bytes 2500000 | tf_op jit(solution)/shard_map/interior/pallas_call | solution.py:327
  8.7 0.0 collective-permute-done.1.rowrecv
  8.8 0.0 collective-permute-done.colrecv
  8.8 0.1 collective-permute-start.2
  8.9 0.9 %strips.1 = (f32[3,8,8,128]{3,2,1,0:T(8,128)S(1)}, f32[4,144,128]{2,1,0:T(8,128)S(1)}, f32[3,144,128]{2,1,0:T(8,128)S(1)}) custom-call(f32[4,8,8,128]{3,2,1,0:T(8,128)S(1)} %get-tuple-element.33.ownrow, f32[14,8,128]{2,1,0:T(8,128)S(1)} %collective-permute-done.1.rowrecv, f32[4,128,128]{2,1,0:T(8,128)S(1)} %get-tuple-element.35.owncol, ...), custom_call_target="tpu_custom_call" | custom-call | flops 18000000 | bytes 700000 | tf_op jit(solution)/shard_map/strips/pallas_call | solution.py:360
  9.7 0.4 collective-permute-done.2.cornrecv
  10.1 1.0 %merge.1 = (f32[4,144,128]{2,1,0:T(8,128)S(1)}, f32[3,144,128]{2,1,0:T(8,128)S(1)}, f32[1568,128]{1,0:T(8,128)S(1)}) custom-call(f32[4,3,128,128]{3,2,1,0:T(8,128)S(1)} %get-tuple-element.32.inner, f32[3,8,8,128]{3,2,1,0:T(8,128)S(1)} %get-tuple-element.37.edge, ...), custom_call_target="tpu_custom_call", output_to_operand_aliasing={{0}: (2, {}), {1}: (3, {})} | custom-call | tf_op jit(solution)/shard_map/merge/pallas_call | solution.py:372
  11.1 22.4 %all_to_all.10 = f32[32,49,1,128]{3,2,1,0:T(1,128)S(1)} all-to-all(f32[32,49,1,128]{3,2,1,0:T(1,128)S(1)} %bitcast.10), channel_id=1, replica_groups=mesh['mem'=32,'gx'=2,'gy'=2] {'mem'}, dimensions={0} | all-to-all | bytes 1605632 | tf_op jit(solution)/shard_map/all_to_all | solution.py:382
  33.4 0.3 select.1
  33.8 17.0 %all_to_all.11.back = f32[32,2,24,128]{3,2,1,0:T(8,128)S(1)} all-to-all(f32[32,2,24,128]{3,2,1,0:T(8,128)S(1)} %bitcast.9), channel_id=1, replica_groups=mesh['mem'=32,'gx'=2,'gy'=2] {'mem'}, dimensions={0} | all-to-all | bytes 1572864 | tf_op jit(solution)/shard_map/all_to_all | solution.py:391
  50.8 0.9 %finish.1 = (f32[2,32,24,128]{3,2,1,0:T(8,128)}, f32[1,1,4]{2,1,0:T(1,128)}) custom-call(f32[32,2,24,128]{3,2,1,0:T(8,128)S(1)} %all_to_all.11.back, f32[1568,128]{1,0:T(8,128)S(1)} %bitcast.8), custom_call_target="tpu_custom_call" | custom-call | tf_op jit(solution)/shard_map/finish/pallas_call | solution.py:392
Async XLA Ops:
  2.1 6.7 %collective-permute-start = (f32[128,128]{1,0:T(8,128)S(1)}, f32[128,128]{1,0:T(8,128)S(1)}, u32[]{:S(2)}, u32[]{:S(2)}) collective-permute-start(f32[128,128]{1,0:T(8,128)S(1)} %get-tuple-element.29), channel_id=1, source_target_pairs={{0,1},{1,0},{2,3},{3,2},{4,5},{5,4},{6,7},{7,6},{8,9},{9,8},{10,11... | collective-permute-start | bytes 196616 | tf_op jit(solution)/shard_map/ppermute | solution.py:324
  6.1 2.6 %collective-permute-start.1 = (f32[14,8,128]{2,1,0:T(8,128)S(1)}, f32[14,8,128]{2,1,0:T(8,128)S(1)}, u32[]{:S(2)}, u32[]{:S(2)}) collective-permute-start(f32[14,8,128]{2,1,0:T(8,128)S(1)} %get-tuple-element.30), channel_id=1, source_target_pairs={{0,2},{2,0},{1,3},{3,1},{4,6},{6,4},{5,7},{7,5},{8,10},{10,8},{9,1... | collective-permute-start | bytes 172040 | tf_op jit(solution)/shard_map/ppermute | solution.py:325
  8.8 1.3 %collective-permute-start.2 = (f32[128,128]{1,0:T(8,128)S(1)}, f32[128,128]{1,0:T(8,128)S(1)}, u32[]{:S(2)}, u32[]{:S(2)}) collective-permute-start(f32[128,128]{1,0:T(8,128)S(1)} %collective-permute-done.colrecv), channel_id=1, source_target_pairs={{0,2},{2,0},{1,3},{3,1},{4,6},{6,4},{5,7},{7,5},{8,10},{10,8},{9,1... | collective-permute-start | bytes 196616 | tf_op jit(solution)/shard_map/ppermute | solution.py:359

commit v15 on v14

--- a/solution.py
+++ b/solution.py
@@ -106,13 +106,11 @@
 
 def own_columns(tiles, every=1):
     shape = tiles[0].shape
-    ln = lanes(shape) // 8
+    lane = lanes(shape)
     acc = jnp.zeros(shape, F32)
     for m in range(0, len(tiles), every):
-        a = tiles[m]
-        acc = jnp.where(ln == 4 * m, lroll(a, 32 * m + 8), acc)
-        acc = jnp.where(ln == 4 * m + 3, lroll(a, 32 * m + 24), acc)
-    return acc
+        acc = jnp.where(lane // 32 == m, lroll(tiles[m], 32 * m + 24), acc)
+    return jnp.where(lane % 32 < 8, lroll(acc, -16), acc)
 
 
 def own_strips(fields, noise, ownrow, owncol):
@@ -222,20 +220,21 @@
     per = 96 // devices
     stride = members // 2 * 8 * per + 1
     top = subl((8, T)) < 4
-    left = lanes((8, T)) < 4
-    right = lanes((8, T)) >= T - 4
-    for m in range(members):
-        p, mm = m // 2, m % 2
-        for f in range(3):
-            for t in range(T // 8):
+    lane = lanes((8, T))
+    moved = (lane % 32 >= 20) & (lane % 32 < 24)
+    outer = (lane < 4) | (lane >= T - 4)
+    for f in range(3):
+        for t in range(T // 8):
+            col = cs[f, 8 * t + 8 : 8 * t + 16]
+            col = jnp.where(moved, lroll(col, 16), col)
+            for m in range(members):
+                p, mm = m // 2, m % 2
                 a = inner[m, f, 8 * t : 8 * t + 8]
                 if t == 0:
                     a = jnp.where(top, edge[f, 2 * m], a)
                 if t == T // 8 - 1:
                     a = jnp.where(top, a, edge[f, 2 * m + 1])
-                col = cs[f, 8 * t + 8 : 8 * t + 16]
-                a = jnp.where(left, lroll(col, 104 - 32 * m), a)
-                a = jnp.where(right, lroll(col, 120 - 32 * m), a)
+                a = jnp.where(outer, lroll(col, 104 - 32 * m), a)
                 k = mm * 48 + f * 16 + t
                 first = (k // per) * stride + p * 8 * per + 8 * (k % per)
                 out[first : first + 8] = a

time: 51.9 us -> 53.9 us (1.039)
  Pallas kernels: 7.13 us -> 8.93 us
    pallas_call x1, Pallas kernels: 0.96 us -> 2.61 us  [shards(): pl.pallas_call(functools.partial(merge_kernel, total_y, devices), out_sha...]
where the time goes in v15:
time: 53.9 us; the launch traced here: 53.7 us
  blocking collectives  39.8 us (74%)
  Pallas kernels  8.93 us (17%)
  starting transfers between devices  4.13 us (8%)
  between operations  0.69 us (1%)
    all_to_all x1, blocking collectives, shards(): lax.all_to_all(pieces.reshape(devices, stride, 1, T), 'mem', 0, 0)  22.6 us
    all_to_all x1, blocking collectives, shards(): lax.all_to_all(picked.reshape(devices, members // 2, rows, T), 'mem', 0, 0)  17.2 us
    ppermute x1, starting transfers between devices, shards(): colrecv = lax.ppermute(colpack, 'gy', swap)  4.04 us
    pallas_call x1, Pallas kernels, shards(): pl.pallas_call(functools.partial(merge_kernel, total_y, devices), out_sha...  2.61 us
    pallas_call x1, Pallas kernels, shards(): pl.pallas_call(functools.partial(interior_kernel, total_y), out_shape=(sd...  2.59 us
    pallas_call x1, Pallas kernels, shards(): pl.pallas_call(pack_kernel, out_shape=(sds(*fields.shape), sds(*noise.sha...  1.43 us
  transfers between devices with their start and end apart: 3, of which 1 were waited for; matrix products, arithmetic and copies ran while one was open for 0% of the time, Pallas kernels for 7%

profile of v15, /device:TPU:0, one launch (start us, length us, event | category | flops | bytes accessed | tf_op | source)
XLA Modules:
  0.0 53.7 jit_solution(3009602290054346544)
XLA Ops:
  0.6 1.4 %pack.1 = (f32[4,3,128,128]{3,2,1,0:T(8,128)S(1)}, f32[2,128,128]{2,1,0:T(8,128)S(1)}, f32[14,8,128]{2,1,0:T(8,128)S(1)}, f32[128,128]{1,0:T(8,128)S(1)}, f32[4,...) custom-call(f32[4,3,128,128]{3,2,1,0:T(8,128)} %fields_hbm.1, f32[2,128,128]{2,1,0:T(8,128)} %noise_hbm.1), custom_call_target="tpu_custom_call" | custom-call | tf_op jit(solution)/shard_map/pack/pallas_call | solution.py:306
  2.1 4.0 %collective-permute-start = (f32[128,128]{1,0:T(8,128)S(1)}, f32[128,128]{1,0:T(8,128)S(1)}, u32[]{:S(2)}, u32[]{:S(2)}) collective-permute-start(f32[128,128]{1,0:T(8,128)S(1)} %get-tuple-element.29), channel_id=1, source_target_pairs={{0,1},{1,0},{2,3},{3,2},{4,5},{5,4},{6,7},{7,6},{8,9},{9,8},{10,11... | collective-permute-start | bytes 196616 | tf_op jit(solution)/shard_map/ppermute | solution.py:323
  6.1 0.0 collective-permute-start.1
  6.1 2.6 %interior.1 = (f32[4,8,8,128]{3,2,1,0:T(8,128)S(1)}, f32[4,128,128]{2,1,0:T(8,128)S(1)}, f32[4,3,128,128]{3,2,1,0:T(8,128)S(1)}, bf16[128,256]{1,0:T(8,128)(2,1)...) custom-call(f32[4,3,128,128]{3,2,1,0:T(8,128)S(1)} %get-tuple-elemen, ...), custom_call_target="tpu_custom_call", output_to_operand_aliasing={{0}: (2, {}), {1}: (3, {})} | custom-call | flops 50000000 | bytes 2500000 | tf_op jit(solution)/shard_map/interior/pallas_call | solution.py:326
  8.7 0.0 collective-permute-done.1.rowrecv
  8.7 0.0 collective-permute-done.colrecv
  8.7 0.1 collective-permute-start.2
  8.8 1.1 %strips.1 = (f32[3,8,8,128]{3,2,1,0:T(8,128)S(1)}, f32[4,144,128]{2,1,0:T(8,128)S(1)}, f32[3,144,128]{2,1,0:T(8,128)S(1)}) custom-call(f32[4,8,8,128]{3,2,1,0:T(8,128)S(1)} %get-tuple-element.33.ownrow, f32[14,8,128]{2,1,0:T(8,128)S(1)} %collective-permute-done.1.rowrecv, f32[4,128,128]{2,1,0:T(8,128)S(1)} %get-tuple-element.35.owncol, ...), custom_call_target="tpu_custom_call" | custom-call | flops 18000000 | bytes 700000 | tf_op jit(solution)/shard_map/strips/pallas_call | solution.py:359
  9.9 0.2 collective-permute-done.2.cornrecv
  10.1 2.6 %merge.1 = (f32[4,144,128]{2,1,0:T(8,128)S(1)}, f32[3,144,128]{2,1,0:T(8,128)S(1)}, f32[1568,128]{1,0:T(8,128)S(1)}) custom-call(f32[4,3,128,128]{3,2,1,0:T(8,128)S(1)} %get-tuple-element.32.inner, f32[3,8,8,128]{3,2,1,0:T(8,128)S(1)} %get-tuple-element.37.edge, ...), custom_call_target="tpu_custom_call", output_to_operand_aliasing={{0}: (2, {}), {1}: (3, {})} | custom-call | tf_op jit(solution)/shard_map/merge/pallas_call | solution.py:371
  12.7 22.6 %all_to_all.10 = f32[32,49,1,128]{3,2,1,0:T(1,128)S(1)} all-to-all(f32[32,49,1,128]{3,2,1,0:T(1,128)S(1)} %bitcast.10), channel_id=1, replica_groups=mesh['mem'=32,'gx'=2,'gy'=2] {'mem'}, dimensions={0} | all-to-all | bytes 1605632 | tf_op jit(solution)/shard_map/all_to_all | solution.py:381
  35.2 0.3 select.1
  35.6 17.2 %all_to_all.11.back = f32[32,2,24,128]{3,2,1,0:T(8,128)S(1)} all-to-all(f32[32,2,24,128]{3,2,1,0:T(8,128)S(1)} %bitcast.9), channel_id=1, replica_groups=mesh['mem'=32,'gx'=2,'gy'=2] {'mem'}, dimensions={0} | all-to-all | bytes 1572864 | tf_op jit(solution)/shard_map/all_to_all | solution.py:390
  52.8 0.9 %finish.1 = (f32[2,32,24,128]{3,2,1,0:T(8,128)}, f32[1,1,4]{2,1,0:T(1,128)}) custom-call(f32[32,2,24,128]{3,2,1,0:T(8,128)S(1)} %all_to_all.11.back, f32[1568,128]{1,0:T(8,128)S(1)} %bitcast.8), custom_call_target="tpu_custom_call" | custom-call | tf_op jit(solution)/shard_map/finish/pallas_call | solution.py:391
Async XLA Ops:
  2.1 6.6 %collective-permute-start = (f32[128,128]{1,0:T(8,128)S(1)}, f32[128,128]{1,0:T(8,128)S(1)}, u32[]{:S(2)}, u32[]{:S(2)}) collective-permute-start(f32[128,128]{1,0:T(8,128)S(1)} %get-tuple-element.29), channel_id=1, source_target_pairs={{0,1},{1,0},{2,3},{3,2},{4,5},{5,4},{6,7},{7,6},{8,9},{9,8},{10,11... | collective-permute-start | bytes 196616 | tf_op jit(solution)/shard_map/ppermute | solution.py:323
  6.1 2.6 %collective-permute-start.1 = (f32[14,8,128]{2,1,0:T(8,128)S(1)}, f32[14,8,128]{2,1,0:T(8,128)S(1)}, u32[]{:S(2)}, u32[]{:S(2)}) collective-permute-start(f32[14,8,128]{2,1,0:T(8,128)S(1)} %get-tuple-element.30), channel_id=1, source_target_pairs={{0,2},{2,0},{1,3},{3,1},{4,6},{6,4},{5,7},{7,5},{8,10},{10,8},{9,1... | collective-permute-start | bytes 172040 | tf_op jit(solution)/shard_map/ppermute | solution.py:324
  8.7 1.3 %collective-permute-start.2 = (f32[128,128]{1,0:T(8,128)S(1)}, f32[128,128]{1,0:T(8,128)S(1)}, u32[]{:S(2)}, u32[]{:S(2)}) collective-permute-start(f32[128,128]{1,0:T(8,128)S(1)} %collective-permute-done.colrecv), channel_id=1, source_target_pairs={{0,2},{2,0},{1,3},{3,1},{4,6},{6,4},{5,7},{7,5},{8,10},{10,8},{9,1... | collective-permute-start | bytes 196616 | tf_op jit(solution)/shard_map/ppermute | solution.py:358

commit v16 on v14

--- a/solution.py
+++ b/solution.py
@@ -115,6 +115,14 @@
     return acc
 
 
+def own_tall(tiles, every=1):
+    lane = lanes((T, T))
+    acc = jnp.zeros((T, T), F32)
+    for m in range(0, len(tiles), every):
+        acc = jnp.where(lane // 32 == m, lroll(tiles[m], 32 * m + 24), acc)
+    return jnp.where(lane % 32 < 8, lroll(acc, -16), acc)
+
+
 def own_strips(fields, noise, ownrow, owncol):
     members = fields.shape[0]
     for f in range(4):
@@ -123,9 +131,9 @@
             ownrow[f, 2 * m] = a[0:8]
             ownrow[f, 2 * m + 1] = a[T - 8 : T]
         if f < 3:
-            owncol[f] = own_columns(tiles)
+            owncol[f] = own_tall(tiles)
         else:
-            even = own_columns(tiles, 2)
+            even = own_tall(tiles, 2)
             owncol[f] = even + lroll(even, 32)
 
 
@@ -224,9 +232,9 @@
     top = subl((8, T)) < 4
     left = lanes((8, T)) < 4
     right = lanes((8, T)) >= T - 4
-    for m in range(members):
-        p, mm = m // 2, m % 2
-        for f in range(3):
+    for f in range(3):
+        for m in range(members):
+            p, mm = m // 2, m % 2
             for t in range(T // 8):
                 a = inner[m, f, 8 * t : 8 * t + 8]
                 if t == 0:
@@ -241,14 +249,14 @@
                 out[first : first + 8] = a
                 if f == 0:
                     eta_s[m * T + 8 * t : m * T + 8 * t + 8] = a
-
-    eta = eta_s[...]
-    hi = eta.astype(jnp.bfloat16)
-    rest = eta - hi.astype(F32)
-    mid = rest.astype(jnp.bfloat16)
-    low = (rest - mid.astype(F32)).astype(jnp.bfloat16)
-    dot = lambda part: jnp.dot(part, pick_y[...], preferred_element_type=F32)
-    seen = dot(hi) + (dot(mid) + dot(low))
+        if f == 0:
+            eta = eta_s[...]
+            hi = eta.astype(jnp.bfloat16)
+            rest = eta - hi.astype(F32)
+            mid = rest.astype(jnp.bfloat16)
+            low = (rest - mid.astype(F32)).astype(jnp.bfloat16)
+            dot = lambda part: jnp.dot(part, pick_y[...], preferred_element_type=F32)
+            seen = dot(hi) + (dot(mid) + dot(low))
     pick_x = lax.broadcasted_iota(jnp.int32, pick_y.shape, 0) == cell_x[...]
     logw = jnp.zeros((1, T), F32)
     for m in range(members):

time: 51.9 us -> 51.9 us (level)
  no operation moved by 1% of the time
where the time goes in v16:
time: 51.9 us; the launch traced here: 51.7 us
  blocking collectives  39.4 us (76%)
  Pallas kernels  7.09 us (14%)
  starting transfers between devices  4.13 us (8%)
  between operations  0.69 us (1%)
    all_to_all x1, blocking collectives, shards(): lax.all_to_all(pieces.reshape(devices, stride, 1, T), 'mem', 0, 0)  22.4 us
    all_to_all x1, blocking collectives, shards(): lax.all_to_all(picked.reshape(devices, members // 2, rows, T), 'mem', 0, 0)  17 us
    ppermute x1, starting transfers between devices, shards(): colrecv = lax.ppermute(colpack, 'gy', swap)  4.04 us
    pallas_call x1, Pallas kernels, shards(): pl.pallas_call(functools.partial(interior_kernel, total_y), out_shape=(sd...  2.59 us
    pallas_call x1, Pallas kernels, shards(): pl.pallas_call(pack_kernel, out_shape=(sds(*fields.shape), sds(*noise.sha...  1.43 us
  transfers between devices with their start and end apart: 3, of which 1 were waited for; matrix products, arithmetic and copies ran while one was open for 0% of the time, Pallas kernels for 7%

profile of v16, /device:TPU:0, one launch (start us, length us, event | category | flops | bytes accessed | tf_op | source)
XLA Modules:
  0.0 51.7 jit_solution(1670274774162163479)
XLA Ops:
  0.6 1.4 %pack.1 = (f32[4,3,128,128]{3,2,1,0:T(8,128)S(1)}, f32[2,128,128]{2,1,0:T(8,128)S(1)}, f32[14,8,128]{2,1,0:T(8,128)S(1)}, f32[128,128]{1,0:T(8,128)S(1)}, f32[4,...) custom-call(f32[4,3,128,128]{3,2,1,0:T(8,128)} %fields_hbm.1, f32[2,128,128]{2,1,0:T(8,128)} %noise_hbm.1), custom_call_target="tpu_custom_call" | custom-call | tf_op jit(solution)/shard_map/pack/pallas_call | solution.py:315
  2.1 4.0 %collective-permute-start = (f32[128,128]{1,0:T(8,128)S(1)}, f32[128,128]{1,0:T(8,128)S(1)}, u32[]{:S(2)}, u32[]{:S(2)}) collective-permute-start(f32[128,128]{1,0:T(8,128)S(1)} %get-tuple-element.29), channel_id=1, source_target_pairs={{0,1},{1,0},{2,3},{3,2},{4,5},{5,4},{6,7},{7,6},{8,9},{9,8},{10,11... | collective-permute-start | bytes 196616 | tf_op jit(solution)/shard_map/ppermute | solution.py:332
  6.1 0.0 collective-permute-start.1
  6.1 2.6 %interior.1 = (f32[4,8,8,128]{3,2,1,0:T(8,128)S(1)}, f32[4,128,128]{2,1,0:T(8,128)S(1)}, f32[4,3,128,128]{3,2,1,0:T(8,128)S(1)}, bf16[128,256]{1,0:T(8,128)(2,1)...) custom-call(f32[4,3,128,128]{3,2,1,0:T(8,128)S(1)} %get-tuple-elemen, ...), custom_call_target="tpu_custom_call", output_to_operand_aliasing={{0}: (2, {}), {1}: (3, {})} | custom-call | flops 50000000 | bytes 2500000 | tf_op jit(solution)/shard_map/interior/pallas_call | solution.py:335
  8.7 0.0 collective-permute-done.1.rowrecv
  8.7 0.0 collective-permute-done.colrecv
  8.7 0.1 collective-permute-start.2
  8.8 0.9 %strips.1 = (f32[3,8,8,128]{3,2,1,0:T(8,128)S(1)}, f32[4,144,128]{2,1,0:T(8,128)S(1)}, f32[3,144,128]{2,1,0:T(8,128)S(1)}) custom-call(f32[4,8,8,128]{3,2,1,0:T(8,128)S(1)} %get-tuple-element.33.ownrow, f32[14,8,128]{2,1,0:T(8,128)S(1)} %collective-permute-done.1.rowrecv, f32[4,128,128]{2,1,0:T(8,128)S(1)} %get-tuple-element.35.owncol, ...), custom_call_target="tpu_custom_call" | custom-call | flops 18000000 | bytes 700000 | tf_op jit(solution)/shard_map/strips/pallas_call | solution.py:368
  9.7 0.4 collective-permute-done.2.cornrecv
  10.1 1.0 %merge.1 = (f32[4,144,128]{2,1,0:T(8,128)S(1)}, f32[3,144,128]{2,1,0:T(8,128)S(1)}, f32[1568,128]{1,0:T(8,128)S(1)}) custom-call(f32[4,3,128,128]{3,2,1,0:T(8,128)S(1)} %get-tuple-element.32.inner, f32[3,8,8,128]{3,2,1,0:T(8,128)S(1)} %get-tuple-element.37.edge, ...), custom_call_target="tpu_custom_call", output_to_operand_aliasing={{0}: (2, {}), {1}: (3, {})} | custom-call | tf_op jit(solution)/shard_map/merge/pallas_call | solution.py:380
  11.0 22.4 %all_to_all.10 = f32[32,49,1,128]{3,2,1,0:T(1,128)S(1)} all-to-all(f32[32,49,1,128]{3,2,1,0:T(1,128)S(1)} %bitcast.10), channel_id=1, replica_groups=mesh['mem'=32,'gx'=2,'gy'=2] {'mem'}, dimensions={0} | all-to-all | bytes 1605632 | tf_op jit(solution)/shard_map/all_to_all | solution.py:390
  33.4 0.3 select.1
  33.8 17.0 %all_to_all.11.back = f32[32,2,24,128]{3,2,1,0:T(8,128)S(1)} all-to-all(f32[32,2,24,128]{3,2,1,0:T(8,128)S(1)} %bitcast.9), channel_id=1, replica_groups=mesh['mem'=32,'gx'=2,'gy'=2] {'mem'}, dimensions={0} | all-to-all | bytes 1572864 | tf_op jit(solution)/shard_map/all_to_all | solution.py:399
  50.8 0.9 %finish.1 = (f32[2,32,24,128]{3,2,1,0:T(8,128)}, f32[1,1,4]{2,1,0:T(1,128)}) custom-call(f32[32,2,24,128]{3,2,1,0:T(8,128)S(1)} %all_to_all.11.back, f32[1568,128]{1,0:T(8,128)S(1)} %bitcast.8), custom_call_target="tpu_custom_call" | custom-call | tf_op jit(solution)/shard_map/finish/pallas_call | solution.py:400
Async XLA Ops:
  2.1 6.6 %collective-permute-start = (f32[128,128]{1,0:T(8,128)S(1)}, f32[128,128]{1,0:T(8,128)S(1)}, u32[]{:S(2)}, u32[]{:S(2)}) collective-permute-start(f32[128,128]{1,0:T(8,128)S(1)} %get-tuple-element.29), channel_id=1, source_target_pairs={{0,1},{1,0},{2,3},{3,2},{4,5},{5,4},{6,7},{7,6},{8,9},{9,8},{10,11... | collective-permute-start | bytes 196616 | tf_op jit(solution)/shard_map/ppermute | solution.py:332
  6.1 2.6 %collective-permute-start.1 = (f32[14,8,128]{2,1,0:T(8,128)S(1)}, f32[14,8,128]{2,1,0:T(8,128)S(1)}, u32[]{:S(2)}, u32[]{:S(2)}) collective-permute-start(f32[14,8,128]{2,1,0:T(8,128)S(1)} %get-tuple-element.30), channel_id=1, source_target_pairs={{0,2},{2,0},{1,3},{3,1},{4,6},{6,4},{5,7},{7,5},{8,10},{10,8},{9,1... | collective-permute-start | bytes 172040 | tf_op jit(solution)/shard_map/ppermute | solution.py:333
  8.7 1.3 %collective-permute-start.2 = (f32[128,128]{1,0:T(8,128)S(1)}, f32[128,128]{1,0:T(8,128)S(1)}, u32[]{:S(2)}, u32[]{:S(2)}) collective-permute-start(f32[128,128]{1,0:T(8,128)S(1)} %collective-permute-done.colrecv), channel_id=1, source_target_pairs={{0,2},{2,0},{1,3},{3,1},{4,6},{6,4},{5,7},{7,5},{8,10},{10,8},{9,1... | collective-permute-start | bytes 196616 | tf_op jit(solution)/shard_map/ppermute | solution.py:367

commit v17 on v14

--- a/solution.py
+++ b/solution.py
@@ -198,8 +198,10 @@
             rs[f, 32 * m + 24 : 32 * m + 32] = halo(m, f)
         cs[f, 0:8] = own_columns([halo(m, f) for m in range(members)])
         cs[f, 8 : T + 8] = with_halo(owncol[f], colrecv[...], f, is_low, is_high)
-    some_rows(cs, cs1, 16, T - 16, coriolis(cols, total_y), cs)
+    cor_col = coriolis(cols, total_y)
+    some_rows(cs, cs1, 16, T - 16, cor_col, cs)
     twice(rs, rs1, T, coriolis(lanes((1, T)), total_y))
+    some_rows(cs1, cs, 24, T - 32, cor_col, cs)
     for f in range(3):
         for m in range(members):
             edge[f, 2 * m] = rs[f, 32 * m + 8 : 32 * m + 16]
@@ -217,7 +219,8 @@
         cs[f, T + 8 : T + 16] = ends
     some_rows(cs, cs1, 0, 16, cor_col, cs)
     some_rows(cs, cs1, T, 16, cor_col, cs)
-    some_rows(cs1, cs, 8, T, cor_col, cs)
+    some_rows(cs1, cs, 8, 16, cor_col, cs)
+    some_rows(cs1, cs, T - 8, 16, cor_col, cs)
 
     per = 96 // devices
     stride = members // 2 * 8 * per + 1

time: 51.9 us -> 52.2 us (level)
  no operation moved by 1% of the time
where the time goes in v17:
time: 52.2 us; the launch traced here: 52 us
  blocking collectives  39.8 us (76%)
  Pallas kernels  7.25 us (14%)
  starting transfers between devices  4.13 us (8%)
  between operations  0.69 us (1%)
    all_to_all x1, blocking collectives, shards(): lax.all_to_all(pieces.reshape(devices, stride, 1, T), 'mem', 0, 0)  22.6 us
    all_to_all x1, blocking collectives, shards(): lax.all_to_all(picked.reshape(devices, members // 2, rows, T), 'mem', 0, 0)  17.2 us
    ppermute x1, starting transfers between devices, shards(): colrecv = lax.ppermute(colpack, 'gy', swap)  4.04 us
    pallas_call x1, Pallas kernels, shards(): pl.pallas_call(functools.partial(interior_kernel, total_y), out_shape=(sd...  2.62 us
    pallas_call x1, Pallas kernels, shards(): pl.pallas_call(pack_kernel, out_shape=(sds(*fields.shape), sds(*noise.sha...  1.43 us
    pallas_call x1, Pallas kernels, shards(): pl.pallas_call(functools.partial(strips_kernel, total_y), out_shape=(sds(...  1.08 us
  transfers between devices with their start and end apart: 3, of which 1 were waited for; matrix products, arithmetic and copies ran while one was open for 0% of the time, Pallas kernels for 7%

profile of v17, /device:TPU:0, one launch (start us, length us, event | category | flops | bytes accessed | tf_op | source)
XLA Modules:
  0.0 52.0 jit_solution(8497110996134519935)
XLA Ops:
  0.6 1.4 %pack.1 = (f32[4,3,128,128]{3,2,1,0:T(8,128)S(1)}, f32[2,128,128]{2,1,0:T(8,128)S(1)}, f32[14,8,128]{2,1,0:T(8,128)S(1)}, f32[128,128]{1,0:T(8,128)S(1)}, f32[4,...) custom-call(f32[4,3,128,128]{3,2,1,0:T(8,128)} %fields_hbm.1, f32[2,128,128]{2,1,0:T(8,128)} %noise_hbm.1), custom_call_target="tpu_custom_call" | custom-call | tf_op jit(solution)/shard_map/pack/pallas_call | solution.py:310
  2.1 4.0 %collective-permute-start = (f32[128,128]{1,0:T(8,128)S(1)}, f32[128,128]{1,0:T(8,128)S(1)}, u32[]{:S(2)}, u32[]{:S(2)}) collective-permute-start(f32[128,128]{1,0:T(8,128)S(1)} %get-tuple-element.29), channel_id=1, source_target_pairs={{0,1},{1,0},{2,3},{3,2},{4,5},{5,4},{6,7},{7,6},{8,9},{9,8},{10,11... | collective-permute-start | bytes 196616 | tf_op jit(solution)/shard_map/ppermute | solution.py:327
  6.1 0.0 collective-permute-start.1
  6.1 2.6 %interior.1 = (f32[4,8,8,128]{3,2,1,0:T(8,128)S(1)}, f32[4,128,128]{2,1,0:T(8,128)S(1)}, f32[4,3,128,128]{3,2,1,0:T(8,128)S(1)}, bf16[128,256]{1,0:T(8,128)(2,1)...) custom-call(f32[4,3,128,128]{3,2,1,0:T(8,128)S(1)} %get-tuple-elemen, ...), custom_call_target="tpu_custom_call", output_to_operand_aliasing={{0}: (2, {}), {1}: (3, {})} | custom-call | flops 50000000 | bytes 2500000 | tf_op jit(solution)/shard_map/interior/pallas_call | solution.py:330
  8.7 0.0 collective-permute-done.1.rowrecv
  8.8 0.0 collective-permute-done.colrecv
  8.8 0.1 collective-permute-start.2
  8.9 1.1 %strips.1 = (f32[3,8,8,128]{3,2,1,0:T(8,128)S(1)}, f32[4,144,128]{2,1,0:T(8,128)S(1)}, f32[3,144,128]{2,1,0:T(8,128)S(1)}) custom-call(f32[4,8,8,128]{3,2,1,0:T(8,128)S(1)} %get-tuple-element.33.ownrow, f32[14,8,128]{2,1,0:T(8,128)S(1)} %collective-permute-done.1.rowrecv, f32[4,128,128]{2,1,0:T(8,128)S(1)} %get-tuple-element.35.owncol, ...), custom_call_target="tpu_custom_call" | custom-call | flops 18000000 | bytes 700000 | tf_op jit(solution)/shard_map/strips/pallas_call | solution.py:363
  9.9 0.2 collective-permute-done.2.cornrecv
  10.1 0.9 %merge.1 = (f32[4,144,128]{2,1,0:T(8,128)S(1)}, f32[3,144,128]{2,1,0:T(8,128)S(1)}, f32[1568,128]{1,0:T(8,128)S(1)}) custom-call(f32[4,3,128,128]{3,2,1,0:T(8,128)S(1)} %get-tuple-element.32.inner, f32[3,8,8,128]{3,2,1,0:T(8,128)S(1)} %get-tuple-element.37.edge, ...), custom_call_target="tpu_custom_call", output_to_operand_aliasing={{0}: (2, {}), {1}: (3, {})} | custom-call | tf_op jit(solution)/shard_map/merge/pallas_call | solution.py:375
  11.0 22.6 %all_to_all.10 = f32[32,49,1,128]{3,2,1,0:T(1,128)S(1)} all-to-all(f32[32,49,1,128]{3,2,1,0:T(1,128)S(1)} %bitcast.10), channel_id=1, replica_groups=mesh['mem'=32,'gx'=2,'gy'=2] {'mem'}, dimensions={0} | all-to-all | bytes 1605632 | tf_op jit(solution)/shard_map/all_to_all | solution.py:385
  33.5 0.3 select.1
  33.9 17.2 %all_to_all.11.back = f32[32,2,24,128]{3,2,1,0:T(8,128)S(1)} all-to-all(f32[32,2,24,128]{3,2,1,0:T(8,128)S(1)} %bitcast.9), channel_id=1, replica_groups=mesh['mem'=32,'gx'=2,'gy'=2] {'mem'}, dimensions={0} | all-to-all | bytes 1572864 | tf_op jit(solution)/shard_map/all_to_all | solution.py:394
  51.1 0.9 %finish.1 = (f32[2,32,24,128]{3,2,1,0:T(8,128)}, f32[1,1,4]{2,1,0:T(1,128)}) custom-call(f32[32,2,24,128]{3,2,1,0:T(8,128)S(1)} %all_to_all.11.back, f32[1568,128]{1,0:T(8,128)S(1)} %bitcast.8), custom_call_target="tpu_custom_call" | custom-call | tf_op jit(solution)/shard_map/finish/pallas_call | solution.py:395
Async XLA Ops:
  2.1 6.7 %collective-permute-start = (f32[128,128]{1,0:T(8,128)S(1)}, f32[128,128]{1,0:T(8,128)S(1)}, u32[]{:S(2)}, u32[]{:S(2)}) collective-permute-start(f32[128,128]{1,0:T(8,128)S(1)} %get-tuple-element.29), channel_id=1, source_target_pairs={{0,1},{1,0},{2,3},{3,2},{4,5},{5,4},{6,7},{7,6},{8,9},{9,8},{10,11... | collective-permute-start | bytes 196616 | tf_op jit(solution)/shard_map/ppermute | solution.py:327
  6.1 2.6 %collective-permute-start.1 = (f32[14,8,128]{2,1,0:T(8,128)S(1)}, f32[14,8,128]{2,1,0:T(8,128)S(1)}, u32[]{:S(2)}, u32[]{:S(2)}) collective-permute-start(f32[14,8,128]{2,1,0:T(8,128)S(1)} %get-tuple-element.30), channel_id=1, source_target_pairs={{0,2},{2,0},{1,3},{3,1},{4,6},{6,4},{5,7},{7,5},{8,10},{10,8},{9,1... | collective-permute-start | bytes 172040 | tf_op jit(solution)/shard_map/ppermute | solution.py:328
  8.8 1.3 %collective-permute-start.2 = (f32[128,128]{1,0:T(8,128)S(1)}, f32[128,128]{1,0:T(8,128)S(1)}, u32[]{:S(2)}, u32[]{:S(2)}) collective-permute-start(f32[128,128]{1,0:T(8,128)S(1)} %collective-permute-done.colrecv), channel_id=1, source_target_pairs={{0,2},{2,0},{1,3},{3,1},{4,6},{6,4},{5,7},{7,5},{8,10},{10,8},{9,1... | collective-permute-start | bytes 196616 | tf_op jit(solution)/shard_map/ppermute | solution.py:362

commit v18 on v14

--- a/solution.py
+++ b/solution.py
@@ -101,7 +101,8 @@
 
 
 def strips_first():
-    return (lax.axis_index("gx") != 0) & (lax.axis_index("gy") == 0)
+    first = (lax.axis_index("gx") != 0) | (lax.axis_index("mem") < lax.axis_size("mem") // 2)
+    return first & (lax.axis_index("gy") == 0)
 
 
 def own_columns(tiles, every=1):

time: 51.9 us -> 51.9 us (level)
    ppermute x1, starting transfers between devices: 4.04 us -> 3.43 us  [shards(): colrecv = lax.ppermute(colpack, 'gy', swap)]
    pallas_call x1, Pallas kernels: 2.62 us -> 2.02 us  [shards(): pl.pallas_call(functools.partial(interior_kernel, total_y), out_shape=(sd...]
    pallas_call x1, Pallas kernels: 1.43 us -> 2.04 us  [shards(): pl.pallas_call(pack_kernel, out_shape=(sds(*fields.shape), sds(*noise.sha...]
  transfers between devices with their start and end apart: 3 -> 3, of which waited for: 1 -> 2; matrix products, arithmetic and copies ran while one was open for 0% -> 0% of each run, Pallas kernels for 7% -> 6%
where the time goes in v18:
time: 51.9 us; the launch traced here: 51.7 us
  blocking collectives  39.7 us (76%)
  Pallas kernels  7.13 us (14%)
  starting transfers between devices  3.65 us (7%)
  between operations  0.68 us (1%)
  waiting for transfers between devices  0.55 us (1%)
    all_to_all x1, blocking collectives, shards(): lax.all_to_all(pieces.reshape(devices, stride, 1, T), 'mem', 0, 0)  22.7 us
    all_to_all x1, blocking collectives, shards(): lax.all_to_all(picked.reshape(devices, members // 2, rows, T), 'mem', 0, 0)  17 us
    ppermute x1, starting transfers between devices, shards(): colrecv = lax.ppermute(colpack, 'gy', swap)  3.43 us
    pallas_call x1, Pallas kernels, shards(): pl.pallas_call(pack_kernel, out_shape=(sds(*fields.shape), sds(*noise.sha...  2.04 us
    pallas_call x1, Pallas kernels, shards(): pl.pallas_call(functools.partial(interior_kernel, total_y), out_shape=(sd...  2.02 us
  transfers between devices with their start and end apart: 3, of which 2 were waited for; matrix products, arithmetic and copies ran while one was open for 0% of the time, Pallas kernels for 6%

profile of v18, /device:TPU:0, one launch (start us, length us, event | category | flops | bytes accessed | tf_op | source)
XLA Modules:
  0.0 51.7 jit_solution(10926557881350234171)
XLA Ops:
  0.6 2.0 %pack.1 = (f32[4,3,128,128]{3,2,1,0:T(8,128)S(1)}, f32[2,128,128]{2,1,0:T(8,128)S(1)}, f32[14,8,128]{2,1,0:T(8,128)S(1)}, f32[128,128]{1,0:T(8,128)S(1)}, f32[4,...) custom-call(f32[4,3,128,128]{3,2,1,0:T(8,128)} %fields_hbm.1, f32[2,128,128]{2,1,0:T(8,128)} %noise_hbm.1), custom_call_target="tpu_custom_call" | custom-call | tf_op jit(solution)/shard_map/pack/pallas_call | solution.py:308
  2.7 3.4 %collective-permute-start = (f32[128,128]{1,0:T(8,128)S(1)}, f32[128,128]{1,0:T(8,128)S(1)}, u32[]{:S(2)}, u32[]{:S(2)}) collective-permute-start(f32[128,128]{1,0:T(8,128)S(1)} %get-tuple-element.29), channel_id=1, source_target_pairs={{0,1},{1,0},{2,3},{3,2},{4,5},{5,4},{6,7},{7,6},{8,9},{9,8},{10,11... | collective-permute-start | bytes 196616 | tf_op jit(solution)/shard_map/ppermute | solution.py:325
  6.1 0.0 collective-permute-start.1
  6.1 2.0 %interior.1 = (f32[4,8,8,128]{3,2,1,0:T(8,128)S(1)}, f32[4,128,128]{2,1,0:T(8,128)S(1)}, f32[4,3,128,128]{3,2,1,0:T(8,128)S(1)}, bf16[128,256]{1,0:T(8,128)(2,1)...) custom-call(f32[4,3,128,128]{3,2,1,0:T(8,128)S(1)} %get-tuple-elemen, ...), custom_call_target="tpu_custom_call", output_to_operand_aliasing={{0}: (2, {}), {1}: (3, {})} | custom-call | flops 50000000 | bytes 2500000 | tf_op jit(solution)/shard_map/interior/pallas_call | solution.py:328
  8.1 0.0 collective-permute-done.1.rowrecv
  8.1 0.4 collective-permute-done.colrecv
  8.5 0.2 collective-permute-start.2
  8.7 0.9 %strips.1 = (f32[3,8,8,128]{3,2,1,0:T(8,128)S(1)}, f32[4,144,128]{2,1,0:T(8,128)S(1)}, f32[3,144,128]{2,1,0:T(8,128)S(1)}) custom-call(f32[4,8,8,128]{3,2,1,0:T(8,128)S(1)} %get-tuple-element.33.ownrow, f32[14,8,128]{2,1,0:T(8,128)S(1)} %collective-permute-done.1.rowrecv, f32[4,128,128]{2,1,0:T(8,128)S(1)} %get-tuple-element.35.owncol, ...), custom_call_target="tpu_custom_call" | custom-call | flops 18000000 | bytes 700000 | tf_op jit(solution)/shard_map/strips/pallas_call | solution.py:361
  9.6 0.2 collective-permute-done.2.cornrecv
  9.8 1.0 %merge.1 = (f32[4,144,128]{2,1,0:T(8,128)S(1)}, f32[3,144,128]{2,1,0:T(8,128)S(1)}, f32[1568,128]{1,0:T(8,128)S(1)}) custom-call(f32[4,3,128,128]{3,2,1,0:T(8,128)S(1)} %get-tuple-element.32.inner, f32[3,8,8,128]{3,2,1,0:T(8,128)S(1)} %get-tuple-element.37.edge, ...), custom_call_target="tpu_custom_call", output_to_operand_aliasing={{0}: (2, {}), {1}: (3, {})} | custom-call | tf_op jit(solution)/shard_map/merge/pallas_call | solution.py:373
  10.7 22.7 %all_to_all.10 = f32[32,49,1,128]{3,2,1,0:T(1,128)S(1)} all-to-all(f32[32,49,1,128]{3,2,1,0:T(1,128)S(1)} %bitcast.10), channel_id=1, replica_groups=mesh['mem'=32,'gx'=2,'gy'=2] {'mem'}, dimensions={0} | all-to-all | bytes 1605632 | tf_op jit(solution)/shard_map/all_to_all | solution.py:383
  33.4 0.3 select.1
  33.8 17.0 %all_to_all.11.back = f32[32,2,24,128]{3,2,1,0:T(8,128)S(1)} all-to-all(f32[32,2,24,128]{3,2,1,0:T(8,128)S(1)} %bitcast.9), channel_id=1, replica_groups=mesh['mem'=32,'gx'=2,'gy'=2] {'mem'}, dimensions={0} | all-to-all | bytes 1572864 | tf_op jit(solution)/shard_map/all_to_all | solution.py:392
  50.8 0.9 %finish.1 = (f32[2,32,24,128]{3,2,1,0:T(8,128)}, f32[1,1,4]{2,1,0:T(1,128)}) custom-call(f32[32,2,24,128]{3,2,1,0:T(8,128)S(1)} %all_to_all.11.back, f32[1568,128]{1,0:T(8,128)S(1)} %bitcast.8), custom_call_target="tpu_custom_call" | custom-call | tf_op jit(solution)/shard_map/finish/pallas_call | solution.py:393
Async XLA Ops:
  2.7 5.8 %collective-permute-start = (f32[128,128]{1,0:T(8,128)S(1)}, f32[128,128]{1,0:T(8,128)S(1)}, u32[]{:S(2)}, u32[]{:S(2)}) collective-permute-start(f32[128,128]{1,0:T(8,128)S(1)} %get-tuple-element.29), channel_id=1, source_target_pairs={{0,1},{1,0},{2,3},{3,2},{4,5},{5,4},{6,7},{7,6},{8,9},{9,8},{10,11... | collective-permute-start | bytes 196616 | tf_op jit(solution)/shard_map/ppermute | solution.py:325
  6.1 2.0 %collective-permute-start.1 = (f32[14,8,128]{2,1,0:T(8,128)S(1)}, f32[14,8,128]{2,1,0:T(8,128)S(1)}, u32[]{:S(2)}, u32[]{:S(2)}) collective-permute-start(f32[14,8,128]{2,1,0:T(8,128)S(1)} %get-tuple-element.30), channel_id=1, source_target_pairs={{0,2},{2,0},{1,3},{3,1},{4,6},{6,4},{5,7},{7,5},{8,10},{10,8},{9,1... | collective-permute-start | bytes 172040 | tf_op jit(solution)/shard_map/ppermute | solution.py:326
  8.5 1.3 %collective-permute-start.2 = (f32[128,128]{1,0:T(8,128)S(1)}, f32[128,128]{1,0:T(8,128)S(1)}, u32[]{:S(2)}, u32[]{:S(2)}) collective-permute-start(f32[128,128]{1,0:T(8,128)S(1)} %collective-permute-done.colrecv), channel_id=1, source_target_pairs={{0,2},{2,0},{1,3},{3,1},{4,6},{6,4},{5,7},{7,5},{8,10},{10,8},{9,1... | collective-permute-start | bytes 196616 | tf_op jit(solution)/shard_map/ppermute | solution.py:360

commit v19 on v18

--- a/solution.py
+++ b/solution.py
@@ -116,6 +116,14 @@
     return acc
 
 
+def own_tall(tiles, every=1):
+    lane = lanes((T, T))
+    acc = jnp.zeros((T, T), F32)
+    for m in range(0, len(tiles), every):
+        acc = jnp.where(lane // 32 == m, lroll(tiles[m], 32 * m + 24), acc)
+    return jnp.where(lane % 32 < 8, lroll(acc, -16), acc)
+
+
 def own_strips(fields, noise, ownrow, owncol):
     members = fields.shape[0]
     for f in range(4):
@@ -124,9 +132,9 @@
             ownrow[f, 2 * m] = a[0:8]
             ownrow[f, 2 * m + 1] = a[T - 8 : T]
         if f < 3:
-            owncol[f] = own_columns(tiles)
+            owncol[f] = own_tall(tiles)
         else:
-            even = own_columns(tiles, 2)
+            even = own_tall(tiles, 2)
             owncol[f] = even + lroll(even, 32)
 
 

time: 51.9 us -> 51.9 us (level)
  no operation moved by 1% of the time
where the time goes in v19:
time: 51.9 us; the launch traced here: 51.7 us
  blocking collectives  39.7 us (76%)
  Pallas kernels  7.1 us (14%)
  starting transfers between devices  3.72 us (7%)
  between operations  0.68 us (1%)
    all_to_all x1, blocking collectives, shards(): lax.all_to_all(pieces.reshape(devices, stride, 1, T), 'mem', 0, 0)  22.7 us
    all_to_all x1, blocking collectives, shards(): lax.all_to_all(picked.reshape(devices, members // 2, rows, T), 'mem', 0, 0)  17 us
    ppermute x1, starting transfers between devices, shards(): colrecv = lax.ppermute(colpack, 'gy', swap)  3.47 us
    pallas_call x1, Pallas kernels, shards(): pl.pallas_call(functools.partial(interior_kernel, total_y), out_shape=(sd...  2.02 us
    pallas_call x1, Pallas kernels, shards(): pl.pallas_call(pack_kernel, out_shape=(sds(*fields.shape), sds(*noise.sha...  2 us
  transfers between devices with their start and end apart: 3, of which 2 were waited for; matrix products, arithmetic and copies ran while one was open for 0% of the time, Pallas kernels for 6%

profile of v19, /device:TPU:0, one launch (start us, length us, event | category | flops | bytes accessed | tf_op | source)
XLA Modules:
  0.0 51.7 jit_solution(17598964545800107857)
XLA Ops:
  0.6 2.0 %pack.1 = (f32[4,3,128,128]{3,2,1,0:T(8,128)S(1)}, f32[2,128,128]{2,1,0:T(8,128)S(1)}, f32[14,8,128]{2,1,0:T(8,128)S(1)}, f32[128,128]{1,0:T(8,128)S(1)}, f32[4,...) custom-call(f32[4,3,128,128]{3,2,1,0:T(8,128)} %fields_hbm.1, f32[2,128,128]{2,1,0:T(8,128)} %noise_hbm.1), custom_call_target="tpu_custom_call" | custom-call | tf_op jit(solution)/shard_map/pack/pallas_call | solution.py:316
  2.6 3.5 %collective-permute-start = (f32[128,128]{1,0:T(8,128)S(1)}, f32[128,128]{1,0:T(8,128)S(1)}, u32[]{:S(2)}, u32[]{:S(2)}) collective-permute-start(f32[128,128]{1,0:T(8,128)S(1)} %get-tuple-element.29), channel_id=1, source_target_pairs={{0,1},{1,0},{2,3},{3,2},{4,5},{5,4},{6,7},{7,6},{8,9},{9,8},{10,11... | collective-permute-start | bytes 196616 | tf_op jit(solution)/shard_map/ppermute | solution.py:333
  6.1 0.0 collective-permute-start.1
  6.1 2.0 %interior.1 = (f32[4,8,8,128]{3,2,1,0:T(8,128)S(1)}, f32[4,128,128]{2,1,0:T(8,128)S(1)}, f32[4,3,128,128]{3,2,1,0:T(8,128)S(1)}, bf16[128,256]{1,0:T(8,128)(2,1)...) custom-call(f32[4,3,128,128]{3,2,1,0:T(8,128)S(1)} %get-tuple-elemen, ...), custom_call_target="tpu_custom_call", output_to_operand_aliasing={{0}: (2, {}), {1}: (3, {})} | custom-call | flops 50000000 | bytes 2500000 | tf_op jit(solution)/shard_map/interior/pallas_call | solution.py:336
  8.1 0.0 collective-permute-done.1.rowrecv
  8.1 0.3 collective-permute-done.colrecv
  8.5 0.3 collective-permute-start.2
  8.7 0.9 %strips.1 = (f32[3,8,8,128]{3,2,1,0:T(8,128)S(1)}, f32[4,144,128]{2,1,0:T(8,128)S(1)}, f32[3,144,128]{2,1,0:T(8,128)S(1)}) custom-call(f32[4,8,8,128]{3,2,1,0:T(8,128)S(1)} %get-tuple-element.33.ownrow, f32[14,8,128]{2,1,0:T(8,128)S(1)} %collective-permute-done.1.rowrecv, f32[4,128,128]{2,1,0:T(8,128)S(1)} %get-tuple-element.35.owncol, ...), custom_call_target="tpu_custom_call" | custom-call | flops 18000000 | bytes 700000 | tf_op jit(solution)/shard_map/strips/pallas_call | solution.py:369
  9.6 0.1 collective-permute-done.2.cornrecv
  9.7 1.0 %merge.1 = (f32[4,144,128]{2,1,0:T(8,128)S(1)}, f32[3,144,128]{2,1,0:T(8,128)S(1)}, f32[1568,128]{1,0:T(8,128)S(1)}) custom-call(f32[4,3,128,128]{3,2,1,0:T(8,128)S(1)} %get-tuple-element.32.inner, f32[3,8,8,128]{3,2,1,0:T(8,128)S(1)} %get-tuple-element.37.edge, ...), custom_call_target="tpu_custom_call", output_to_operand_aliasing={{0}: (2, {}), {1}: (3, {})} | custom-call | tf_op jit(solution)/shard_map/merge/pallas_call | solution.py:381
  10.7 22.7 %all_to_all.10 = f32[32,49,1,128]{3,2,1,0:T(1,128)S(1)} all-to-all(f32[32,49,1,128]{3,2,1,0:T(1,128)S(1)} %bitcast.10), channel_id=1, replica_groups=mesh['mem'=32,'gx'=2,'gy'=2] {'mem'}, dimensions={0} | all-to-all | bytes 1605632 | tf_op jit(solution)/shard_map/all_to_all | solution.py:391
  33.4 0.3 select.1
  33.8 17.0 %all_to_all.11.back = f32[32,2,24,128]{3,2,1,0:T(8,128)S(1)} all-to-all(f32[32,2,24,128]{3,2,1,0:T(8,128)S(1)} %bitcast.9), channel_id=1, replica_groups=mesh['mem'=32,'gx'=2,'gy'=2] {'mem'}, dimensions={0} | all-to-all | bytes 1572864 | tf_op jit(solution)/shard_map/all_to_all | solution.py:400
  50.8 0.9 %finish.1 = (f32[2,32,24,128]{3,2,1,0:T(8,128)}, f32[1,1,4]{2,1,0:T(1,128)}) custom-call(f32[32,2,24,128]{3,2,1,0:T(8,128)S(1)} %all_to_all.11.back, f32[1568,128]{1,0:T(8,128)S(1)} %bitcast.8), custom_call_target="tpu_custom_call" | custom-call | tf_op jit(solution)/shard_map/finish/pallas_call | solution.py:401
Async XLA Ops:
  2.6 5.8 %collective-permute-start = (f32[128,128]{1,0:T(8,128)S(1)}, f32[128,128]{1,0:T(8,128)S(1)}, u32[]{:S(2)}, u32[]{:S(2)}) collective-permute-start(f32[128,128]{1,0:T(8,128)S(1)} %get-tuple-element.29), channel_id=1, source_target_pairs={{0,1},{1,0},{2,3},{3,2},{4,5},{5,4},{6,7},{7,6},{8,9},{9,8},{10,11... | collective-permute-start | bytes 196616 | tf_op jit(solution)/shard_map/ppermute | solution.py:333
  6.1 2.0 %collective-permute-start.1 = (f32[14,8,128]{2,1,0:T(8,128)S(1)}, f32[14,8,128]{2,1,0:T(8,128)S(1)}, u32[]{:S(2)}, u32[]{:S(2)}) collective-permute-start(f32[14,8,128]{2,1,0:T(8,128)S(1)} %get-tuple-element.30), channel_id=1, source_target_pairs={{0,2},{2,0},{1,3},{3,1},{4,6},{6,4},{5,7},{7,5},{8,10},{10,8},{9,1... | collective-permute-start | bytes 172040 | tf_op jit(solution)/shard_map/ppermute | solution.py:334
  8.5 1.3 %collective-permute-start.2 = (f32[128,128]{1,0:T(8,128)S(1)}, f32[128,128]{1,0:T(8,128)S(1)}, u32[]{:S(2)}, u32[]{:S(2)}) collective-permute-start(f32[128,128]{1,0:T(8,128)S(1)} %collective-permute-done.colrecv), channel_id=1, source_target_pairs={{0,2},{2,0},{1,3},{3,1},{4,6},{6,4},{5,7},{7,5},{8,10},{10,8},{9,1... | collective-permute-start | bytes 196616 | tf_op jit(solution)/shard_map/ppermute | solution.py:368
